TPU v7x, 32 devices: a whole 2x2x4 slice. The times are simulated.
32 devices in a mesh: ckpt: 2 (over y), row: 16 (over z, x, core).
Axes of the slice: x: 2, y: 2, z: 4, core: 2. Of those that a mesh axis runs over, the one named last changes fastest.
Arguments:
- activations: bfloat16 [4096, 4096], P(('ckpt', 'row')), parts along dimension 0, may hold values from -6 to 6
- gate_pre: bfloat16 [4096, 7168], P(('ckpt', 'row')), parts along dimension 0, may hold values from -8 to 8
- out_grad: bfloat16 [4096, 4096], P(('ckpt', 'row')), parts along dimension 0, may hold values from -6 to 6
- down_weight: bfloat16 [14336, 4096], P(('ckpt', 'row')), parts along dimension 0, may hold values from -0.09375 to 0.09375
- proj_in: bfloat16 [4096, 64], replicated, may hold values from -0.09375 to 0.09375
- proj_out: bfloat16 [7168, 64], replicated, may hold values from -0.0625 to 0.0625
- stored: bfloat16 [24576, 4096], P(('ckpt', 'row')), parts along dimension 0, may hold values from -0.09375 to 0.09375
- visible: int32 [16], replicated, may hold values from 1 to 12288, as said below
Outputs:
- scores: float32 [32, 12288], P('ckpt', 'row'), parts along dimension 0
There are 2 independent parts, one for each index of `ckpt`. A program takes and returns all parts, laid end to end along the dimension named above; an argument that names none is the same for every part. Nothing has to cross between parts.
Inputs may be any that keep to these rules, and one draw needn't show every extreme that they name: `visible`: some query example sees all 12288 stored examples and some sees exactly one.
All inputs are finite; a program needn't handle non-finite values.
Results may differ from a plain program's by a relative error of at most 0.0064.
Values may be sent and summed in bfloat16 or wider, within the bound.
No kernel may reach another device: no remote copies, remote signals or barrier semaphores. Data moves between devices by JAX's collectives and lax.ppermute only.
A program may use at most 128 MiB of HBM per device.

v0:
```python
import jax
import jax.numpy as jnp
from jax import lax
from jax.sharding import PartitionSpec as P

SEQ_LEN = 128


def partner(value, axis, bit):
    return lax.ppermute(value, axis, [(i, i ^ 1 << bit) for i in range(lax.axis_size(axis))])


def collect(pieces, position, bit_list, sender):
    for bit_level in bit_list:
        partner_rows = sender(pieces, bit_level)
        upper_half = position >> bit_level & 1 == 1
        pieces = jnp.where(
            upper_half,
            jnp.concatenate([partner_rows, pieces], axis=0),
            jnp.concatenate([pieces, partner_rows], axis=0),
        )
    return pieces


def xor_order(slot_data, lane_id, lane_bits):
    lane_total = 1 << lane_bits
    for bit_level in range(lane_bits):
        shaped = slot_data.reshape(
            (lane_total >> bit_level + 1, 2, 1 << bit_level) + slot_data.shape[1:]
        )
        flipped = shaped[:, ::-1].reshape(slot_data.shape)
        slot_data = jnp.where(lane_id >> bit_level & 1 == 1, flipped, slot_data)
    return slot_data


def lane_exchange(slot_data, lane_id, lane_bits):
    lane_total = 1 << lane_bits
    slot_data = xor_order(slot_data, lane_id, lane_bits)
    for bit_level in range(lane_bits):
        shaped = slot_data.reshape(
            (lane_total >> bit_level + 1, 2, 1 << bit_level) + slot_data.shape[1:]
        )
        arrived = partner(shaped[:, 1], "row", bit_level)
        slot_data = jnp.concatenate([shaped[:, :1], arrived[:, None]], axis=1).reshape(
            slot_data.shape
        )
    return xor_order(slot_data, lane_id, lane_bits)


def shards(activations, gate_pre, out_grad, down_weight, proj_in, proj_out, stored, visible):
    devices = lax.axis_size("row")
    position = lax.axis_index("row")
    total_bits = devices.bit_length() - 1
    lane_bits = 3
    lane_total = 1 << lane_bits
    lane_id = position % lane_total
    tokens_dev = activations.shape[0]
    hidden_total = gate_pre.shape[1]
    rows_piece = down_weight.shape[0]
    groups = hidden_total // (rows_piece * lane_total)
    rank_size = proj_in.shape[1]
    weights_lane = collect(
        down_weight,
        position,
        range(lane_bits, total_bits),
        lambda pieces, bit_level: partner(pieces, "row", bit_level),
    )
    grad_group = collect(
        out_grad,
        position,
        range(0, lane_bits),
        lambda pieces, bit_level: partner(pieces, "row", bit_level),
    )
    hidden_block = lax.dot_general(
        grad_group, weights_lane, (((1,), (1,)), ((), ())), preferred_element_type=jnp.float32
    ).astype(jnp.bfloat16)
    received = lane_exchange(
        hidden_block.reshape(lane_total, tokens_dev, groups * rows_piece), lane_id, lane_bits
    )
    full_grad = (
        received.reshape(lane_total, tokens_dev, groups, rows_piece)
        .transpose(1, 2, 0, 3)
        .reshape(tokens_dev, hidden_total)
    )
    up_grad = (
        lax.optimization_barrier(full_grad).astype(jnp.float32)
        * jax.nn.silu(gate_pre.astype(jnp.float32))
    ).astype(jnp.bfloat16)
    out_proj = jnp.dot(up_grad, proj_out, preferred_element_type=jnp.float32).astype(jnp.bfloat16)
    in_proj = jnp.dot(activations, proj_in, preferred_element_type=jnp.float32).astype(jnp.bfloat16)
    examples_dev = tokens_dev // SEQ_LEN
    in_split = in_proj.astype(jnp.float32).reshape(examples_dev, SEQ_LEN, rank_size)
    out_split = out_proj.astype(jnp.float32).reshape(examples_dev, SEQ_LEN, rank_size)
    raw_feature = jnp.einsum(
        "esa,esb->eab", in_split, out_split, preferred_element_type=jnp.float32
    ).reshape(examples_dev, rank_size * rank_size)
    scale = lax.rsqrt(jnp.mean(raw_feature * raw_feature, axis=1, keepdims=True) + 1e-06)
    queries = (raw_feature * scale).astype(jnp.bfloat16)
    stored_rows = stored.shape[0]
    column = position * stored_rows + jnp.arange(stored_rows, dtype=jnp.int32)
    products = lax.dot_general(
        lax.all_gather(queries, "row", axis=0, tiled=True),
        stored,
        (((1,), (1,)), ((), ())),
        preferred_element_type=jnp.float32,
    )
    return jnp.where(column[None, :] < visible[:, None], products, jnp.float32(0.0))


def solution(mesh):
    return jax.shard_map(
        shards,
        mesh=mesh,
        in_specs=(
            P(("ckpt", "row"), None),
            P(("ckpt", "row"), None),
            P(("ckpt", "row"), None),
            P(("ckpt", "row"), None),
            P(),
            P(),
            P(("ckpt", "row"), None),
            P(),
        ),
        out_specs=P("ckpt", "row"),
        check_vma=False,
    )
```

profile of v0, /device:TPU:0, one launch (start us, length us, event | category | flops | bytes accessed | tf_op | source)
XLA Modules:
  0.0 381.6 jit_solution(10606979016936965666)
XLA Ops:
  0.5 2.6 collective-permute-done
  3.1 3.1 maximum_select_fusion.5
  6.2 2.9 collective-permute-start.1
  9.2 46.0 %collective-permute-done.1 = bf16[256,4096]{1,0:T(8,128)(2,1)} collective-permute-done((bf16[256,4096]{1,0:T(8,128)(2,1)S(1)}, bf16[256,4096]{1,0:T(8,128)(2,1)}, u32[]{:S(2)}, u32[]{:S(2)}) %collective-permute-start.1) | collective-permute-done | bytes 2097184 | tf_op jit(solution)/shard_map/ppermute | solution.py:10
  55.2 4.7 %maximum_select_fusion.4 = bf16[512,4096]{1,0:T(8,128)(2,1)} fusion(bf16[256,4096]{1,0:T(8,128)(2,1)S(1)} %maximum_select_fusion.5, bf16[256,4096]{1,0:T(8,128)(2,1)} %collective-permute-done.1, pred[]{:T(512)S(6)} %eq.30), kind=kLoop, calls=%fused_computation.17 | loop fusion | flops 18874368 | bytes 8388609 | tf_op jit(solution)/shard_map/jit(_where)/select_n | solution.py:17
  59.9 1.8 collective-permute-start.2
  61.8 2.6 collective-permute-start.3
  64.4 165.7 %collective-permute-done.3 = bf16[448,4096]{1,0:T(8,128)(2,1)} collective-permute-done((bf16[448,4096]{1,0:T(8,128)(2,1)}, bf16[448,4096]{1,0:T(8,128)(2,1)}, u32[]{:S(2)}, u32[]{:S(2)}) %collective-permute-start.3) | collective-permute-done | bytes 3670048 | tf_op jit(solution)/shard_map/ppermute | solution.py:10
  231.0 14.4 %fusion.20 = bf16[1024,896]{1,0:T(8,128)(2,1)S(1)} fusion(bf16[448,4096]{1,0:T(8,128)(2,1)} %param.11, bf16[448,4096]{1,0:T(8,128)(2,1)} %collective-permute-done.3, pred[]{:T(512)S(6)} %eq.32, bf16[512,4096]{1,0:T(8,128)(2,1)} %maximum_select_fusion.4, bf16[512,4096]{1,0:T(8,128)(2,1)} %collective-permute-done.2, pred[]{:T(512)S(6)} %eq.29), kind=kOutput, calls=%fused_computation.35 | convolution fusion | flops 7587889152 | bytes 17563650 | tf_op jit(solution)/shard_map/dot_general | solution.py:74
  246.9 3.6 copy.27
  250.5 2.4 copy.28
  252.9 2.9 broadcast_select_fusion
  255.9 2.9 rev.19
  258.8 2.4 copy.30
  261.2 3.0 select_select_fusion.2
  264.2 2.9 rev.20
  267.1 3.6 copy.32
  270.7 3.6 copy.31
  276.8 2.2 collective-permute-done.4
  280.8 3.5 collective-permute-start.5
  284.3 20.7 %collective-permute-done.5 = bf16[2,2,128,896]{2,3,1,0:T(8,128)(2,1)S(1)} collective-permute-done((bf16[2,2,128,896]{2,3,1,0:T(8,128)(2,1)S(1)}, bf16[2,2,128,896]{2,3,1,0:T(8,128)(2,1)S(1)}, u32[]{:S(2)}, u32[]{:S(2)}) %collective-permute-start.5) | collective-permute-done | bytes 917536 | tf_op jit(solution)/shard_map/ppermute | solution.py:10
  306.2 3.1 collective-permute-start.6
  309.3 3.9 %copy.37 = bf16[128,7168]{0,1:T(8,128)(2,1)} copy(bf16[128,7168]{1,0:T(8,128)(2,1)} %param.9) | data formatting | bytes 3670016 | tf_op args[1]
  313.7 15.9 %collective-permute-done.6 = bf16[1,4,128,896]{2,3,1,0:T(8,128)(2,1)S(1)} collective-permute-done((bf16[1,4,128,896]{2,3,1,0:T(8,128)(2,1)}, bf16[1,4,128,896]{2,3,1,0:T(8,128)(2,1)S(1)}, u32[]{:S(2)}, u32[]{:S(2)}) %collective-permute-start.6) | collective-permute-done | bytes 917536 | tf_op jit(solution)/shard_map/ppermute | solution.py:10
  332.9 2.9 maximum_select_fusion.6
  335.9 2.9 rev.22
  338.7 2.9 select_select_fusion
  341.7 2.9 rev.23
  344.6 1.8 select_bitcast_fusion
  348.6 4.0 %multiply_reduce_fusion = (f32[]{:T(128)}, f32[64,64]{1,0:T(8,128)S(1)}) fusion(bf16[128,64]{0,1:T(8,128)(2,1)S(1)} %convolution_convert_fusion, bf16[7168,64]{0,1:T(8,128)(2,1)} %param.13, bf16[128,7168]{0,1:T(8,128)(2,1)S(1)} %copy-done.3, bf16[128,7168]{0,1:T(8,128)(2,1)} %bitcast.65), kind=kOutput, calls=%fused_computation.49 | convolution fusion | flops 125845504 | bytes 4620292 | tf_op jit(solution)/shard_map/esa,esb->eab/dot_general | solution.py:94
  353.4 23.0 %all-gather = bf16[16,1,4096]{2,1,0:T(2,128)(2,1)S(1)} all-gather(bf16[1,1,4096]{2,1,0:T(2,128)(2,1)S(1)} %reshape.191), channel_id=1, replica_groups=mesh['ckpt'=2,'row'=16] {'row'}, dimensions={0}, use_global_device_ids=true | all-gather | bytes 139264 | tf_op jit(solution)/shard_map/all_gather | solution.py:102
  376.4 5.2 %convolution_select_fusion = f32[16,768]{1,0:T(8,128)} fusion(bf16[768,4096]{1,0:T(8,128)(2,1)} %param.14, bf16[16,1,4096]{2,1,0:T(2,128)(2,1)S(1)} %all-gather, s32[768]{0:T(1024)S(1)} %iota_add_fusion, s32[16]{0:T(128)S(1)} %copy-done.5), kind=kOutput, calls=%fused_computation.36 | convolution fusion | flops 100687872 | bytes 6474816 | tf_op jit(solution)/shard_map/dot_general | solution.py:101
  (30 shorter events, 14.4 us)
Async XLA Ops:
  0.0 313.2 %copy-start = (bf16[128,4096]{1,0:T(8,128)(2,1)S(1)}, bf16[128,4096]{1,0:T(8,128)(2,1)}, u32[]{:S(2)}) copy-start(bf16[128,4096]{1,0:T(8,128)(2,1)} %param.8) | copy-start | bytes 3145732
  0.0 3.1 collective-permute-start
  6.2 49.0 %collective-permute-start.1 = (bf16[256,4096]{1,0:T(8,128)(2,1)S(1)}, bf16[256,4096]{1,0:T(8,128)(2,1)}, u32[]{:S(2)}, u32[]{:S(2)}) collective-permute-start(bf16[256,4096]{1,0:T(8,128)(2,1)S(1)} %maximum_select_fusion.5), channel_id=1, source_target_pairs={{0,2},{1,3},{2,0},{3,1},{4,6},{5,7},{6,4},{7,5},{8,10},{9,11},{10,... | collective-permute-start | bytes 6291464 | tf_op jit(solution)/shard_map/ppermute | solution.py:10
  59.9 171.1 %collective-permute-start.2 = (bf16[512,4096]{1,0:T(8,128)(2,1)}, bf16[512,4096]{1,0:T(8,128)(2,1)}, u32[]{:S(2)}, u32[]{:S(2)}) collective-permute-start(bf16[512,4096]{1,0:T(8,128)(2,1)} %maximum_select_fusion.4), channel_id=1, source_target_pairs={{0,4},{1,5},{2,6},{3,7},{4,0},{5,1},{6,2},{7,3},{8,12},{9,13},{10,... | collective-permute-start | bytes 12582920 | tf_op jit(solution)/shard_map/ppermute | solution.py:10
  61.8 168.3 %collective-permute-start.3 = (bf16[448,4096]{1,0:T(8,128)(2,1)}, bf16[448,4096]{1,0:T(8,128)(2,1)}, u32[]{:S(2)}, u32[]{:S(2)}) collective-permute-start(bf16[448,4096]{1,0:T(8,128)(2,1)} %param.11), channel_id=1, source_target_pairs={{0,8},{1,9},{2,10},{3,11},{4,12},{5,13},{6,14},{7,15},{8,0},{9,1},... | collective-permute-start | bytes 11010056 | tf_op jit(solution)/shard_map/ppermute | solution.py:10
  276.2 2.8 collective-permute-start.4
  280.8 24.2 %collective-permute-start.5 = (bf16[2,2,128,896]{2,3,1,0:T(8,128)(2,1)S(1)}, bf16[2,2,128,896]{2,3,1,0:T(8,128)(2,1)S(1)}, u32[]{:S(2)}, u32[]{:S(2)}) collective-permute-start(bf16[2,2,128,896]{2,3,1,0:T(8,128)(2,1)S(1)} %get-tuple-element.8), channel_id=1, source_target_pairs={{0,2},{1,3},{2,0},{3,1},{4,6},{5,7},{6,4},{7,5},{8,10},{9,11},{10,... | collective-permute-start | bytes 2752520 | tf_op jit(solution)/shard_map/ppermute | solution.py:10
  306.2 23.5 %copy-start.1 = (bf16[1,1,4,128,896]{3,4,2,1,0:T(8,128)(2,1)}, bf16[1,1,4,128,896]{3,4,2,1,0:T(8,128)(2,1)S(1)}, u32[]{:S(2)}) copy-start(bf16[1,1,4,128,896]{3,4,2,1,0:T(8,128)(2,1)S(1)} %get-tuple-element.5) | copy-start | bytes 2752516
  306.2 7.1 %copy-start.4 = (bf16[4096,64]{0,1:T(8,128)(2,1)S(1)}, bf16[4096,64]{0,1:T(8,128)(2,1)}, u32[]{:S(2)}) copy-start(bf16[4096,64]{0,1:T(8,128)(2,1)} %param.12) | copy-start | bytes 1572868
  306.2 23.5 %collective-permute-start.6 = (bf16[1,4,128,896]{2,3,1,0:T(8,128)(2,1)}, bf16[1,4,128,896]{2,3,1,0:T(8,128)(2,1)S(1)}, u32[]{:S(2)}, u32[]{:S(2)}) collective-permute-start(bf16[1,4,128,896]{2,3,1,0:T(8,128)(2,1)} %get-tuple-element.6), channel_id=1, source_target_pairs={{0,4},{1,5},{2,6},{3,7},{4,0},{5,1},{6,2},{7,3},{8,12},{9,13},{10,... | collective-permute-start | bytes 2752520 | tf_op jit(solution)/shard_map/ppermute | solution.py:10
  329.7 1.6 copy-start.2
  346.5 2.2 copy-start.3
  348.6 27.8 %copy-start.5 = (s32[16]{0:T(128)S(1)}, s32[16]{0:T(128)}, u32[]{:S(2)}) copy-start(s32[16]{0:T(128)} %param.15) | copy-start | bytes 196
where the time goes:
time: 382 us
  waiting for transfers between devices  254 us (66%)
  local copies, waits for them, and re-layouts  40.9 us (11%)
  other arithmetic  24.3 us (6%)
  matrix products  24 us (6%)
  blocking collectives  23 us (6%)
  starting transfers between devices  14.5 us (4%)
    ppermute x7, waiting for transfers between devices, partner(): lax.ppermute(value, axis, [(i, i ^ 1 << bit) for i in range(lax.axis_size...  254 us
    all_gather x1, blocking collectives, shards(): lax.all_gather(queries, 'row', axis=0, tiled=True)  23 us
    rev x7, local copies, waits for them, and re-layouts, xor_order(): flipped = shaped[:, ::-1].reshape(slot_data.shape)  18.3 us
    ppermute x7, starting transfers between devices, partner(): lax.ppermute(value, axis, [(i, i ^ 1 << bit) for i in range(lax.axis_size...  14.5 us
    dot_general x1, matrix products, shards(): lax.dot_general(grad_group, weights_lane, (((1,), (1,)), ((), ())), prefe...  14.4 us
    select_n x5, other arithmetic, xor_order(): slot_data = jnp.where(lane_id >> bit_level & 1 == 1, flipped, slot_data)  12.6 us
    select_n x2, other arithmetic, collect(): jnp.where(upper_half, jnp.concatenate([partner_rows, pieces], axis=0), jn...  7.89 us
  transfers between devices with their start and end apart: 7, of which 7 were waited for; matrix products, arithmetic and copies ran while one was open for 1% of the time, Pallas kernels for 0%

commit v1 on v0

v1 whole, which is shorter than its diff:
```python
import jax
import jax.numpy as jnp
from jax import lax
from jax.sharding import PartitionSpec as P

SEQ_LEN = 128
LANE_SHIFT = 2
LANES = 4


def shards(activations, gate_pre, out_grad, down_weight, proj_in, proj_out, stored, visible):
    devices = lax.axis_size("row")
    position = lax.axis_index("row")
    total_bits = devices.bit_length() - 1
    lane = position >> LANE_SHIFT & LANES - 1
    quad = position & (1 << LANE_SHIFT) - 1
    quads = 1 << LANE_SHIFT
    tokens = out_grad.shape[0]
    rank = proj_in.shape[1]
    piece = down_weight.shape[0]
    blocks = LANES * quads
    outer = devices // blocks
    bf16, f32 = jnp.bfloat16, jnp.float32

    def send(value, move):
        pairs = []
        for i in range(devices):
            target = move(i)
            if target is not None:
                pairs.append((i, target))
        return lax.ppermute(value, "row", pairs)

    def flip(bits):
        return lambda i: i ^ bits

    def lane_move(table):
        def move(i):
            to = table.get(i >> LANE_SHIFT & LANES - 1)
            return None if to is None else i & ~((LANES - 1) << LANE_SHIFT) | to << LANE_SHIFT

        return move

    def gather_high(value, axis):
        for bit in range(LANE_SHIFT + 2, total_bits):
            other = send(value, flip(1 << bit))
            high = position >> bit & 1 == 1
            value = jnp.where(
                high,
                jnp.concatenate([other, value], axis=axis),
                jnp.concatenate([value, other], axis=axis),
            )
        return value

    middle_swap = lane_move({1: 2, 2: 1})
    to_ends = lane_move({1: 0, 2: 3})
    at_end = (lane == 0) | (lane == LANES - 1)

    own_w = gather_high(down_weight, 0)
    rows = own_w.shape[0]

    grad_a = send(out_grad, flip(1 << LANE_SHIFT))
    grad_b = send(out_grad, middle_swap)
    far_w = send(own_w, flip(2))
    core_w = send(own_w, flip(1))

    in_proj = jnp.dot(activations, proj_in, preferred_element_type=f32).astype(bf16)

    def columns(block):
        parts = [
            lax.dynamic_slice_in_dim(gate_pre, (o * blocks + block) * piece, piece, axis=1)
            for o in range(outer)
        ]
        return parts

    def gate_block(k):
        parts = []
        for w in range(quads):
            parts += columns((lane ^ k) * quads + (quad ^ w))
        return jnp.concatenate(parts, axis=1)

    grad_c = send(grad_a, middle_swap)
    grad_d = send(grad_b, to_ends)
    grad_e = send(grad_c, to_ends)

    gates, ins = [gate_block(0)], [in_proj]
    hidden_group = rows * quads
    for k in range(1, LANES):
        got = send(jnp.concatenate([gate_block(k), in_proj], axis=1), flip(k << LANE_SHIFT))
        gates.append(got[:, :hidden_group])
        ins.append(got[:, hidden_group:])
    gates = jnp.concatenate(gates, axis=0)

    grads = jnp.concatenate(
        [out_grad, grad_a, jnp.where(at_end, grad_d, grad_c), jnp.where(at_end, grad_e, grad_b)],
        axis=0,
    )

    cross_w = send(far_w, flip(1))

    out_rows = []
    for w in range(quads):
        parts = [
            lax.dynamic_slice_in_dim(
                proj_out, (o * blocks + lane * quads + (quad ^ w)) * piece, piece, axis=0
            )
            for o in range(outer)
        ]
        out_rows.append(jnp.concatenate(parts, axis=0))
    weights = [
        (own_w, 0),
        (core_w, rows),
        (far_w, 2 * rows),
        (cross_w, 3 * rows),
    ]
    out_rows = jnp.concatenate(out_rows, axis=0)
    out = jnp.zeros((LANES * tokens, rank), f32)
    for weight, start in weights:
        stop = start + weight.shape[0]
        hidden = lax.dot_general(
            grads, weight, (((1,), (1,)), ((), ())), preferred_element_type=f32
        ).astype(bf16)
        up_grad = (
            lax.optimization_barrier(hidden).astype(f32)
            * jax.nn.silu(gates[:, start:stop].astype(f32))
        ).astype(bf16)
        out += jnp.dot(up_grad, out_rows[start:stop], preferred_element_type=f32)

    examples_dev = tokens // SEQ_LEN
    feature = jnp.einsum(
        "kesa,kesb->keab",
        jnp.stack(ins).reshape(LANES, examples_dev, SEQ_LEN, rank).astype(f32),
        out.reshape(LANES, examples_dev, SEQ_LEN, rank),
        preferred_element_type=f32,
    ).reshape(LANES, examples_dev, rank * rank)
    for bit in range(2):
        other = send(feature, flip(1 << bit + LANE_SHIFT))
        order = [k ^ 1 << bit for k in range(LANES)]
        feature = feature + jnp.stack([other[k] for k in order])
    scale = lax.rsqrt(jnp.mean(feature * feature, axis=2, keepdims=True) + 1e-06)
    queries = (feature * scale).astype(bf16)
    for bit in range(2):
        flipped = queries.reshape(LANES >> bit + 1, 2, 1 << bit, examples_dev, -1)[:, ::-1]
        queries = jnp.where(lane >> bit & 1 == 1, flipped.reshape(queries.shape), queries)
    queries = queries[:, None]
    for bit in range(LANE_SHIFT):
        other = send(queries, flip(1 << bit))
        high = position >> bit & 1 == 1
        queries = jnp.where(
            high,
            jnp.concatenate([other, queries], axis=1),
            jnp.concatenate([queries, other], axis=1),
        )
    queries = gather_high(queries, 0).reshape(devices * examples_dev, rank * rank)
    stored_rows = stored.shape[0]
    column = position * stored_rows + jnp.arange(stored_rows, dtype=jnp.int32)
    products = lax.dot_general(
        queries, stored, (((1,), (1,)), ((), ())), preferred_element_type=f32
    )
    return jnp.where(column[None, :] < visible[:, None], products, f32(0.0))


def solution(mesh):
    return jax.shard_map(
        shards,
        mesh=mesh,
        in_specs=(
            P(("ckpt", "row"), None),
            P(("ckpt", "row"), None),
            P(("ckpt", "row"), None),
            P(("ckpt", "row"), None),
            P(),
            P(),
            P(("ckpt", "row"), None),
            P(),
        ),
        out_specs=P("ckpt", "row"),
        check_vma=False,
    )
```

time: 382 us -> 179 us (0.47)
  waiting for transfers between devices: 254 us -> 83.6 us
  blocking collectives: 23 us -> 0 us
  other arithmetic: 24.3 us -> 5.96 us
  local copies, waits for them, and re-layouts: 40.9 us -> 44.8 us
    ppermute x7 -> x15, waiting for transfers between devices: 254 us -> 83.6 us  [send(): return lax.ppermute(value, 'row', pairs)]
    unnamed x14 -> x39, local copies, waits for them, and re-layouts: 4.8 us -> 32.7 us
    all_gather x1 -> x0, blocking collectives: 23 us -> none  [shards(): lax.all_gather(queries, 'row', axis=0, tiled=True)]
    select_n x7 -> x6, other arithmetic: 20.5 us -> 1.91 us  [the longest x1 1.34 us: shards(): jnp.where(at_end, grad_d, grad_c)]
    rev x7 -> x2, local copies, waits for them, and re-layouts: 18.3 us -> 0.97 us  [shards(): queries.reshape(LANES >> bit + 1, 2, 1 << bit, examples_dev, -1)[:, ::-1]]
    reshape x4 -> x8, local copies, waits for them, and re-layouts: 12.1 us -> 0.52 us  [the longest x4 0.45 us: shards(): feature = jnp.einsum('kesa,kesb->keab', jnp.stack(ins).reshape(LANES, exa...]
    dynamic_slice x0 -> x1, local copies, waits for them, and re-layouts: none -> 4.13 us  [columns(): lax.dynamic_slice_in_dim(gate_pre, (o * blocks + block) * piece, piece, a...]
    ppermute x7 -> x15, starting transfers between devices: 14.5 us -> 16.7 us  [send(): return lax.ppermute(value, 'row', pairs)]
  transfers between devices with their start and end apart: 7 -> 15, of which waited for: 7 -> 9; matrix products, arithmetic and copies ran while one was open for 1% -> 36% of each run, Pallas kernels for 0% -> 0%
where the time goes in v1:
time: 179 us; the launch traced here: 178 us
  waiting for transfers between devices  83.6 us (47%)
  local copies, waits for them, and re-layouts  44.8 us (25%)
  matrix products  26.2 us (15%)
  starting transfers between devices  16.7 us (9%)
  other arithmetic  5.96 us (3%)
    ppermute x15, waiting for transfers between devices, send(): return lax.ppermute(value, 'row', pairs)  83.6 us
    unnamed x39, local copies, waits for them, and re-layouts  32.7 us
    ppermute x15, starting transfers between devices, send(): return lax.ppermute(value, 'row', pairs)  16.7 us
    dot_general x4, matrix products, shards(): lax.dot_general(grads, weight, (((1,), (1,)), ((), ())), preferred_elemen...  14.5 us
    dot_general x4, matrix products, shards(): out += jnp.dot(up_grad, out_rows[start:stop], preferred_element_type=f32)  5.28 us
    dot_general x1, matrix products, shards(): lax.dot_general(queries, stored, (((1,), (1,)), ((), ())), preferred_elem...  5.14 us
    dynamic_slice x1, local copies, waits for them, and re-layouts, columns(): lax.dynamic_slice_in_dim(gate_pre, (o * blocks + block) * piece, piece, a...  4.13 us
    concatenate x1, other arithmetic, shards(): gates = jnp.concatenate(gates, axis=0)  3.61 us
  transfers between devices with their start and end apart: 15, of which 9 were waited for; matrix products, arithmetic and copies ran while one was open for 36% of the time, Pallas kernels for 0%

profile of v1, /device:TPU:0, one launch (start us, length us, event | category | flops | bytes accessed | tf_op | source)
XLA Modules:
  0.0 177.7 jit_solution(6561541786006215141)
XLA Ops:
  0.0 3.0 %collective-permute-start.3 = (bf16[128,4096]{1,0:T(8,128)(2,1)}, bf16[128,4096]{1,0:T(8,128)(2,1)}, u32[]{:S(2)}, u32[]{:S(2)}) collective-permute-start(bf16[128,4096]{1,0:T(8,128)(2,1)} %param.10), channel_id=1, source_target_pairs={{0,4},{1,5},{2,6},{3,7},{4,0},{5,1},{6,2},{7,3},{8,12},{9,13},{10,... | collective-permute-start | bytes 3145736 | tf_op jit(solution)/shard_map/ppermute | solution.py:31
  3.8 1.6 collective-permute-start.9
  5.3 4.1 %constant_dynamic-slice_fusion.3 = (bf16[128,448]{1,0:T(8,128)(2,1)}, bf16[128,448]{1,0:T(8,128)(2,1)S(1)}, bf16[128,448]{1,0:T(8,128)(2,1)S(1)}, bf16[128,448]{...) fusion(bf16[128,7168]{1,0:T(8,128)(2,1)} %param.9, ...), kind=kLoop, calls=%fused_computation.102 | loop fusion | bytes 3670080 | tf_op jit(solution)/shard_map/dynamic_slice | solution.py:70
  9.4 1.7 copy.70
  11.1 1.7 copy.68
  12.8 1.7 copy.67
  14.4 1.7 copy.66
  16.1 1.7 copy.64
  17.8 1.7 copy.63
  19.5 1.7 copy.62
  21.2 1.6 constant_dynamic-update-slice_fusion.4
  22.7 1.6 constant_dynamic-update-slice_fusion.9
  24.3 1.6 constant_dynamic-update-slice_fusion.14
  25.8 1.6 constant_dynamic-update-slice_fusion.3
  32.0 1.7 copy.73
  40.5 4.3 %collective-permute-start = (bf16[128,1856]{0,1:T(8,128)(2,1)}, bf16[128,1856]{0,1:T(8,128)(2,1)S(1)}, u32[]{:S(2)}, u32[]{:S(2)}) collective-permute-start(bf16[128,1856]{0,1:T(8,128)(2,1)} %get-tuple-element.43), channel_id=1, source_target_pairs={{0,4},{1,5},{2,6},{3,7},{4,0},{5,1},{6,2},{7,3},{8,12},{9,13},{10,... | collective-permute-start | bytes 1425416 | tf_op jit(solution)/shard_map/ppermute | solution.py:31
  45.8 10.7 %collective-permute-done = bf16[128,1856]{0,1:T(8,128)(2,1)S(1)} collective-permute-done((bf16[128,1856]{0,1:T(8,128)(2,1)}, bf16[128,1856]{0,1:T(8,128)(2,1)S(1)}, u32[]{:S(2)}, u32[]{:S(2)}) %collective-permute-start) | collective-permute-done | bytes 475168 | tf_op jit(solution)/shard_map/ppermute | solution.py:31
  56.5 1.8 %collective-permute-start.1 = (bf16[128,1856]{0,1:T(8,128)(2,1)}, bf16[128,1856]{0,1:T(8,128)(2,1)}, u32[]{:S(2)}, u32[]{:S(2)}) collective-permute-start(bf16[128,1856]{0,1:T(8,128)(2,1)} %get-tuple-element.45), channel_id=1, source_target_pairs={{0,8},{1,9},{2,10},{3,11},{4,12},{5,13},{6,14},{7,15},{8,0},{9,1},... | collective-permute-start | bytes 1425416 | tf_op jit(solution)/shard_map/ppermute | solution.py:31
  60.4 1.7 copy.74
  64.2 4.0 %collective-permute-done.2 = bf16[128,1856]{0,1:T(8,128)(2,1)} collective-permute-done((bf16[128,1856]{0,1:T(8,128)(2,1)}, bf16[128,1856]{0,1:T(8,128)(2,1)}, u32[]{:S(2)}, u32[]{:S(2)}) %collective-permute-start.2) | collective-permute-done | bytes 475168 | tf_op jit(solution)/shard_map/ppermute | solution.py:31
  69.2 18.2 %collective-permute-done.1 = bf16[128,1856]{0,1:T(8,128)(2,1)} collective-permute-done((bf16[128,1856]{0,1:T(8,128)(2,1)}, bf16[128,1856]{0,1:T(8,128)(2,1)}, u32[]{:S(2)}, u32[]{:S(2)}) %collective-permute-start.1) | collective-permute-done | bytes 475168 | tf_op jit(solution)/shard_map/ppermute | solution.py:31
  90.0 3.6 %pad_maximum_fusion.1 = bf16[512,1792]{0,1:T(8,128)(2,1)S(1)} fusion(bf16[128,1792]{0,1:T(8,128)(2,1)S(1)} %slice.73, bf16[128,1792]{0,1:T(8,128)(2,1)S(1)} %slice.72, bf16[128,1792]{0,1:T(8,128)(2,1)S(1)} %slice.71, bf16[128,448]{0,1:T(8,128)(2,1)S(1)} %copy.77, bf16[128,448]{0,1:T(8,128)(2,1)} %copy.76, bf16[128,448]{0,1:T(8,128)(2,1)S(1)} %copy.75, ...), kind=kLoop, calls=%fused_computation.1 | loop fusion | flops 12845056 | bytes 3670016 | tf_op jit(solution)/shard_map/concatenate | solution.py:91
  95.8 3.1 %collective-permute-done.5 = bf16[128,4096]{1,0:T(8,128)(2,1)} collective-permute-done((bf16[128,4096]{1,0:T(8,128)(2,1)S(1)}, bf16[128,4096]{1,0:T(8,128)(2,1)}, u32[]{:S(2)}, u32[]{:S(2)}) %collective-permute-start.5) | collective-permute-done | bytes 1048608 | tf_op jit(solution)/shard_map/ppermute | solution.py:31
  100.3 33.9 %collective-permute-done.7 = bf16[128,4096]{1,0:T(8,128)(2,1)S(1)} collective-permute-done((bf16[128,4096]{1,0:T(8,128)(2,1)S(1)}, bf16[128,4096]{1,0:T(8,128)(2,1)S(1)}, u32[]{:S(2)}, u32[]{:S(2)}) %collective-permute-start.7) | collective-permute-done | bytes 1048608 | tf_op jit(solution)/shard_map/ppermute | solution.py:31
  134.3 3.3 %convolution_convert_fusion.3 = bf16[512,448]{0,1:T(8,128)(2,1)S(1)} fusion(bf16[448,4096]{1,0:T(8,128)(2,1)S(1)} %copy-done.4, bf16[128,4096]{1,0:T(8,128)(2,1)S(1)} %broadcast_select_fusion, bf16[128,4096]{1,0:T(8,128)(2,1)S(1)} %broadcast_select_fusion.1, bf16[128,4096]{1,0:T(8,128)(2,1)} %collective-permute-done.3, bf16[128,4096]{1,0:T(8,128)(2,1)S(1)} %copy-done.5), kind=kOutput, calls=%fused_computation.5 | convolution fusion | flops 1896054784 | bytes 8323072 | tf_op jit(solution)/shard_map/dot_general | solution.py:119
  139.0 4.5 %convolution_convert_fusion.1 = bf16[512,448]{0,1:T(8,128)(2,1)S(1)} fusion(bf16[448,4096]{1,0:T(8,128)(2,1)} %collective-permute-done.9, bf16[128,4096]{1,0:T(8,128)(2,1)S(1)} %broadcast_select_fusion, bf16[128,4096]{1,0:T(8,128)(2,1)S(1)} %broadcast_select_fusion.1, bf16[128,4096]{1,0:T(8,128)(2,1)} %collective-permute-done.3, ...), kind=kOutput, calls=%fused_computation.3 | convolution fusion | flops 1896054784 | bytes 8323072 | tf_op jit(solution)/shard_map/dot_general | solution.py:119
  143.5 3.3 %convolution_convert_fusion.2 = bf16[512,448]{0,1:T(8,128)(2,1)S(1)} fusion(bf16[448,4096]{1,0:T(8,128)(2,1)S(1)} %collective-permute-done.8, bf16[128,4096]{1,0:T(8,128)(2,1)S(1)} %broadcast_select_fusion, bf16[128,4096]{1,0:T(8,128)(2,1)S(1)} %broadcast_select_fusion.1, bf16[128,4096]{1,0:T(8,128)(2,1)} %collective-permute-done.3, ...), kind=kOutput, calls=%fused_computation.4 | convolution fusion | flops 1896054784 | bytes 8323072 | tf_op jit(solution)/shard_map/dot_general | solution.py:119
  149.5 3.3 %convolution_convert_fusion = bf16[512,448]{0,1:T(8,128)(2,1)S(1)} fusion(bf16[448,4096]{1,0:T(8,128)(2,1)S(1)} %collective-permute-done.10, bf16[128,4096]{1,0:T(8,128)(2,1)S(1)} %broadcast_select_fusion, bf16[128,4096]{1,0:T(8,128)(2,1)S(1)} %broadcast_select_fusion.1, bf16[128,4096]{1,0:T(8,128)(2,1)} %collective-permute-done.3, ...), kind=kOutput, calls=%fused_computation.2 | convolution fusion | flops 1896054784 | bytes 8323072 | tf_op jit(solution)/shard_map/dot_general | solution.py:119
  154.6 4.3 %collective-permute-done.11 = f32[4,1,4096]{2,0,1:T(4,128)S(1)} collective-permute-done((f32[4,1,4096]{2,0,1:T(4,128)S(1)}, f32[4,1,4096]{2,0,1:T(4,128)S(1)}, u32[]{:S(2)}, u32[]{:S(2)}) %collective-permute-start.11) | collective-permute-done | bytes 65568 | tf_op jit(solution)/shard_map/ppermute | solution.py:31
  159.9 4.5 %collective-permute-done.12 = f32[4,1,4096]{2,0,1:T(4,128)S(1)} collective-permute-done((f32[4,1,4096]{2,0,1:T(4,128)S(1)}, f32[4,1,4096]{2,0,1:T(4,128)S(1)}, u32[]{:S(2)}, u32[]{:S(2)}) %collective-permute-start.12) | collective-permute-done | bytes 65568 | tf_op jit(solution)/shard_map/ppermute | solution.py:31
  168.5 3.7 %collective-permute-done.14 = bf16[4,2,1,4096]{3,0,2,1:T(4,128)(2,1)S(1)} collective-permute-done((bf16[4,2,1,4096]{3,0,2,1:T(4,128)(2,1)S(1)}, bf16[4,2,1,4096]{3,0,2,1:T(4,128)(2,1)S(1)}, u32[]{:S(2)}, u32[]{:S(2)}) %collective-permute-start.14) | collective-permute-done | bytes 65568 | tf_op jit(solution)/shard_map/ppermute | solution.py:31
  172.5 5.1 %convolution_select_fusion = f32[16,768]{1,0:T(8,128)} fusion(bf16[16,4096]{1,0:T(8,128)(2,1)S(1)} %select_n.220, bf16[768,4096]{1,0:T(8,128)(2,1)} %param.14, s32[768]{0:T(1024)S(1)} %iota_add_fusion, s32[16]{0:T(128)S(1)} %copy-done.3), kind=kOutput, calls=%fused_computation.18 | convolution fusion | flops 100687872 | bytes 6474816 | tf_op jit(solution)/shard_map/dot_general | solution.py:156
  (94 shorter events, 35.3 us)
Async XLA Ops:
  0.0 39.4 %copy-start = (bf16[128,4096]{1,0:T(8,128)(2,1)S(1)}, bf16[128,4096]{1,0:T(8,128)(2,1)}, u32[]{:S(2)}) copy-start(bf16[128,4096]{1,0:T(8,128)(2,1)} %param.8) | copy-start | bytes 3145732
  0.0 58.3 %collective-permute-start.3 = (bf16[128,4096]{1,0:T(8,128)(2,1)}, bf16[128,4096]{1,0:T(8,128)(2,1)}, u32[]{:S(2)}, u32[]{:S(2)}) collective-permute-start(bf16[128,4096]{1,0:T(8,128)(2,1)} %param.10), channel_id=1, source_target_pairs={{0,4},{1,5},{2,6},{3,7},{4,0},{5,1},{6,2},{7,3},{8,12},{9,13},{10,... | collective-permute-start | bytes 3145736 | tf_op jit(solution)/shard_map/ppermute | solution.py:31
  3.0 56.0 %collective-permute-start.4 = (bf16[128,4096]{1,0:T(8,128)(2,1)}, bf16[128,4096]{1,0:T(8,128)(2,1)S(1)}, u32[]{:S(2)}, u32[]{:S(2)}) collective-permute-start(bf16[128,4096]{1,0:T(8,128)(2,1)} %param.10), channel_id=1, source_target_pairs={{4,8},{5,9},{6,10},{7,11},{8,4},{9,5},{10,6},{11,7},{20,24},{21,25... | collective-permute-start | bytes 3145736 | tf_op jit(solution)/shard_map/ppermute | solution.py:31
  3.8 96.5 %collective-permute-start.9 = (bf16[448,4096]{1,0:T(8,128)(2,1)}, bf16[448,4096]{1,0:T(8,128)(2,1)}, u32[]{:S(2)}, u32[]{:S(2)}) collective-permute-start(bf16[448,4096]{1,0:T(8,128)(2,1)} %param.11), channel_id=1, source_target_pairs={{0,2},{1,3},{2,0},{3,1},{4,6},{5,7},{6,4},{7,5},{8,10},{9,11},{10,... | collective-permute-start | bytes 11010056 | tf_op jit(solution)/shard_map/ppermute | solution.py:31
  5.3 34.1 %copy-start.1 = (bf16[4096,64]{0,1:T(8,128)(2,1)S(1)}, bf16[4096,64]{0,1:T(8,128)(2,1)}, u32[]{:S(2)}) copy-start(bf16[4096,64]{0,1:T(8,128)(2,1)} %param.12) | copy-start | bytes 1572868
  40.5 16.0 %collective-permute-start = (bf16[128,1856]{0,1:T(8,128)(2,1)}, bf16[128,1856]{0,1:T(8,128)(2,1)S(1)}, u32[]{:S(2)}, u32[]{:S(2)}) collective-permute-start(bf16[128,1856]{0,1:T(8,128)(2,1)} %get-tuple-element.43), channel_id=1, source_target_pairs={{0,4},{1,5},{2,6},{3,7},{4,0},{5,1},{6,2},{7,3},{8,12},{9,13},{10,... | collective-permute-start | bytes 1425416 | tf_op jit(solution)/shard_map/ppermute | solution.py:31
  44.8 23.3 %collective-permute-start.2 = (bf16[128,1856]{0,1:T(8,128)(2,1)}, bf16[128,1856]{0,1:T(8,128)(2,1)}, u32[]{:S(2)}, u32[]{:S(2)}) collective-permute-start(bf16[128,1856]{0,1:T(8,128)(2,1)} %get-tuple-element.44), channel_id=1, source_target_pairs={{0,12},{1,13},{2,14},{3,15},{4,8},{5,9},{6,10},{7,11},{8,4},{9,5},... | collective-permute-start | bytes 1425416 | tf_op jit(solution)/shard_map/ppermute | solution.py:31
  56.5 2.6 %copy-start.2 = (bf16[128,1856]{0,1:T(8,128)(2,1)}, bf16[128,1856]{0,1:T(8,128)(2,1)S(1)}, u32[]{:S(2)}) copy-start(bf16[128,1856]{0,1:T(8,128)(2,1)S(1)} %collective-permute-done) | copy-start | bytes 1425412
  56.5 31.0 %collective-permute-start.1 = (bf16[128,1856]{0,1:T(8,128)(2,1)}, bf16[128,1856]{0,1:T(8,128)(2,1)}, u32[]{:S(2)}, u32[]{:S(2)}) collective-permute-start(bf16[128,1856]{0,1:T(8,128)(2,1)} %get-tuple-element.45), channel_id=1, source_target_pairs={{0,8},{1,9},{2,10},{3,11},{4,12},{5,13},{6,14},{7,15},{8,0},{9,1},... | collective-permute-start | bytes 1425416 | tf_op jit(solution)/shard_map/ppermute | solution.py:31
  58.3 35.3 %collective-permute-start.6 = (bf16[128,4096]{1,0:T(8,128)(2,1)}, bf16[128,4096]{1,0:T(8,128)(2,1)S(1)}, u32[]{:S(2)}, u32[]{:S(2)}) collective-permute-start(bf16[128,4096]{1,0:T(8,128)(2,1)} %collective-permute-done.3), channel_id=1, source_target_pairs={{4,8},{5,9},{6,10},{7,11},{8,4},{9,5},{10,6},{11,7},{20,24},{21,25... | collective-permute-start | bytes 3145736 | tf_op jit(solution)/shard_map/ppermute | solution.py:31
  59.1 39.8 %collective-permute-start.5 = (bf16[128,4096]{1,0:T(8,128)(2,1)S(1)}, bf16[128,4096]{1,0:T(8,128)(2,1)}, u32[]{:S(2)}, u32[]{:S(2)}) collective-permute-start(bf16[128,4096]{1,0:T(8,128)(2,1)S(1)} %collective-permute-done.4), channel_id=1, source_target_pairs={{4,0},{5,1},{6,2},{7,3},{8,12},{9,13},{10,14},{11,15},{20,16},{21,... | collective-permute-start | bytes 3145736 | tf_op jit(solution)/shard_map/ppermute | solution.py:31
  68.2 75.3 %collective-permute-start.8 = (bf16[448,4096]{1,0:T(8,128)(2,1)}, bf16[448,4096]{1,0:T(8,128)(2,1)S(1)}, u32[]{:S(2)}, u32[]{:S(2)}) collective-permute-start(bf16[448,4096]{1,0:T(8,128)(2,1)} %param.11), channel_id=1, source_target_pairs={{0,1},{1,0},{2,3},{3,2},{4,5},{5,4},{6,7},{7,6},{8,9},{9,8},{10,11... | collective-permute-start | bytes 11010056 | tf_op jit(solution)/shard_map/ppermute | solution.py:31
  90.0 44.4 %copy-start.4 = (bf16[448,4096]{1,0:T(8,128)(2,1)S(1)}, bf16[448,4096]{1,0:T(8,128)(2,1)}, u32[]{:S(2)}) copy-start(bf16[448,4096]{1,0:T(8,128)(2,1)} %param.11) | copy-start | bytes 11010052
  90.0 44.4 %copy-start.5 = (bf16[128,4096]{1,0:T(8,128)(2,1)S(1)}, bf16[128,4096]{1,0:T(8,128)(2,1)}, u32[]{:S(2)}) copy-start(bf16[128,4096]{1,0:T(8,128)(2,1)} %param.10) | copy-start | bytes 3145732
  93.6 40.6 %collective-permute-start.7 = (bf16[128,4096]{1,0:T(8,128)(2,1)S(1)}, bf16[128,4096]{1,0:T(8,128)(2,1)S(1)}, u32[]{:S(2)}, u32[]{:S(2)}) collective-permute-start(bf16[128,4096]{1,0:T(8,128)(2,1)S(1)} %collective-permute-done.6), channel_id=1, source_target_pairs={{4,0},{5,1},{6,2},{7,3},{8,12},{9,13},{10,14},{11,15},{20,16},{21,... | collective-permute-start | bytes 3145736 | tf_op jit(solution)/shard_map/ppermute | solution.py:31
  100.2 49.3 %collective-permute-start.10 = (bf16[448,4096]{1,0:T(8,128)(2,1)}, bf16[448,4096]{1,0:T(8,128)(2,1)S(1)}, u32[]{:S(2)}, u32[]{:S(2)}) collective-permute-start(bf16[448,4096]{1,0:T(8,128)(2,1)} %collective-permute-done.9), channel_id=1, source_target_pairs={{0,1},{1,0},{2,3},{3,2},{4,5},{5,4},{6,7},{7,6},{8,9},{9,8},{10,11... | collective-permute-start | bytes 11010056 | tf_op jit(solution)/shard_map/ppermute | solution.py:31
  152.9 19.6 %copy-start.3 = (s32[16]{0:T(128)S(1)}, s32[16]{0:T(128)}, u32[]{:S(2)}) copy-start(s32[16]{0:T(128)} %param.15) | copy-start | bytes 196
  154.5 4.3 %collective-permute-start.11 = (f32[4,1,4096]{2,0,1:T(4,128)S(1)}, f32[4,1,4096]{2,0,1:T(4,128)S(1)}, u32[]{:S(2)}, u32[]{:S(2)}) collective-permute-start(f32[4,1,4096]{2,0,1:T(4,128)S(1)} %reshape.768), channel_id=1, source_target_pairs={{0,4},{1,5},{2,6},{3,7},{4,0},{5,1},{6,2},{7,3},{8,12},{9,13},{10,... | collective-permute-start | bytes 196616 | tf_op jit(solution)/shard_map/ppermute | solution.py:31
  159.1 5.4 %collective-permute-start.12 = (f32[4,1,4096]{2,0,1:T(4,128)S(1)}, f32[4,1,4096]{2,0,1:T(4,128)S(1)}, u32[]{:S(2)}, u32[]{:S(2)}) collective-permute-start(f32[4,1,4096]{2,0,1:T(4,128)S(1)} %get-tuple-element.42), channel_id=1, source_target_pairs={{0,8},{1,9},{2,10},{3,11},{4,12},{5,13},{6,14},{7,15},{8,0},{9,1},... | collective-permute-start | bytes 196616 | tf_op jit(solution)/shard_map/ppermute | solution.py:31
  166.5 1.3 collective-permute-start.13
  167.9 4.3 %collective-permute-start.14 = (bf16[4,2,1,4096]{3,0,2,1:T(4,128)(2,1)S(1)}, bf16[4,2,1,4096]{3,0,2,1:T(4,128)(2,1)S(1)}, u32[]{:S(2)}, u32[]{:S(2)}) collective-permute-start(bf16[4,2,1,4096]{3,0,2,1:T(4,128)(2,1)S(1)} %maximum_select_fusion.1), channel_id=1, source_target_pairs={{0,2},{1,3},{2,0},{3,1},{4,6},{5,7},{6,4},{7,5},{8,10},{9,11},{10,... | collective-permute-start | bytes 196616 | tf_op jit(solution)/shard_map/ppermute | solution.py:31

commit v2 on v1

v2 whole, which is shorter than its diff:
```python
import functools

import jax
import jax.numpy as jnp
from jax import lax
from jax.experimental import pallas as pl
from jax.experimental.pallas import tpu as pltpu
from jax.sharding import PartitionSpec as P

SEQ_LEN = 128
LANE_SHIFT = 2
LANES = 4
QUADS = 1 << LANE_SHIFT
BF16, F32 = jnp.bfloat16, jnp.float32
LINK = jnp.bfloat16


def chunk_sizes(rows):
    return [rows]


def place(both, core_first, piece, target, far):
    parts = [both[:, :piece], both[:, piece:]]
    if not core_first:
        parts = parts[::-1]
    if not far:
        target[:, : 2 * piece] = jnp.concatenate(parts, axis=1)
        return
    start = 2 * piece
    cut = 0
    for size in chunk_sizes(piece):
        pair = [part[:, cut : cut + size] for part in parts]
        target[:, start : start + 2 * size] = jnp.concatenate(pair, axis=1)
        cut += size
        start += 2 * size


def arrange_kernel(piece, where_ref, gate_ref, rows_ref, g0, g1, g2, g3, out_ref):
    lane, side, core = where_ref[0], where_ref[1], where_ref[2]
    wide = 2 * piece
    for value in range(2):

        @pl.when(core == value)
        def _():
            for k, target in enumerate((g0, g1, g2, g3)):
                for far in range(2):
                    block = (lane ^ k) * 2 + (side ^ far)
                    start = pl.multiple_of(block * wide, 128)
                    both = gate_ref[:, pl.ds(start, wide)]
                    place(both, value == 0, piece, target, far)
                    if k == 0:
                        both = rows_ref[:, pl.ds(start, wide)]
                        place(both, value == 0, piece, out_ref, far)


def arrange(gate, rows, position, piece):
    lane = position >> LANE_SHIFT & LANES - 1
    quad = position & QUADS - 1
    total = gate.shape[1]
    outer = total // (piece * QUADS * LANES)
    mine = total // LANES
    if outer == 1 and 2 * piece % 128 == 0:
        where = jnp.stack([lane, quad >> 1, quad & 1]).astype(jnp.int32)
        vmem = pl.BlockSpec(memory_space=pltpu.VMEM)
        return pl.pallas_call(
            functools.partial(arrange_kernel, piece),
            out_shape=[jax.ShapeDtypeStruct((gate.shape[0], mine), gate.dtype)] * LANES
            + [jax.ShapeDtypeStruct((rows.shape[0], mine), rows.dtype)],
            in_specs=[pl.BlockSpec(memory_space=pltpu.SMEM), vmem, vmem],
            out_specs=[vmem] * (LANES + 1),
            cost_estimate=pl.CostEstimate(
                flops=0, bytes_accessed=4 * gate.size + 4 * rows.size, transcendentals=0
            ),
        )(where, gate, rows)

    def block(value, k):
        whole = []
        for w in range(QUADS):
            index = (lane ^ k) * QUADS + (quad ^ w)
            parts = []
            for o in range(outer):
                start = (o * QUADS * LANES + index) * piece
                parts.append(lax.dynamic_slice_in_dim(value, start, piece, axis=1))
            whole.append(jnp.concatenate(parts, axis=1))
        parts = whole[:2]
        cut = 0
        for size in chunk_sizes(outer * piece):
            parts += [whole[2][:, cut : cut + size], whole[3][:, cut : cut + size]]
            cut += size
        return jnp.concatenate(parts, axis=1)

    return [block(gate, k) for k in range(LANES)] + [block(rows, 0)]


def after(value, *others):
    return lax.optimization_barrier((value,) + others)[0]


def call(body, out_shape, in_specs, out_specs, **kwargs):
    return pl.pallas_call(
        body,
        out_shape=out_shape,
        in_specs=in_specs,
        out_specs=out_specs,
        cost_estimate=pl.CostEstimate(flops=1000, bytes_accessed=1000, transcendentals=0),
        **kwargs,
    )


def feature_kernel(spans, slots, tokens, examples, *refs):
    count = sum(len(span) for span in spans)
    blocks = refs[:count]
    gates = refs[count : count + len(slots)]
    ins = refs[count + len(slots) : count + 2 * len(slots)]
    rows_ref, *before, out_ref = refs[count + 2 * len(slots) :]
    rank = rows_ref.shape[0]
    for k in range(LANES):
        if before and k not in slots:
            out_ref[k] = before[0][k]
    for slot, k in enumerate(slots):
        total = jnp.zeros((rank, tokens), F32)
        start = 0
        index = 0
        for span in spans:
            first = 0
            for i, height in enumerate(span):
                if first <= k * tokens < first + height:
                    block = blocks[index + i]
                    top = k * tokens - first
                first += height
            index += len(span)
            stop = start + block.shape[1]
            gate = gates[slot][:, start:stop].astype(F32)
            up_grad = (
                block[top : top + tokens, :].astype(F32)
                * (0.5 * gate * (1.0 + jnp.tanh(0.5 * gate)))
            ).astype(BF16)
            total += lax.dot_general(
                rows_ref[:, start:stop],
                up_grad,
                (((1,), (1,)), ((), ())),
                preferred_element_type=F32,
            )
            start = stop
        for e in range(examples):
            cut = slice(e * SEQ_LEN, (e + 1) * SEQ_LEN)
            feature = lax.dot_general(
                ins[slot][:, cut].astype(F32),
                total[:, cut],
                (((1,), (1,)), ((), ())),
                precision=lax.Precision.HIGHEST,
                preferred_element_type=F32,
            )
            out_ref[k, e] = jnp.concatenate(
                [feature[: rank // 2], feature[rank // 2 :]], axis=1
            ).astype(out_ref.dtype)


def features(slots, blocks, gates, ins, out_rows, *before):
    tokens = gates[0].shape[0]
    rank = out_rows.shape[0]
    examples = tokens // SEQ_LEN
    spans = [[part.shape[0] for part in parts] for parts in blocks]
    operands = (*[part for parts in blocks for part in parts], *gates, *ins, out_rows, *before)
    vmem = pl.BlockSpec(memory_space=pltpu.VMEM)
    return call(
        functools.partial(feature_kernel, spans, slots, tokens, examples),
        jax.ShapeDtypeStruct((LANES, examples, rank // 2, 2 * rank), LINK),
        [vmem] * len(operands),
        vmem,
    )(*operands)


def scale_kernel(own, *refs):
    others, out_ref = refs[:-1], refs[-1]
    width = own.shape[2] * own.shape[3]
    for j in range(LANES):
        total = own[j].astype(F32)
        for k in range(1, LANES):
            total += others[k - 1][j ^ k].astype(F32)
        square = jnp.sum(jnp.sum(total * total, axis=2, keepdims=True), axis=1, keepdims=True)
        out_ref[j] = (total * lax.rsqrt(square / width + 1e-06)).astype(BF16)


def scaled(own, others):
    vmem = pl.BlockSpec(memory_space=pltpu.VMEM)
    return call(
        scale_kernel,
        jax.ShapeDtypeStruct(own.shape, BF16),
        [vmem] * LANES,
        vmem,
    )(own, *others)


def score_kernel(where_ref, q0, q1, q2, q3, visible_ref, stored_ref, out_ref, rows):
    position = where_ref[0]
    for w, source in enumerate((q0, q1, q2, q3)):
        for k in range(LANES):
            row = k * QUADS + w
            value = source[k, 0].astype(F32)
            for j in range(value.shape[0]):
                rows[row : row + 1, j * 128 : (j + 1) * 128] = value[j : j + 1, :]
    products = lax.dot_general(
        rows[...].astype(BF16),
        stored_ref[...],
        (((1,), (1,)), ((), ())),
        preferred_element_type=F32,
    )
    count = out_ref.shape[1]
    index = lax.broadcasted_iota(jnp.int32, products.shape, 0)
    for bit in (1, 2, 4, 8):
        swapped = jnp.where(
            index & bit != 0,
            pltpu.roll(products, bit, 0),
            pltpu.roll(products, products.shape[0] - bit, 0),
        )
        products = jnp.where(jnp.full(products.shape, position) & bit != 0, swapped, products)
    column = position * count + lax.broadcasted_iota(jnp.int32, products.shape, 1)
    out_ref[...] = jnp.where(column < visible_ref[...], products, 0.0)


def scores(where, queries, visible, stored):
    vmem = pl.BlockSpec(memory_space=pltpu.VMEM)
    examples = LANES * QUADS
    return call(
        score_kernel,
        jax.ShapeDtypeStruct((examples, stored.shape[0]), F32),
        [pl.BlockSpec(memory_space=pltpu.SMEM)] + [vmem] * 6,
        vmem,
        scratch_shapes=[pltpu.VMEM((examples, stored.shape[1]), F32)],
    )(where, *queries, visible[:, None], stored)


def shards(activations, gate_pre, out_grad, down_weight, proj_in, proj_out, stored, visible):
    devices = lax.axis_size("row")
    position = lax.axis_index("row")
    total_bits = devices.bit_length() - 1
    lane = position >> LANE_SHIFT & LANES - 1
    tokens = out_grad.shape[0]
    rank = proj_in.shape[1]

    def send(value, move):
        pairs = []
        for i in range(devices):
            target = move(i)
            if target is not None:
                pairs.append((i, target))
        return lax.ppermute(value, "row", pairs)

    def flip(bits):
        return lambda i: i ^ bits

    def lane_move(table):
        def move(i):
            to = table.get(i >> LANE_SHIFT & LANES - 1)
            return None if to is None else i & ~((LANES - 1) << LANE_SHIFT) | to << LANE_SHIFT

        return move

    def join(value, other, bit, axis):
        return jnp.where(
            position >> bit & 1 == 1,
            jnp.concatenate([other, value], axis=axis),
            jnp.concatenate([value, other], axis=axis),
        )

    def gather_high(value, axis):
        for bit in range(LANE_SHIFT + 2, total_bits):
            value = join(value, send(value, flip(1 << bit)), bit, axis)
        return value

    middle_swap = lane_move({1: 2, 2: 1})
    to_ends = lane_move({1: 0, 2: 3})
    at_end = (lane == 0) | (lane == LANES - 1)

    own_w = gather_high(down_weight, 0)
    rows = own_w.shape[0]

    tie = lax.optimization_barrier
    grad_a = send(out_grad, flip(1 << LANE_SHIFT))
    grad_b = send(out_grad, middle_swap)
    far_w = send(own_w, flip(2))
    core_w = send(own_w, flip(1))

    *gate_out, out_rows = arrange(gate_pre, proj_out.T, position, down_weight.shape[0])
    width = proj_in.shape[0]
    paired = proj_in.T.reshape(rank // 2, 2, width).transpose(1, 0, 2).reshape(rank, width)
    in_proj = lax.dot_general(
        paired, activations, (((1,), (1,)), ((), ())), preferred_element_type=F32
    ).astype(BF16)
    grad_a, core_w, in_proj, gate_out = tie((grad_a, core_w, in_proj, gate_out))

    grad_c = send(grad_a, middle_swap)
    in_1 = send(in_proj, flip(1 << LANE_SHIFT))
    grad_d = send(grad_b, to_ends)
    grad_c, in_1, gate_out = tie((grad_c, in_1, gate_out))

    grad_e = send(grad_c, to_ends)
    gate_3 = send(gate_out[3], flip(3 << LANE_SHIFT))
    in_2 = send(jnp.stack([in_proj, in_1]), flip(2 << LANE_SHIFT))
    ins = [in_proj, in_1, in_2[0], in_2[1]]
    early = jnp.concatenate([out_grad, grad_a, jnp.where(at_end, grad_d, grad_c)], axis=0)

    def hidden(grads, weight):
        return lax.dot_general(
            grads, weight, (((1,), (1,)), ((), ())), preferred_element_type=F32
        ).astype(BF16)

    first = [hidden(early, w) for w in (own_w, core_w)]
    grad_e, gate_3, far_w, gate_out, first, ins = tie(
        (grad_e, gate_3, far_w, gate_out, first, ins)
    )

    cross_w = send(far_w, flip(1))
    gate_2 = send(gate_out[2], flip(2 << LANE_SHIFT))
    gate_1 = send(gate_out[1], flip(1 << LANE_SHIFT))
    late = jnp.where(at_end, grad_e, grad_b)
    grads = jnp.concatenate([early, late], axis=0)
    blocks = [(h, hidden(late, w)) for h, w in zip(first, (own_w, core_w))]
    blocks += [(hidden(grads, w),) for w in (far_w, cross_w)]
    half = features((0, 3), blocks, [gate_out[0], gate_3], [ins[0], ins[3]], out_rows)
    gate_1, gate_2, half = tie((gate_1, gate_2, half))
    own = features((1, 2), blocks, [gate_1, gate_2], ins[1:3], out_rows, half)
    queries = scaled(own, [send(own, flip(k << LANE_SHIFT)) for k in range(1, LANES)])
    quad = position & QUADS - 1
    everyone = [queries] + [send(queries, flip(q)) for q in range(1, QUADS)]
    if devices == LANES * QUADS and tokens == SEQ_LEN:
        where = position.astype(jnp.int32).reshape(1)
        return scores(where, everyone, visible, stored)

    examples_dev = tokens // SEQ_LEN
    everyone = jnp.stack(everyone, axis=1).reshape(LANES * QUADS, examples_dev, rank * rank)
    order = jnp.arange(LANES * QUADS)
    order = (order >> LANE_SHIFT ^ lane) * QUADS + (order & QUADS - 1 ^ quad)
    pick = (order[:, None] == jnp.arange(LANES * QUADS)[None, :]).astype(BF16)
    everyone = jnp.einsum("ij,jef->ief", pick, everyone, preferred_element_type=F32).astype(BF16)
    queries = gather_high(everyone, 0).reshape(devices * examples_dev, rank * rank)
    stored_rows = stored.shape[0]
    column = position * stored_rows + jnp.arange(stored_rows, dtype=jnp.int32)
    products = lax.dot_general(
        queries, stored, (((1,), (1,)), ((), ())), preferred_element_type=F32
    )
    return jnp.where(column[None, :] < visible[:, None], products, F32(0.0))


def solution(mesh):
    return jax.shard_map(
        shards,
        mesh=mesh,
        in_specs=(
            P(("ckpt", "row"), None),
            P(("ckpt", "row"), None),
            P(("ckpt", "row"), None),
            P(("ckpt", "row"), None),
            P(),
            P(),
            P(("ckpt", "row"), None),
            P(),
        ),
        out_specs=P("ckpt", "row"),
        check_vma=False,
    )
```

time: 179 us -> 143 us (0.80)
  local copies, waits for them, and re-layouts: 44.8 us -> 5.6 us
  waiting for transfers between devices: 83.6 us -> 64.2 us
  Pallas kernels: 0 us -> 17.8 us
  starting transfers between devices: 16.7 us -> 26.3 us
  other arithmetic: 5.96 us -> 2.14 us
    unnamed x39 -> x34, local copies, waits for them, and re-layouts: 32.7 us -> 2.65 us
    ppermute x15 -> x19, waiting for transfers between devices: 83.6 us -> 64.2 us  [send(): return lax.ppermute(value, 'row', pairs)]
    pallas_call x0 -> x5, Pallas kernels: none -> 17.8 us  [the longest x2 7.7 us: features(): call(functools.partial(feature_kernel, spans, slots, tokens, examples), j...]
    ppermute x15 -> x19, starting transfers between devices: 16.7 us -> 26.3 us  [send(): return lax.ppermute(value, 'row', pairs)]
    dynamic_slice x1 -> x0, local copies, waits for them, and re-layouts: 4.13 us -> none  [columns(): lax.dynamic_slice_in_dim(gate_pre, (o * blocks + block) * piece, piece, a...]
    concatenate x2 -> x0, other arithmetic: 3.71 us -> none  [the longest x1 3.61 us: shards(): gates = jnp.concatenate(gates, axis=0)]
    slice x3 -> x0, local copies, waits for them, and re-layouts: 3.15 us -> none  [shards(): gates.append(got[:, :hidden_group])]
    another operation x15 -> x0, local copies, waits for them, and re-layouts: 3.12 us -> none  [the longest x3 2.16 us: shards(): jnp.stack(ins).reshape(LANES, examples_dev, SEQ_LEN, rank).astype(f32)]
  transfers between devices with their start and end apart: 15 -> 19, of which waited for: 9 -> 9; matrix products, arithmetic and copies ran while one was open for 36% -> 22% of each run, Pallas kernels for 0% -> 5%
where the time goes in v2:
time: 143 us; the launch traced here: 142 us
  waiting for transfers between devices  64.2 us (45%)
  starting transfers between devices  26.3 us (18%)
  matrix products  26.3 us (18%)
  Pallas kernels  17.8 us (12%)
  local copies, waits for them, and re-layouts  5.6 us (4%)
  other arithmetic  2.14 us (1%)
    ppermute x19, waiting for transfers between devices, send(): return lax.ppermute(value, 'row', pairs)  64.2 us
    ppermute x19, starting transfers between devices, send(): return lax.ppermute(value, 'row', pairs)  26.3 us
    dot_general x6, matrix products, hidden(): lax.dot_general(grads, weight, (((1,), (1,)), ((), ())), preferred_elemen...  25.8 us
    pallas_call x2, Pallas kernels, features(): call(functools.partial(feature_kernel, spans, slots, tokens, examples), j...  7.7 us
    pallas_call x1, Pallas kernels, scores(): call(score_kernel, jax.ShapeDtypeStruct((examples, stored.shape[0]), F32)...  5.29 us
    pallas_call x1, Pallas kernels, arrange(): pl.pallas_call(functools.partial(arrange_kernel, piece), out_shape=[jax.S...  3.24 us
  transfers between devices with their start and end apart: 19, of which 9 were waited for; matrix products, arithmetic and copies ran while one was open for 22% of the time, Pallas kernels for 5%

profile of v2, /device:TPU:0, one launch (start us, length us, event | category | flops | bytes accessed | tf_op | source)
XLA Modules:
  0.0 142.4 jit_solution(12249313323660933916)
XLA Ops:
  0.5 2.6 %collective-permute-start = (bf16[128,4096]{1,0:T(8,128)(2,1)}, bf16[128,4096]{1,0:T(8,128)(2,1)}, u32[]{:S(2)}, u32[]{:S(2)}) collective-permute-start(bf16[128,4096]{1,0:T(8,128)(2,1)} %param.10), channel_id=1, source_target_pairs={{0,4},{1,5},{2,6},{3,7},{4,0},{5,1},{6,2},{7,3},{8,12},{9,13},{10,... | collective-permute-start | bytes 3145736 | tf_op jit(solution)/shard_map/ppermute | solution.py:248
  3.8 1.6 %collective-permute-start.6 = (bf16[448,4096]{1,0:T(8,128)(2,1)}, bf16[448,4096]{1,0:T(8,128)(2,1)}, u32[]{:S(2)}, u32[]{:S(2)}) collective-permute-start(bf16[448,4096]{1,0:T(8,128)(2,1)} %param.11), channel_id=1, source_target_pairs={{0,2},{1,3},{2,0},{3,1},{4,6},{5,7},{6,4},{7,5},{8,10},{9,11},{10,... | collective-permute-start | bytes 11010056 | tf_op jit(solution)/shard_map/ppermute | solution.py:248
  5.4 1.4 reshape.10
  8.2 3.2 %shard_map.82 = (bf16[128,1792]{1,0:T(8,128)(2,1)}, bf16[128,1792]{1,0:T(8,128)(2,1)}, bf16[128,1792]{1,0:T(8,128)(2,1)}, bf16[128,1792]{1,0:T(8,128)(2,1)}, bf16[64,1792]{1,0:T(8,128)(2,1)}) custom-call(s32[3]{0:T(128)} %pad_add_fusion.where_ref, bf16[128,7168]{1,0:T(8,128)(2,1)} %gate_ref.1, bf16[64,7168]{1,0:T(8,128)(2,1)} %bitcast.27), custom_call_target="tpu_custom_call" | custom-call | bytes 5505024 | tf_op jit(solution)/shard_map/pallas_call | solution.py:65
  11.5 15.7 %collective-permute-done = bf16[128,4096]{1,0:T(8,128)(2,1)} collective-permute-done((bf16[128,4096]{1,0:T(8,128)(2,1)}, bf16[128,4096]{1,0:T(8,128)(2,1)}, u32[]{:S(2)}, u32[]{:S(2)}) %collective-permute-start) | collective-permute-done | bytes 1048608 | tf_op jit(solution)/shard_map/ppermute | solution.py:248
  27.2 1.7 %collective-permute-start.2 = (bf16[128,4096]{1,0:T(8,128)(2,1)}, bf16[128,4096]{1,0:T(8,128)(2,1)}, u32[]{:S(2)}, u32[]{:S(2)}) collective-permute-start(bf16[128,4096]{1,0:T(8,128)(2,1)} %collective-permute-done), channel_id=1, source_target_pairs={{4,8},{5,9},{6,10},{7,11},{8,4},{9,5},{10,6},{11,7},{20,24},{21,25... | collective-permute-start | bytes 3145736 | tf_op jit(solution)/shard_map/ppermute | solution.py:248
  28.9 1.3 collective-permute-start.8
  30.1 4.6 %collective-permute-start.3 = (bf16[64,128]{1,0:T(8,128)(2,1)S(1)}, bf16[64,128]{1,0:T(8,128)(2,1)S(1)}, u32[]{:S(2)}, u32[]{:S(2)}) collective-permute-start(bf16[64,128]{1,0:T(8,128)(2,1)S(1)} %convolution_convert_fusion.4.refs_8_), channel_id=1, source_target_pairs={{0,4},{1,5},{2,6},{3,7},{4,0},{5,1},{6,2},{7,3},{8,12},{9,13},{10,... | collective-permute-start | bytes 49160 | tf_op jit(solution)/shard_map/ppermute | solution.py:248
  34.7 22.0 %collective-permute-done.3.refs_8_ = bf16[64,128]{1,0:T(8,128)(2,1)S(1)} collective-permute-done((bf16[64,128]{1,0:T(8,128)(2,1)S(1)}, bf16[64,128]{1,0:T(8,128)(2,1)S(1)}, u32[]{:S(2)}, u32[]{:S(2)}) %collective-permute-start.3) | collective-permute-done | bytes 16416 | tf_op jit(solution)/shard_map/ppermute | solution.py:248
  57.7 1.5 %collective-permute-start.4 = (bf16[128,4096]{1,0:T(8,128)(2,1)}, bf16[128,4096]{1,0:T(8,128)(2,1)S(1)}, u32[]{:S(2)}, u32[]{:S(2)}) collective-permute-start(bf16[128,4096]{1,0:T(8,128)(2,1)} %collective-permute-done.2), channel_id=1, source_target_pairs={{4,0},{5,1},{6,2},{7,3},{8,12},{9,13},{10,14},{11,15},{20,16},{21,... | collective-permute-start | bytes 3145736 | tf_op jit(solution)/shard_map/ppermute | solution.py:248
  59.2 1.3 broadcast_select_fusion.1
  60.6 5.0 %fusion.2.refs_0_ = bf16[384,448]{1,0:T(8,128)(2,1)} fusion(bf16[448,4096]{1,0:T(8,128)(2,1)} %param.11, bf16[128,4096]{1,0:T(8,128)(2,1)S(1)} %broadcast_select_fusion.1, bf16[128,4096]{1,0:T(8,128)(2,1)} %collective-permute-done, bf16[128,4096]{1,0:T(8,128)(2,1)S(1)} %copy-done.14), kind=kOutput, calls=%fused_computation.6 | convolution fusion | flops 1418895360 | bytes 7159808 | tf_op jit(solution)/shard_map/dot_general | solution.py:305
  65.6 2.0 %collective-permute-start.5 = (bf16[128,1792]{1,0:T(8,128)(2,1)S(1)}, bf16[128,1792]{1,0:T(8,128)(2,1)S(1)}, u32[]{:S(2)}, u32[]{:S(2)}) collective-permute-start(bf16[128,1792]{1,0:T(8,128)(2,1)S(1)} %copy-done.16), channel_id=1, source_target_pairs={{0,12},{1,13},{2,14},{3,15},{4,8},{5,9},{6,10},{7,11},{8,4},{9,5},... | collective-permute-start | bytes 1376264 | tf_op jit(solution)/shard_map/ppermute | solution.py:248
  67.6 5.0 %fusion.3.refs_2_ = bf16[384,448]{1,0:T(8,128)(2,1)} fusion(bf16[448,4096]{1,0:T(8,128)(2,1)} %collective-permute-done.1, bf16[128,4096]{1,0:T(8,128)(2,1)S(1)} %broadcast_select_fusion.1, bf16[128,4096]{1,0:T(8,128)(2,1)} %collective-permute-done, bf16[128,4096]{1,0:T(8,128)(2,1)S(1)} %copy-done.14), kind=kOutput, calls=%fused_computation.7 | convolution fusion | flops 1418895360 | bytes 7159808 | tf_op jit(solution)/shard_map/dot_general | solution.py:305
  73.2 12.4 %collective-permute-done.6 = bf16[448,4096]{1,0:T(8,128)(2,1)} collective-permute-done((bf16[448,4096]{1,0:T(8,128)(2,1)}, bf16[448,4096]{1,0:T(8,128)(2,1)}, u32[]{:S(2)}, u32[]{:S(2)}) %collective-permute-start.6) | collective-permute-done | bytes 3670048 | tf_op jit(solution)/shard_map/ppermute | solution.py:248
  85.6 8.2 %collective-permute-done.4 = bf16[128,4096]{1,0:T(8,128)(2,1)S(1)} collective-permute-done((bf16[128,4096]{1,0:T(8,128)(2,1)}, bf16[128,4096]{1,0:T(8,128)(2,1)S(1)}, u32[]{:S(2)}, u32[]{:S(2)}) %collective-permute-start.4) | collective-permute-done | bytes 1048608 | tf_op jit(solution)/shard_map/ppermute | solution.py:248
  93.8 2.7 %collective-permute-start.12 = (bf16[128,1792]{1,0:T(8,128)(2,1)}, bf16[128,1792]{1,0:T(8,128)(2,1)S(1)}, u32[]{:S(2)}, u32[]{:S(2)}) collective-permute-start(bf16[128,1792]{1,0:T(8,128)(2,1)} %get-tuple-element.60), channel_id=1, source_target_pairs={{0,8},{1,9},{2,10},{3,11},{4,12},{5,13},{6,14},{7,15},{8,0},{9,1},... | collective-permute-start | bytes 1376264 | tf_op jit(solution)/shard_map/ppermute | solution.py:248
  96.6 4.0 %convolution_convert_fusion.2.refs_3_ = bf16[128,448]{1,0:T(8,128)(2,1)} fusion(bf16[128,4096]{1,0:T(8,128)(2,1)S(1)} %broadcast_select_fusion, bf16[448,4096]{1,0:T(8,128)(2,1)} %collective-permute-done.1), kind=kOutput, calls=%fused_computation.8 | convolution fusion | flops 469819392 | bytes 4833280 | tf_op jit(solution)/shard_map/dot_general | solution.py:305
  100.6 1.9 %convolution_convert_fusion.3.refs_1_ = bf16[128,448]{1,0:T(8,128)(2,1)} fusion(bf16[128,4096]{1,0:T(8,128)(2,1)S(1)} %broadcast_select_fusion, bf16[448,4096]{1,0:T(8,128)(2,1)S(1)} %copy-done.1), kind=kOutput, calls=%fused_computation.9 | convolution fusion | flops 469819392 | bytes 4833280 | tf_op jit(solution)/shard_map/dot_general | solution.py:305
  102.5 5.5 %convolution_convert_fusion.1.refs_4_ = bf16[512,448]{1,0:T(8,128)(2,1)} fusion(bf16[448,4096]{1,0:T(8,128)(2,1)} %collective-permute-done.6, bf16[128,4096]{1,0:T(8,128)(2,1)S(1)} %broadcast_select_fusion, bf16[128,4096]{1,0:T(8,128)(2,1)S(1)} %broadcast_select_fusion.1, bf16[128,4096]{1,0:T(8,128)(2,1)} %collective-permute-done, ...), kind=kOutput, calls=%fused_computation.3 | convolution fusion | flops 1896054784 | bytes 8323072 | tf_op jit(solution)/shard_map/dot_general | solution.py:305
  108.0 4.4 %convolution_convert_fusion.refs_5_ = bf16[512,448]{1,0:T(8,128)(2,1)} fusion(bf16[448,4096]{1,0:T(8,128)(2,1)S(1)} %collective-permute-done.10, bf16[128,4096]{1,0:T(8,128)(2,1)S(1)} %broadcast_select_fusion, bf16[128,4096]{1,0:T(8,128)(2,1)S(1)} %broadcast_select_fusion.1, bf16[128,4096]{1,0:T(8,128)(2,1)} %collective-permute-done, ...), kind=kOutput, calls=%fused_computation.2 | convolution fusion | flops 1896054784 | bytes 8323072 | tf_op jit(solution)/shard_map/dot_general | solution.py:305
  112.4 3.9 %shard_map.83.refs_11_ = bf16[4,1,32,128]{3,2,1,0:T(8,128)(2,1)} custom-call(bf16[384,448]{1,0:T(8,128)(2,1)} %fusion.2.refs_0_, bf16[128,448]{1,0:T(8,128)(2,1)} %convolution_convert_fusion.3.refs_1_, bf16[384,448]{1,0:T(8,128)(2,1)} %fusion.3.refs_2_, bf16[128,448]{1,0:T(8,128)(2,1)} %convolution_convert_fusion.2.refs_3_, ...), custom_call_target="tpu_custom_call" | custom-call | flops 1000 | bytes 1000 | tf_op jit(solution)/shard_map/pallas_call | solution.py:166
  116.3 1.4 collective-permute-done.12.refs_7_
  118.5 3.8 %shard_map.84.own = bf16[4,1,32,128]{3,2,1,0:T(8,128)(2,1)} custom-call(bf16[384,448]{1,0:T(8,128)(2,1)} %fusion.2.refs_0_, bf16[128,448]{1,0:T(8,128)(2,1)} %convolution_convert_fusion.3.refs_1_, bf16[384,448]{1,0:T(8,128)(2,1)} %fusion.3.refs_2_, bf16[128,448]{1,0:T(8,128)(2,1)} %convolution_convert_fusion.2.refs_3_, ...), custom_call_target="tpu_custom_call" | custom-call | flops 1000 | bytes 1000 | tf_op jit(solution)/shard_map/pallas_call | solution.py:166
  122.3 2.1 %collective-permute-start.15 = (bf16[4,1,32,128]{3,2,1,0:T(8,128)(2,1)}, bf16[4,1,32,128]{3,2,1,0:T(8,128)(2,1)S(1)}, u32[]{:S(2)}, u32[]{:S(2)}) collective-permute-start(bf16[4,1,32,128]{3,2,1,0:T(8,128)(2,1)} %shard_map.84.own), channel_id=1, source_target_pairs={{0,12},{1,13},{2,14},{3,15},{4,8},{5,9},{6,10},{7,11},{8,4},{9,5},... | collective-permute-start | bytes 98312 | tf_op jit(solution)/shard_map/ppermute | solution.py:248
  124.4 2.3 %collective-permute-start.13 = (bf16[4,1,32,128]{3,2,1,0:T(8,128)(2,1)}, bf16[4,1,32,128]{3,2,1,0:T(8,128)(2,1)S(1)}, u32[]{:S(2)}, u32[]{:S(2)}) collective-permute-start(bf16[4,1,32,128]{3,2,1,0:T(8,128)(2,1)} %shard_map.84.own), channel_id=1, source_target_pairs={{0,4},{1,5},{2,6},{3,7},{4,0},{5,1},{6,2},{7,3},{8,12},{9,13},{10,... | collective-permute-start | bytes 98312 | tf_op jit(solution)/shard_map/ppermute | solution.py:248
  126.7 1.6 %collective-permute-done.15.refs_2_ = bf16[4,1,32,128]{3,2,1,0:T(8,128)(2,1)S(1)} collective-permute-done((bf16[4,1,32,128]{3,2,1,0:T(8,128)(2,1)}, bf16[4,1,32,128]{3,2,1,0:T(8,128)(2,1)S(1)}, u32[]{:S(2)}, u32[]{:S(2)}) %collective-permute-start.15) | collective-permute-done | bytes 32800 | tf_op jit(solution)/shard_map/ppermute | solution.py:248
  128.3 1.2 collective-permute-done.14.refs_1_
  130.7 1.5 %shard_map.85.q0 = bf16[4,1,32,128]{3,2,1,0:T(8,128)(2,1)} custom-call(bf16[4,1,32,128]{3,2,1,0:T(8,128)(2,1)} %shard_map.84.own, bf16[4,1,32,128]{3,2,1,0:T(8,128)(2,1)} %copy-done.12, bf16[4,1,32,128]{3,2,1,0:T(8,128)(2,1)} %copy-done.11, bf16[4,1,32,128]{3,2,1,0:T(8,128)(2,1)} %copy-done.10), custom_call_target="tpu_custom_call" | custom-call | flops 1000 | bytes 1000 | tf_op jit(solution)/shard_map/pallas_call | solution.py:187
  132.2 1.5 %collective-permute-start.17 = (bf16[4,1,32,128]{3,2,1,0:T(8,128)(2,1)}, bf16[4,1,32,128]{3,2,1,0:T(8,128)(2,1)S(1)}, u32[]{:S(2)}, u32[]{:S(2)}) collective-permute-start(bf16[4,1,32,128]{3,2,1,0:T(8,128)(2,1)} %shard_map.85.q0), channel_id=1, source_target_pairs={{0,2},{1,3},{2,0},{3,1},{4,6},{5,7},{6,4},{7,5},{8,10},{9,11},{10,... | collective-permute-start | bytes 98312 | tf_op jit(solution)/shard_map/ppermute | solution.py:248
  134.7 1.3 collective-permute-done.18.q3
  137.1 5.3 %shard_map.86 = f32[16,768]{1,0:T(8,128)} custom-call(s32[1]{0:T(128)} %bitcast.where_ref, bf16[4,1,32,128]{3,2,1,0:T(8,128)(2,1)} %shard_map.85.q0, bf16[4,1,32,128]{3,2,1,0:T(8,128)(2,1)} %copy-done.9, bf16[4,1,32,128]{3,2,1,0:T(8,128)(2,1)} %copy-done.8, bf16[4,1,32,128]{3,2,1,0:T(8,128)(2,1)} %copy-done.7, s32[16,1]{1,0:T(8,128)} %copy.30.visible_ref, ...), custom_call_target="tpu_custom_call" | custom-call | flops 1000 | bytes 1000 | tf_op jit(solution)/shard_map/pallas_call | solution.py:225
  (60 shorter events, 8.4 us)
Async XLA Ops:
  0.0 7.1 %copy-start = (bf16[128,4096]{1,0:T(8,128)(2,1)S(1)}, bf16[128,4096]{1,0:T(8,128)(2,1)}, u32[]{:S(2)}) copy-start(bf16[128,4096]{1,0:T(8,128)(2,1)} %param.8) | copy-start | bytes 3145732
  0.0 27.2 %collective-permute-start.1 = (bf16[448,4096]{1,0:T(8,128)(2,1)}, bf16[448,4096]{1,0:T(8,128)(2,1)}, u32[]{:S(2)}, u32[]{:S(2)}) collective-permute-start(bf16[448,4096]{1,0:T(8,128)(2,1)} %param.11), channel_id=1, source_target_pairs={{0,1},{1,0},{2,3},{3,2},{4,5},{5,4},{6,7},{7,6},{8,9},{9,8},{10,11... | collective-permute-start | bytes 11010056 | tf_op jit(solution)/shard_map/ppermute | solution.py:248
  0.5 26.7 %collective-permute-start = (bf16[128,4096]{1,0:T(8,128)(2,1)}, bf16[128,4096]{1,0:T(8,128)(2,1)}, u32[]{:S(2)}, u32[]{:S(2)}) collective-permute-start(bf16[128,4096]{1,0:T(8,128)(2,1)} %param.10), channel_id=1, source_target_pairs={{0,4},{1,5},{2,6},{3,7},{4,0},{5,1},{6,2},{7,3},{8,12},{9,13},{10,... | collective-permute-start | bytes 3145736 | tf_op jit(solution)/shard_map/ppermute | solution.py:248
  3.1 25.8 %collective-permute-start.7 = (bf16[128,4096]{1,0:T(8,128)(2,1)}, bf16[128,4096]{1,0:T(8,128)(2,1)S(1)}, u32[]{:S(2)}, u32[]{:S(2)}) collective-permute-start(bf16[128,4096]{1,0:T(8,128)(2,1)} %param.10), channel_id=1, source_target_pairs={{4,8},{5,9},{6,10},{7,11},{8,4},{9,5},{10,6},{11,7},{20,24},{21,25... | collective-permute-start | bytes 3145736 | tf_op jit(solution)/shard_map/ppermute | solution.py:248
  3.8 81.8 %collective-permute-start.6 = (bf16[448,4096]{1,0:T(8,128)(2,1)}, bf16[448,4096]{1,0:T(8,128)(2,1)}, u32[]{:S(2)}, u32[]{:S(2)}) collective-permute-start(bf16[448,4096]{1,0:T(8,128)(2,1)} %param.11), channel_id=1, source_target_pairs={{0,2},{1,3},{2,0},{3,1},{4,6},{5,7},{6,4},{7,5},{8,10},{9,11},{10,... | collective-permute-start | bytes 11010056 | tf_op jit(solution)/shard_map/ppermute | solution.py:248
  7.1 53.5 %copy-start.14 = (bf16[128,4096]{1,0:T(8,128)(2,1)S(1)}, bf16[128,4096]{1,0:T(8,128)(2,1)}, u32[]{:S(2)}) copy-start(bf16[128,4096]{1,0:T(8,128)(2,1)} %param.10) | copy-start | bytes 3145732
  7.6 58.0 %copy-start.5 = (bf16[64,128]{1,0:T(8,128)(2,1)}, bf16[64,128]{1,0:T(8,128)(2,1)S(1)}, u32[]{:S(2)}) copy-start(bf16[64,128]{1,0:T(8,128)(2,1)S(1)} %convolution_convert_fusion.4.refs_8_) | copy-start | bytes 49156
  27.2 29.6 %collective-permute-start.2 = (bf16[128,4096]{1,0:T(8,128)(2,1)}, bf16[128,4096]{1,0:T(8,128)(2,1)}, u32[]{:S(2)}, u32[]{:S(2)}) collective-permute-start(bf16[128,4096]{1,0:T(8,128)(2,1)} %collective-permute-done), channel_id=1, source_target_pairs={{4,8},{5,9},{6,10},{7,11},{8,4},{9,5},{10,6},{11,7},{20,24},{21,25... | collective-permute-start | bytes 3145736 | tf_op jit(solution)/shard_map/ppermute | solution.py:248
  28.9 30.3 %collective-permute-start.8 = (bf16[128,4096]{1,0:T(8,128)(2,1)S(1)}, bf16[128,4096]{1,0:T(8,128)(2,1)}, u32[]{:S(2)}, u32[]{:S(2)}) collective-permute-start(bf16[128,4096]{1,0:T(8,128)(2,1)S(1)} %collective-permute-done.7), channel_id=1, source_target_pairs={{4,0},{5,1},{6,2},{7,3},{8,12},{9,13},{10,14},{11,15},{20,16},{21,... | collective-permute-start | bytes 3145736 | tf_op jit(solution)/shard_map/ppermute | solution.py:248
  30.1 26.6 %collective-permute-start.3 = (bf16[64,128]{1,0:T(8,128)(2,1)S(1)}, bf16[64,128]{1,0:T(8,128)(2,1)S(1)}, u32[]{:S(2)}, u32[]{:S(2)}) collective-permute-start(bf16[64,128]{1,0:T(8,128)(2,1)S(1)} %convolution_convert_fusion.4.refs_8_), channel_id=1, source_target_pairs={{0,4},{1,5},{2,6},{3,7},{4,0},{5,1},{6,2},{7,3},{8,12},{9,13},{10,... | collective-permute-start | bytes 49160 | tf_op jit(solution)/shard_map/ppermute | solution.py:248
  56.7 8.9 %copy-start.6 = (bf16[64,128]{1,0:T(8,128)(2,1)}, bf16[64,128]{1,0:T(8,128)(2,1)S(1)}, u32[]{:S(2)}) copy-start(bf16[64,128]{1,0:T(8,128)(2,1)S(1)} %collective-permute-done.3.refs_8_) | copy-start | bytes 49156
  56.7 15.8 %collective-permute-start.9 = (bf16[2,64,128]{2,1,0:T(8,128)(2,1)S(1)}, bf16[2,64,128]{2,1,0:T(8,128)(2,1)S(1)}, u32[]{:S(2)}, u32[]{:S(2)}) collective-permute-start(bf16[2,64,128]{2,1,0:T(8,128)(2,1)S(1)} %pad_maximum_fusion.10), channel_id=1, source_target_pairs={{0,8},{1,9},{2,10},{3,11},{4,12},{5,13},{6,14},{7,15},{8,0},{9,1},... | collective-permute-start | bytes 98312 | tf_op jit(solution)/shard_map/ppermute | solution.py:248
  57.7 36.0 %collective-permute-start.4 = (bf16[128,4096]{1,0:T(8,128)(2,1)}, bf16[128,4096]{1,0:T(8,128)(2,1)S(1)}, u32[]{:S(2)}, u32[]{:S(2)}) collective-permute-start(bf16[128,4096]{1,0:T(8,128)(2,1)} %collective-permute-done.2), channel_id=1, source_target_pairs={{4,0},{5,1},{6,2},{7,3},{8,12},{9,13},{10,14},{11,15},{20,16},{21,... | collective-permute-start | bytes 3145736 | tf_op jit(solution)/shard_map/ppermute | solution.py:248
  60.6 5.0 %copy-start.16 = (bf16[128,1792]{1,0:T(8,128)(2,1)S(1)}, bf16[128,1792]{1,0:T(8,128)(2,1)}, u32[]{:S(2)}) copy-start(bf16[128,1792]{1,0:T(8,128)(2,1)} %get-tuple-element.49) | copy-start | bytes 1376260
  65.6 20.0 %collective-permute-start.5 = (bf16[128,1792]{1,0:T(8,128)(2,1)S(1)}, bf16[128,1792]{1,0:T(8,128)(2,1)S(1)}, u32[]{:S(2)}, u32[]{:S(2)}) collective-permute-start(bf16[128,1792]{1,0:T(8,128)(2,1)S(1)} %copy-done.16), channel_id=1, source_target_pairs={{0,12},{1,13},{2,14},{3,15},{4,8},{5,9},{6,10},{7,11},{8,4},{9,5},... | collective-permute-start | bytes 1376264 | tf_op jit(solution)/shard_map/ppermute | solution.py:248
  72.6 28.0 %copy-start.1 = (bf16[448,4096]{1,0:T(8,128)(2,1)S(1)}, bf16[448,4096]{1,0:T(8,128)(2,1)}, u32[]{:S(2)}) copy-start(bf16[448,4096]{1,0:T(8,128)(2,1)} %param.11) | copy-start | bytes 11010052
  85.6 16.9 %copy-start.2 = (bf16[128,1792]{1,0:T(8,128)(2,1)}, bf16[128,1792]{1,0:T(8,128)(2,1)S(1)}, u32[]{:S(2)}) copy-start(bf16[128,1792]{1,0:T(8,128)(2,1)S(1)} %collective-permute-done.5.refs_7_) | copy-start | bytes 1376260
  93.8 14.3 %collective-permute-start.10 = (bf16[448,4096]{1,0:T(8,128)(2,1)}, bf16[448,4096]{1,0:T(8,128)(2,1)S(1)}, u32[]{:S(2)}, u32[]{:S(2)}) collective-permute-start(bf16[448,4096]{1,0:T(8,128)(2,1)} %collective-permute-done.6), channel_id=1, source_target_pairs={{0,1},{1,0},{2,3},{3,2},{4,5},{5,4},{6,7},{7,6},{8,9},{9,8},{10,11... | collective-permute-start | bytes 11010056 | tf_op jit(solution)/shard_map/ppermute | solution.py:248
  93.8 22.5 %collective-permute-start.11 = (bf16[128,1792]{1,0:T(8,128)(2,1)}, bf16[128,1792]{1,0:T(8,128)(2,1)S(1)}, u32[]{:S(2)}, u32[]{:S(2)}) collective-permute-start(bf16[128,1792]{1,0:T(8,128)(2,1)} %get-tuple-element.59), channel_id=1, source_target_pairs={{0,4},{1,5},{2,6},{3,7},{4,0},{5,1},{6,2},{7,3},{8,12},{9,13},{10,... | collective-permute-start | bytes 1376264 | tf_op jit(solution)/shard_map/ppermute | solution.py:248
  93.8 23.9 %collective-permute-start.12 = (bf16[128,1792]{1,0:T(8,128)(2,1)}, bf16[128,1792]{1,0:T(8,128)(2,1)S(1)}, u32[]{:S(2)}, u32[]{:S(2)}) collective-permute-start(bf16[128,1792]{1,0:T(8,128)(2,1)} %get-tuple-element.60), channel_id=1, source_target_pairs={{0,8},{1,9},{2,10},{3,11},{4,12},{5,13},{6,14},{7,15},{8,0},{9,1},... | collective-permute-start | bytes 1376264 | tf_op jit(solution)/shard_map/ppermute | solution.py:248
  96.6 5.9 %copy-start.15 = (bf16[128,4096]{1,0:T(8,128)(2,1)S(1)}, bf16[128,4096]{1,0:T(8,128)(2,1)}, u32[]{:S(2)}) copy-start(bf16[128,4096]{1,0:T(8,128)(2,1)} %param.10) | copy-start | bytes 3145732
  112.4 21.6 %copy-start.13 = (s32[16]{0:T(128)S(1)}, s32[16]{0:T(128)}, u32[]{:S(2)}) copy-start(s32[16]{0:T(128)} %param.15) | copy-start | bytes 196
  116.3 1.4 copy-start.3
  117.7 0.8 copy-start.4
  122.3 6.0 %collective-permute-start.15 = (bf16[4,1,32,128]{3,2,1,0:T(8,128)(2,1)}, bf16[4,1,32,128]{3,2,1,0:T(8,128)(2,1)S(1)}, u32[]{:S(2)}, u32[]{:S(2)}) collective-permute-start(bf16[4,1,32,128]{3,2,1,0:T(8,128)(2,1)} %shard_map.84.own), channel_id=1, source_target_pairs={{0,12},{1,13},{2,14},{3,15},{4,8},{5,9},{6,10},{7,11},{8,4},{9,5},... | collective-permute-start | bytes 98312 | tf_op jit(solution)/shard_map/ppermute | solution.py:248
  124.4 5.0 %collective-permute-start.14 = (bf16[4,1,32,128]{3,2,1,0:T(8,128)(2,1)}, bf16[4,1,32,128]{3,2,1,0:T(8,128)(2,1)S(1)}, u32[]{:S(2)}, u32[]{:S(2)}) collective-permute-start(bf16[4,1,32,128]{3,2,1,0:T(8,128)(2,1)} %shard_map.84.own), channel_id=1, source_target_pairs={{0,8},{1,9},{2,10},{3,11},{4,12},{5,13},{6,14},{7,15},{8,0},{9,1},... | collective-permute-start | bytes 98312 | tf_op jit(solution)/shard_map/ppermute | solution.py:248
  124.4 5.0 %collective-permute-start.13 = (bf16[4,1,32,128]{3,2,1,0:T(8,128)(2,1)}, bf16[4,1,32,128]{3,2,1,0:T(8,128)(2,1)S(1)}, u32[]{:S(2)}, u32[]{:S(2)}) collective-permute-start(bf16[4,1,32,128]{3,2,1,0:T(8,128)(2,1)} %shard_map.84.own), channel_id=1, source_target_pairs={{0,4},{1,5},{2,6},{3,7},{4,0},{5,1},{6,2},{7,3},{8,12},{9,13},{10,... | collective-permute-start | bytes 98312 | tf_op jit(solution)/shard_map/ppermute | solution.py:248
  128.3 1.2 copy-start.10
  130.1 0.6 copy-start.12
  132.2 3.9 %collective-permute-start.18 = (bf16[4,1,32,128]{3,2,1,0:T(8,128)(2,1)}, bf16[4,1,32,128]{3,2,1,0:T(8,128)(2,1)S(1)}, u32[]{:S(2)}, u32[]{:S(2)}) collective-permute-start(bf16[4,1,32,128]{3,2,1,0:T(8,128)(2,1)} %shard_map.85.q0), channel_id=1, source_target_pairs={{0,3},{1,2},{2,1},{3,0},{4,7},{5,6},{6,5},{7,4},{8,11},{9,10},{10,... | collective-permute-start | bytes 98312 | tf_op jit(solution)/shard_map/ppermute | solution.py:248
  132.2 4.2 %collective-permute-start.17 = (bf16[4,1,32,128]{3,2,1,0:T(8,128)(2,1)}, bf16[4,1,32,128]{3,2,1,0:T(8,128)(2,1)S(1)}, u32[]{:S(2)}, u32[]{:S(2)}) collective-permute-start(bf16[4,1,32,128]{3,2,1,0:T(8,128)(2,1)} %shard_map.85.q0), channel_id=1, source_target_pairs={{0,2},{1,3},{2,0},{3,1},{4,6},{5,7},{6,4},{7,5},{8,10},{9,11},{10,... | collective-permute-start | bytes 98312 | tf_op jit(solution)/shard_map/ppermute | solution.py:248
  133.7 2.7 %collective-permute-start.16 = (bf16[4,1,32,128]{3,2,1,0:T(8,128)(2,1)}, bf16[4,1,32,128]{3,2,1,0:T(8,128)(2,1)S(1)}, u32[]{:S(2)}, u32[]{:S(2)}) collective-permute-start(bf16[4,1,32,128]{3,2,1,0:T(8,128)(2,1)} %shard_map.85.q0), channel_id=1, source_target_pairs={{0,1},{1,0},{2,3},{3,2},{4,5},{5,4},{6,7},{7,6},{8,9},{9,8},{10,11... | collective-permute-start | bytes 98312 | tf_op jit(solution)/shard_map/ppermute | solution.py:248
  (4 other events, 2.4 us)

commit v3 on v2

v3 whole, which is shorter than its diff:
```python
import functools

import jax
import jax.numpy as jnp
from jax import lax
from jax.experimental import pallas as pl
from jax.experimental.pallas import tpu as pltpu
from jax.sharding import PartitionSpec as P

SEQ_LEN = 128
LANE_SHIFT = 2
LANES = 4
QUADS = 1 << LANE_SHIFT
BF16, F32 = jnp.bfloat16, jnp.float32
LINK = jnp.bfloat16


EXTRA = 16


def arrange_kernel(piece, where_ref, gate_ref, rows_ref, in_ref, n0, n1, n2, f0, f1, f2, b3, r0, r1, r2):
    lane, side, core = where_ref[0], where_ref[1], where_ref[2]
    wide = 2 * piece
    tokens = gate_ref.shape[0]

    def put(source, target, column, block, first):
        start = pl.multiple_of(block * wide, 128)
        both = source[:, pl.ds(start, wide)]
        if first == 1:
            both = jnp.concatenate([both[:, piece:], both[:, :piece]], axis=1)
        target[: both.shape[0], column : column + wide] = both

    for target in (f1, f2, b3):
        target[tokens:, :] = jnp.zeros((EXTRA, target.shape[1]), target.dtype)
        target[tokens:, : in_ref.shape[1]] = in_ref[...]
    for first in range(2):

        @pl.when(core == first)
        def _():
            for k in range(LANES):
                for far in range(2):
                    block = (lane ^ k) * 2 + (side ^ far)
                    if k == 3:
                        put(gate_ref, b3, far * wide, block, first)
                    else:
                        put(gate_ref, ((n0, n1, n2), (f0, f1, f2))[far][k], 0, block, first)
                    if k == 0:
                        put(rows_ref, r0, far * wide, block, first)
                    elif k < 3 and not far:
                        put(rows_ref, (r1, r2)[k - 1], 0, block, first)


def arrange(gate, rows, in_block, position, piece):
    lane = position >> LANE_SHIFT & LANES - 1
    quad = position & QUADS - 1
    total = gate.shape[1]
    outer = total // (piece * QUADS * LANES)
    mine = total // LANES
    tokens, rank = gate.shape[0], rows.shape[0]
    if outer == 1 and 2 * piece % 128 == 0:
        where = jnp.stack([lane, quad >> 1, quad & 1]).astype(jnp.int32)
        vmem = pl.BlockSpec(memory_space=pltpu.VMEM)
        near, far = (tokens, mine // 2), (tokens + EXTRA, mine // 2)
        shapes = [near] * 4 + [far] * 2 + [(tokens + EXTRA, mine)]
        shapes += [(rank, mine), (rank, mine // 2), (rank, mine // 2)]
        parts = pl.pallas_call(
            functools.partial(arrange_kernel, piece),
            out_shape=[jax.ShapeDtypeStruct(shape, gate.dtype) for shape in shapes],
            in_specs=[pl.BlockSpec(memory_space=pltpu.SMEM), vmem, vmem, vmem],
            out_specs=[vmem] * len(shapes),
            cost_estimate=pl.CostEstimate(
                flops=0, bytes_accessed=4 * gate.size + 4 * rows.size, transcendentals=0
            ),
            compiler_params=pltpu.CompilerParams(vmem_limit_bytes=16 << 20),
        )(where, gate, rows, in_block)
        return parts[:3], parts[3:6], parts[6], parts[7:]

    def block(value, k):
        whole = []
        for w in range(QUADS):
            index = (lane ^ k) * QUADS + (quad ^ w)
            for o in range(outer):
                start = (o * QUADS * LANES + index) * piece
                whole.append(lax.dynamic_slice_in_dim(value, start, piece, axis=1))
        whole = jnp.concatenate(whole, axis=1)
        return whole[:, : mine // 2], whole[:, mine // 2 :], whole

    def extend(value):
        extra = jnp.pad(in_block, ((0, 0), (0, value.shape[1] - in_block.shape[1])))
        return jnp.concatenate([value, extra], axis=0)

    near, far, whole = zip(*[block(gate, k) for k in range(LANES)])
    sides = [block(rows, 0)[2], block(rows, 1)[0], block(rows, 2)[0]]
    return list(near[:3]), [far[0], extend(far[1]), extend(far[2])], extend(whole[3]), sides


def after(value, *others):
    return lax.optimization_barrier((value,) + others)[0]


def call(body, out_shape, in_specs, out_specs, **kwargs):
    return pl.pallas_call(
        body,
        out_shape=out_shape,
        in_specs=in_specs,
        out_specs=out_specs,
        cost_estimate=pl.CostEstimate(flops=1000, bytes_accessed=1000, transcendentals=0),
        **kwargs,
    )


def silu(gate):
    return 0.5 * gate * (1.0 + jnp.tanh(0.5 * gate))


def in_value(refs, k, tokens):
    if k == 0:
        return refs["in"][...]
    source = refs["block"] if k == 3 else refs["far", k]
    width = refs["in"].shape[0] // EXTRA * tokens
    return source[tokens:, :width]


def feature_kernel(slots, blocks, gates, extras, names, *refs):
    out_ref, ups = refs[-2:]
    refs = dict(zip(names, refs))
    tokens = SEQ_LEN * out_ref.shape[1]
    rank = refs["rows"].shape[0]
    for k in range(LANES):
        if "before" in refs and k not in slots:
            out_ref[k] = refs["before"][k]
    for i, k in enumerate(slots):
        start = 0
        for b, width, tops in blocks:
            part, top = tops[k]
            edge = gates[k][0][1].stop - gates[k][0][1].start
            name, cut = gates[k][start >= edge]
            gate = refs[name]
            base = cut.start + start - edge * (start >= edge)
            value = refs[b, part][top : top + tokens, :].astype(F32)
            ups[i * tokens : (i + 1) * tokens, start : start + width] = (
                value * silu(gate[:tokens, base : base + width].astype(F32))
            ).astype(BF16)
            start += width
    total = lax.dot_general(
        refs["rows"][...], ups[...], (((1,), (1,)), ((), ())), preferred_element_type=F32
    )
    totals = [total[:, i * tokens : (i + 1) * tokens] for i in range(len(slots))]
    for j in range(extras):
        side = refs["side", j][...].astype(F32)
        up_grad = refs["back", j][:, side.shape[1] :].astype(F32) * silu(side)
        totals[0] += lax.dot_general(
            refs["beside", j][...],
            up_grad.astype(BF16),
            (((1,), (1,)), ((), ())),
            preferred_element_type=F32,
        )
    for i, k in enumerate(slots):
        for e in range(out_ref.shape[1]):
            cut = slice(e * SEQ_LEN, (e + 1) * SEQ_LEN)
            value = totals[i][:, cut]
            high = value.astype(BF16)
            low = (value - high.astype(F32)).astype(BF16)
            left = in_value(refs, k, tokens)
            if left.shape[0] == EXTRA:
                left = jnp.concatenate(
                    [left[:, j * tokens : (j + 1) * tokens] for j in range(rank // EXTRA)], axis=0
                )
            left = left[:, cut]
            feature = lax.dot_general(
                jnp.concatenate([left, left], axis=1),
                jnp.concatenate([high, low], axis=1),
                (((1,), (1,)), ((), ())),
                preferred_element_type=F32,
            )
            out_ref[k, e] = jnp.concatenate(
                [feature[: rank // 2], feature[rank // 2 :]], axis=1
            ).astype(out_ref.dtype)


def features(slots, blocks, sources, gates, rows, extras=(), before=None):
    names, operands, specs, layout = [], [], [], []
    rank, mine = rows.shape
    tokens = blocks[0][0].shape[0]
    vmem = pl.BlockSpec(memory_space=pltpu.VMEM)

    def add(name, value):
        names.append(name)
        operands.append(value)

    for b, parts in enumerate(blocks):
        tops, first = {}, 0
        for i, part in enumerate(parts):
            add((b, i), part)
            for k in range(LANES):
                if first <= k * tokens < first + part.shape[0]:
                    tops[k] = (i, k * tokens - first)
            first += part.shape[0]
        layout.append((b, parts[0].shape[1], tops))
    for name, value in sources.items():
        add(name, value)
    add("rows", rows)
    for j, (back, side, beside) in enumerate(extras):
        add(("back", j), back)
        add(("side", j), side)
        add(("beside", j), beside)
    if before is not None:
        add("before", before)
    return call(
        functools.partial(feature_kernel, slots, layout, gates, len(extras), names),
        jax.ShapeDtypeStruct((LANES, tokens // SEQ_LEN, rank // 2, 2 * rank), LINK),
        [vmem] * len(operands),
        vmem,
        scratch_shapes=[pltpu.VMEM((len(slots) * tokens, mine), BF16)],
        compiler_params=pltpu.CompilerParams(vmem_limit_bytes=16 << 20),
    )(*operands)


def scale_kernel(own, *refs):
    others, out_ref = refs[:-1], refs[-1]
    width = own.shape[2] * own.shape[3]
    for j in range(LANES):
        total = own[j].astype(F32)
        for k in range(1, LANES):
            total += others[k - 1][j ^ k].astype(F32)
        square = jnp.sum(jnp.sum(total * total, axis=2, keepdims=True), axis=1, keepdims=True)
        out_ref[j] = (total * lax.rsqrt(square / width + 1e-06)).astype(BF16)


def scaled(own, others):
    vmem = pl.BlockSpec(memory_space=pltpu.VMEM)
    return call(
        scale_kernel,
        jax.ShapeDtypeStruct(own.shape, BF16),
        [vmem] * LANES,
        vmem,
        compiler_params=pltpu.CompilerParams(vmem_limit_bytes=4 << 20),
    )(own, *others)


def score_kernel(where_ref, q0, q1, q2, q3, visible_ref, stored_ref, out_ref, rows):
    position = where_ref[0]
    for w, source in enumerate((q0, q1, q2, q3)):
        for k in range(LANES):
            row = k * QUADS + w
            value = source[k, 0].astype(F32)
            for j in range(value.shape[0]):
                rows[row : row + 1, j * 128 : (j + 1) * 128] = value[j : j + 1, :]
    products = lax.dot_general(
        rows[...].astype(BF16),
        stored_ref[...],
        (((1,), (1,)), ((), ())),
        preferred_element_type=F32,
    )
    count = out_ref.shape[1]
    index = lax.broadcasted_iota(jnp.int32, products.shape, 0)
    for bit in (1, 2, 4, 8):
        swapped = jnp.where(
            index & bit != 0,
            pltpu.roll(products, bit, 0),
            pltpu.roll(products, products.shape[0] - bit, 0),
        )
        products = jnp.where(jnp.full(products.shape, position) & bit != 0, swapped, products)
    column = position * count + lax.broadcasted_iota(jnp.int32, products.shape, 1)
    out_ref[...] = jnp.where(column < visible_ref[...], products, 0.0)


def scores(where, queries, visible, stored):
    vmem = pl.BlockSpec(memory_space=pltpu.VMEM)
    examples = LANES * QUADS
    return call(
        score_kernel,
        jax.ShapeDtypeStruct((examples, stored.shape[0]), F32),
        [pl.BlockSpec(memory_space=pltpu.SMEM)] + [vmem] * 6,
        vmem,
        scratch_shapes=[pltpu.VMEM((examples, stored.shape[1]), F32)],
        compiler_params=pltpu.CompilerParams(vmem_limit_bytes=8 << 20),
    )(where, *queries, visible[:, None], stored)


def shards(activations, gate_pre, out_grad, down_weight, proj_in, proj_out, stored, visible):
    devices = lax.axis_size("row")
    position = lax.axis_index("row")
    total_bits = devices.bit_length() - 1
    lane = position >> LANE_SHIFT & LANES - 1
    tokens = out_grad.shape[0]
    rank = proj_in.shape[1]

    def send(value, move):
        pairs = []
        for i in range(devices):
            target = move(i)
            if target is not None:
                pairs.append((i, target))
        return lax.ppermute(value, "row", pairs)

    def flip(bits):
        return lambda i: i ^ bits

    def lane_move(table):
        def move(i):
            to = table.get(i >> LANE_SHIFT & LANES - 1)
            return None if to is None else i & ~((LANES - 1) << LANE_SHIFT) | to << LANE_SHIFT

        return move

    def join(value, other, bit, axis):
        return jnp.where(
            position >> bit & 1 == 1,
            jnp.concatenate([other, value], axis=axis),
            jnp.concatenate([value, other], axis=axis),
        )

    def gather_high(value, axis):
        for bit in range(LANE_SHIFT + 2, total_bits):
            value = join(value, send(value, flip(1 << bit)), bit, axis)
        return value

    middle_swap = lane_move({1: 2, 2: 1})
    to_ends = lane_move({1: 0, 2: 3})
    at_end = (lane == 0) | (lane == LANES - 1)

    own_w = gather_high(down_weight, 0)
    rows = own_w.shape[0]

    tie = lax.optimization_barrier
    grad_a = send(out_grad, flip(1 << LANE_SHIFT))
    grad_b = send(out_grad, middle_swap)
    far_w = send(own_w, flip(2))
    core_w = send(own_w, flip(1))

    width = proj_in.shape[0]
    paired = proj_in.T.reshape(rank // 2, 2, width).transpose(1, 0, 2).reshape(rank, width)
    in_proj = lax.dot_general(
        paired, activations, (((1,), (1,)), ((), ())), preferred_element_type=F32
    ).astype(BF16)
    in_block = in_proj.reshape(rank // EXTRA, EXTRA, tokens).transpose(1, 0, 2)
    in_block = in_block.reshape(EXTRA, rank // EXTRA * tokens)
    near, far, block_3, sides = arrange(
        gate_pre, proj_out.T, in_block, position, down_weight.shape[0]
    )
    grad_a, core_w, near, far, block_3, sides = tie(
        (grad_a, core_w, near, far, block_3, sides)
    )

    def hidden(grads, weight):
        return lax.dot_general(
            grads, weight, (((1,), (1,)), ((), ())), preferred_element_type=F32
        ).astype(BF16)

    def near_hidden(grads):
        return [hidden(grads, w) for w in (own_w, core_w)]

    half = 2 * rows
    grad_c = send(grad_a, middle_swap)
    grad_d = send(grad_b, to_ends)
    slot_1 = near_hidden(grad_a)
    back_1 = send(jnp.concatenate([near[1], *slot_1], axis=1), lane_move({0: 1, 3: 2}))
    grad_c, near, far, block_3 = tie((grad_c, near, far, block_3))

    grad_e = send(grad_c, to_ends)
    block_3 = send(after(block_3, grad_d), flip(3 << LANE_SHIFT))
    slot_0 = near_hidden(after(out_grad, block_3, far_w))
    grad_2 = jnp.where(at_end, grad_d, grad_c)
    slot_2 = near_hidden(grad_2)
    back_2 = send(jnp.concatenate([near[2], *slot_2], axis=1), lane_move({0: 2, 3: 1}))
    grad_e, back_2, slot_0 = tie((grad_e, back_2, slot_0))
    grad_3 = jnp.where(at_end, grad_e, grad_b)
    slot_3 = near_hidden(grad_3)
    grads = jnp.concatenate([out_grad, grad_a, grad_2, grad_3], axis=0)
    block_3, back_1, back_2, far_w, near, far, grad_3 = tie(
        (block_3, back_1, back_2, far_w, near, far, grad_3)
    )

    cross_w = send(far_w, flip(1))
    far_2 = send(far[2], flip(2 << LANE_SHIFT))
    far_1 = send(far[1], flip(1 << LANE_SHIFT))
    blocks = list(zip(slot_0, slot_1, slot_2, slot_3))
    blocks += [(hidden(grads, w),) for w in (far_w, cross_w)]
    low, high = slice(0, half), slice(half, 2 * half)
    extras = [(back, near[j], sides[j]) for j, back in ((1, back_1), (2, back_2))]
    part = features(
        (0, 3),
        blocks,
        {"near": near[0], "far": far[0], "block": block_3, "in": in_proj},
        {0: (("near", low), ("far", low)), 3: (("block", low), ("block", high))},
        sides[0],
        extras,
    )
    far_1, far_2, part = tie((far_1, far_2, part))
    own = features(
        (1, 2),
        blocks,
        {("far", 1): far_1, ("far", 2): far_2, "back1": back_1, "back2": back_2, "in": in_proj},
        {
            1: (("back1", low), (("far", 1), low)),
            2: (("back2", low), (("far", 2), low)),
        },
        sides[0],
        before=part,
    )
    queries = scaled(own, [send(own, flip(k << LANE_SHIFT)) for k in range(1, LANES)])
    quad = position & QUADS - 1
    everyone = [queries] + [send(queries, flip(q)) for q in range(1, QUADS)]
    if devices == LANES * QUADS and tokens == SEQ_LEN:
        where = position.astype(jnp.int32).reshape(1)
        held = pltpu.with_memory_space_constraint(stored, pltpu.VMEM)
        return scores(where, everyone, visible, held)

    examples_dev = tokens // SEQ_LEN
    everyone = jnp.stack(everyone, axis=1).reshape(LANES * QUADS, examples_dev, rank * rank)
    order = jnp.arange(LANES * QUADS)
    order = (order >> LANE_SHIFT ^ lane) * QUADS + (order & QUADS - 1 ^ quad)
    pick = (order[:, None] == jnp.arange(LANES * QUADS)[None, :]).astype(BF16)
    everyone = jnp.einsum("ij,jef->ief", pick, everyone, preferred_element_type=F32).astype(BF16)
    queries = gather_high(everyone, 0).reshape(devices * examples_dev, rank * rank)
    stored_rows = stored.shape[0]
    column = position * stored_rows + jnp.arange(stored_rows, dtype=jnp.int32)
    products = lax.dot_general(
        queries, stored, (((1,), (1,)), ((), ())), preferred_element_type=F32
    )
    return jnp.where(column[None, :] < visible[:, None], products, F32(0.0))


def solution(mesh):
    return jax.shard_map(
        shards,
        mesh=mesh,
        in_specs=(
            P(("ckpt", "row"), None),
            P(("ckpt", "row"), None),
            P(("ckpt", "row"), None),
            P(("ckpt", "row"), None),
            P(),
            P(),
            P(("ckpt", "row"), None),
            P(),
        ),
        out_specs=P("ckpt", "row"),
        check_vma=False,
    )
```

time: 143 us -> 136 us (0.951)
  waiting for transfers between devices: 64.2 us -> 44.4 us
  Pallas kernels: 17.8 us -> 6.67 us
  starting transfers between devices: 26.3 us -> 34.9 us
  matrix products: 26.3 us -> 34.4 us
  local copies, waits for them, and re-layouts: 5.6 us -> 11.8 us
    ppermute x19, waiting for transfers between devices: 64.2 us -> 44.4 us  [send(): return lax.ppermute(value, 'row', pairs)]
    ppermute x19, starting transfers between devices: 26.3 us -> 34.9 us  [send(): return lax.ppermute(value, 'row', pairs)]
    dot_general x6 -> x10, matrix products: 25.8 us -> 33.9 us  [hidden(): lax.dot_general(grads, weight, (((1,), (1,)), ((), ())), preferred_elemen...]
    unnamed x34 -> x42, local copies, waits for them, and re-layouts: 2.65 us -> 8.2 us
    pallas_call x2, Pallas kernels: 7.7 us -> 2.61 us  [features(): call(functools.partial(feature_kernel, slots, layout, gates, len(extras),...]
    pallas_call x1, Pallas kernels: 5.29 us -> 2.41 us  [scores(): call(score_kernel, jax.ShapeDtypeStruct((examples, stored.shape[0]), F32)...]
    concatenate x0 -> x2, local copies, waits for them, and re-layouts: none -> 1.8 us  [the longest x1 0.91 us: shards(): jnp.concatenate([near[2], *slot_2], axis=1)]
    pallas_call x1, Pallas kernels: 3.24 us -> 1.54 us  [arrange(): pl.pallas_call(functools.partial(arrange_kernel, piece), out_shape=[jax.S...]
  transfers between devices with their start and end apart: 19 -> 19, of which waited for: 9 -> 7; matrix products, arithmetic and copies ran while one was open for 22% -> 30% of each run, Pallas kernels for 5% -> 2%
where the time goes in v3:
time: 136 us; the launch traced here: 135 us
  waiting for transfers between devices  44.4 us (33%)
  starting transfers between devices  34.9 us (26%)
  matrix products  34.4 us (25%)
  local copies, waits for them, and re-layouts  11.8 us (9%)
  Pallas kernels  6.67 us (5%)
  other arithmetic  2.76 us (2%)
    ppermute x19, waiting for transfers between devices, send(): return lax.ppermute(value, 'row', pairs)  44.4 us
    ppermute x19, starting transfers between devices, send(): return lax.ppermute(value, 'row', pairs)  34.9 us
    dot_general x10, matrix products, hidden(): lax.dot_general(grads, weight, (((1,), (1,)), ((), ())), preferred_elemen...  33.9 us
    unnamed x42, local copies, waits for them, and re-layouts  8.2 us
  transfers between devices with their start and end apart: 19, of which 7 were waited for; matrix products, arithmetic and copies ran while one was open for 30% of the time, Pallas kernels for 2%

profile of v3, /device:TPU:0, one launch (start us, length us, event | category | flops | bytes accessed | tf_op | source)
XLA Modules:
  0.0 135.4 jit_solution(9903067358409628918)
XLA Ops:
  0.5 2.6 %collective-permute-start = (bf16[128,4096]{1,0:T(8,128)(2,1)}, bf16[128,4096]{1,0:T(8,128)(2,1)}, u32[]{:S(2)}, u32[]{:S(2)}) collective-permute-start(bf16[128,4096]{1,0:T(8,128)(2,1)} %param.10), channel_id=1, source_target_pairs={{0,4},{1,5},{2,6},{3,7},{4,0},{5,1},{6,2},{7,3},{8,12},{9,13},{10,... | collective-permute-start | bytes 3145736 | tf_op jit(solution)/shard_map/ppermute | solution.py:295
  3.1 1.6 %collective-permute-start.4 = (bf16[128,4096]{1,0:T(8,128)(2,1)}, bf16[128,4096]{1,0:T(8,128)(2,1)}, u32[]{:S(2)}, u32[]{:S(2)}) collective-permute-start(bf16[128,4096]{1,0:T(8,128)(2,1)} %param.10), channel_id=1, source_target_pairs={{4,8},{5,9},{6,10},{7,11},{8,4},{9,5},{10,6},{11,7},{20,24},{21,25... | collective-permute-start | bytes 3145736 | tf_op jit(solution)/shard_map/ppermute | solution.py:295
  4.8 1.5 %collective-permute-start.8 = (bf16[448,4096]{1,0:T(8,128)(2,1)}, bf16[448,4096]{1,0:T(8,128)(2,1)}, u32[]{:S(2)}, u32[]{:S(2)}) collective-permute-start(bf16[448,4096]{1,0:T(8,128)(2,1)} %param.11), channel_id=1, source_target_pairs={{0,2},{1,3},{2,0},{3,1},{4,6},{5,7},{6,4},{7,5},{8,10},{9,11},{10,... | collective-permute-start | bytes 11010056 | tf_op jit(solution)/shard_map/ppermute | solution.py:295
  6.2 1.4 %reshape.16 = bf16[32,2,4096]{2,1,0:T(2,128)(2,1)S(1)} reshape(bf16[64,4096]{1,0:T(8,128)(2,1)} %bitcast.41) | data formatting | bytes 1048576 | tf_op jit(solution)/shard_map/reshape | solution.py:333
  9.7 1.5 %shard_map.82 = (bf16[128,896]{1,0:T(8,128)(2,1)S(1)}, bf16[128,896]{1,0:T(8,128)(2,1)S(1)}, bf16[128,896]{1,0:T(8,128)(2,1)S(1)}, bf16[128,896]{1,0:T(8,128)(2,...) custom-call(s32[3]{0:T(128)S(1)} %pad_add_fusion.where_ref, ...), custom_call_target="tpu_custom_call" | custom-call | bytes 5505024 | tf_op jit(solution)/shard_map/pallas_call | solution.py:66
  15.4 11.8 %collective-permute-done = bf16[128,4096]{1,0:T(8,128)(2,1)} collective-permute-done((bf16[128,4096]{1,0:T(8,128)(2,1)}, bf16[128,4096]{1,0:T(8,128)(2,1)}, u32[]{:S(2)}, u32[]{:S(2)}) %collective-permute-start) | collective-permute-done | bytes 1048608 | tf_op jit(solution)/shard_map/ppermute | solution.py:295
  27.2 1.6 %collective-permute-start.2 = (bf16[128,4096]{1,0:T(8,128)(2,1)}, bf16[128,4096]{1,0:T(8,128)(2,1)}, u32[]{:S(2)}, u32[]{:S(2)}) collective-permute-start(bf16[128,4096]{1,0:T(8,128)(2,1)} %collective-permute-done), channel_id=1, source_target_pairs={{4,8},{5,9},{6,10},{7,11},{8,4},{9,5},{10,6},{11,7},{20,24},{21,25... | collective-permute-start | bytes 3145736 | tf_op jit(solution)/shard_map/ppermute | solution.py:295
  30.1 3.6 %convolution_convert_fusion.5.refs_1_ = bf16[128,448]{1,0:T(8,128)(2,1)S(1)} fusion(bf16[128,4096]{1,0:T(8,128)(2,1)} %collective-permute-done, bf16[448,4096]{1,0:T(8,128)(2,1)} %param.11), kind=kOutput, calls=%fused_computation.6 | convolution fusion | flops 469819392 | bytes 4833280 | tf_op jit(solution)/shard_map/dot_general | solution.py:347
  33.7 3.6 %convolution_convert_fusion.3.refs_5_ = bf16[128,448]{1,0:T(8,128)(2,1)S(1)} fusion(bf16[128,4096]{1,0:T(8,128)(2,1)} %collective-permute-done, bf16[448,4096]{1,0:T(8,128)(2,1)} %collective-permute-done.1), kind=kOutput, calls=%fused_computation.4 | convolution fusion | flops 469819392 | bytes 4833280 | tf_op jit(solution)/shard_map/dot_general | solution.py:347
  38.2 6.5 %collective-permute-start.9 = (bf16[128,1792]{1,0:T(8,128)(2,1)}, bf16[128,1792]{1,0:T(8,128)(2,1)S(1)}, u32[]{:S(2)}, u32[]{:S(2)}) collective-permute-start(bf16[128,1792]{1,0:T(8,128)(2,1)} %concatenate.11), channel_id=1, source_target_pairs={{0,4},{1,5},{2,6},{3,7},{12,8},{13,9},{14,10},{15,11},{16,20},{17,... | collective-permute-start | bytes 1376264 | tf_op jit(solution)/shard_map/ppermute | solution.py:295
  46.0 10.7 %collective-permute-done.5 = bf16[128,4096]{1,0:T(8,128)(2,1)} collective-permute-done((bf16[128,4096]{1,0:T(8,128)(2,1)}, bf16[128,4096]{1,0:T(8,128)(2,1)}, u32[]{:S(2)}, u32[]{:S(2)}) %collective-permute-start.5) | collective-permute-done | bytes 1048608 | tf_op jit(solution)/shard_map/ppermute | solution.py:295
  56.7 2.8 %collective-permute-start.7 = (bf16[144,1792]{1,0:T(8,128)(2,1)}, bf16[144,1792]{1,0:T(8,128)(2,1)S(1)}, u32[]{:S(2)}, u32[]{:S(2)}) collective-permute-start(bf16[144,1792]{1,0:T(8,128)(2,1)} %get-tuple-element.76), channel_id=1, source_target_pairs={{0,12},{1,13},{2,14},{3,15},{4,8},{5,9},{6,10},{7,11},{8,4},{9,5},... | collective-permute-start | bytes 1548296 | tf_op jit(solution)/shard_map/ppermute | solution.py:295
  59.5 1.3 broadcast_select_fusion.1
  60.9 3.7 %convolution_convert_fusion.9.refs_2_ = bf16[128,448]{1,0:T(8,128)(2,1)S(1)} fusion(bf16[128,4096]{1,0:T(8,128)(2,1)S(1)} %broadcast_select_fusion.1, bf16[448,4096]{1,0:T(8,128)(2,1)} %param.11), kind=kOutput, calls=%fused_computation.10 | convolution fusion | flops 469819392 | bytes 4833280 | tf_op jit(solution)/shard_map/dot_general | solution.py:347
  64.6 3.3 %convolution_convert_fusion.8.refs_6_ = bf16[128,448]{1,0:T(8,128)(2,1)S(1)} fusion(bf16[128,4096]{1,0:T(8,128)(2,1)S(1)} %broadcast_select_fusion.1, bf16[448,4096]{1,0:T(8,128)(2,1)} %collective-permute-done.1), kind=kOutput, calls=%fused_computation.9 | convolution fusion | flops 469819392 | bytes 4833280 | tf_op jit(solution)/shard_map/dot_general | solution.py:347
  68.7 2.3 %collective-permute-start.6 = (bf16[128,1792]{1,0:T(8,128)(2,1)}, bf16[128,1792]{1,0:T(8,128)(2,1)S(1)}, u32[]{:S(2)}, u32[]{:S(2)}) collective-permute-start(bf16[128,1792]{1,0:T(8,128)(2,1)} %concatenate.9), channel_id=1, source_target_pairs={{0,8},{1,9},{2,10},{3,11},{12,4},{13,5},{14,6},{15,7},{16,24},{17,... | collective-permute-start | bytes 1376264 | tf_op jit(solution)/shard_map/ppermute | solution.py:295
  71.1 15.4 %collective-permute-done.8 = bf16[448,4096]{1,0:T(8,128)(2,1)} collective-permute-done((bf16[448,4096]{1,0:T(8,128)(2,1)}, bf16[448,4096]{1,0:T(8,128)(2,1)}, u32[]{:S(2)}, u32[]{:S(2)}) %collective-permute-start.8) | collective-permute-done | bytes 3670048 | tf_op jit(solution)/shard_map/ppermute | solution.py:295
  86.5 3.6 %convolution_convert_fusion.7.refs_0_ = bf16[128,448]{1,0:T(8,128)(2,1)S(1)} fusion(bf16[128,4096]{1,0:T(8,128)(2,1)} %param.10, bf16[448,4096]{1,0:T(8,128)(2,1)} %param.11), kind=kOutput, calls=%fused_computation.8 | convolution fusion | flops 469819392 | bytes 4833280 | tf_op jit(solution)/shard_map/dot_general | solution.py:347
  90.1 3.4 %convolution_convert_fusion.6.refs_4_ = bf16[128,448]{1,0:T(8,128)(2,1)S(1)} fusion(bf16[128,4096]{1,0:T(8,128)(2,1)S(1)} %copy-done.19, bf16[448,4096]{1,0:T(8,128)(2,1)} %collective-permute-done.1), kind=kOutput, calls=%fused_computation.7 | convolution fusion | flops 469819392 | bytes 4833280 | tf_op jit(solution)/shard_map/dot_general | solution.py:347
  93.6 1.3 broadcast_select_fusion
  95.0 5.3 %collective-permute-start.11 = (bf16[144,896]{1,0:T(8,128)(2,1)S(1)}, bf16[144,896]{1,0:T(8,128)(2,1)S(1)}, u32[]{:S(2)}, u32[]{:S(2)}) collective-permute-start(bf16[144,896]{1,0:T(8,128)(2,1)S(1)} %copy-done.15), channel_id=1, source_target_pairs={{0,4},{1,5},{2,6},{3,7},{4,0},{5,1},{6,2},{7,3},{8,12},{9,13},{10,... | collective-permute-start | bytes 774152 | tf_op jit(solution)/shard_map/ppermute | solution.py:295
  102.6 3.3 %convolution_convert_fusion.2.refs_7_ = bf16[128,448]{1,0:T(8,128)(2,1)S(1)} fusion(bf16[128,4096]{1,0:T(8,128)(2,1)S(1)} %broadcast_select_fusion, bf16[448,4096]{1,0:T(8,128)(2,1)} %collective-permute-done.1), kind=kOutput, calls=%fused_computation.3 | convolution fusion | flops 469819392 | bytes 4833280 | tf_op jit(solution)/shard_map/dot_general | solution.py:347
  105.9 4.7 %convolution_convert_fusion.1.refs_8_ = bf16[512,448]{1,0:T(8,128)(2,1)S(1)} fusion(bf16[448,4096]{1,0:T(8,128)(2,1)} %collective-permute-done.8, bf16[128,4096]{1,0:T(8,128)(2,1)S(1)} %broadcast_select_fusion, bf16[128,4096]{1,0:T(8,128)(2,1)S(1)} %copy-done.18, bf16[128,4096]{1,0:T(8,128)(2,1)} %collective-permute-done, bf16[128,4096]{1,0:T(8,128)(2,1)S(1)} %copy-done.19), kind=kOutput, calls=%fused_computation.2 | convolution fusion | flops 1896054784 | bytes 8323072 | tf_op jit(solution)/shard_map/dot_general | solution.py:347
  110.7 3.6 %convolution_convert_fusion.refs_9_ = bf16[512,448]{1,0:T(8,128)(2,1)S(1)} fusion(bf16[448,4096]{1,0:T(8,128)(2,1)S(1)} %collective-permute-done.10, bf16[128,4096]{1,0:T(8,128)(2,1)S(1)} %broadcast_select_fusion, bf16[128,4096]{1,0:T(8,128)(2,1)S(1)} %copy-done.18, bf16[128,4096]{1,0:T(8,128)(2,1)} %collective-permute-done, bf16[128,4096]{1,0:T(8,128)(2,1)S(1)} %copy-done.19), kind=kOutput, calls=%fused_computation.1 | convolution fusion | flops 1896054784 | bytes 8323072 | tf_op jit(solution)/shard_map/dot_general | solution.py:347
  114.4 1.4 %shard_map.83.refs_16_ = bf16[4,1,32,128]{3,2,1,0:T(8,128)(2,1)S(1)} custom-call(bf16[128,448]{1,0:T(8,128)(2,1)S(1)} %convolution_convert_fusion.7.refs_0_, bf16[128,448]{1,0:T(8,128)(2,1)S(1)} %convolution_convert_fusion.5.refs_1_, bf16[128,448]{1,0:T(8,128)(2,1)S(1)} %convolution_convert_fusion.9.refs_2_, ...), custom_call_target="tpu_custom_call" | custom-call | flops 1000 | bytes 1000 | tf_op jit(solution)/shard_map/pallas_call | solution.py:209
  117.1 2.0 %collective-permute-start.13 = (bf16[4,1,32,128]{3,2,1,0:T(8,128)(2,1)S(1)}, bf16[4,1,32,128]{3,2,1,0:T(8,128)(2,1)S(1)}, u32[]{:S(2)}, u32[]{:S(2)}) collective-permute-start(bf16[4,1,32,128]{3,2,1,0:T(8,128)(2,1)S(1)} %shard_map.84.own), channel_id=1, source_target_pairs={{0,4},{1,5},{2,6},{3,7},{4,0},{5,1},{6,2},{7,3},{8,12},{9,13},{10,... | collective-permute-start | bytes 98312 | tf_op jit(solution)/shard_map/ppermute | solution.py:295
  119.4 2.1 %collective-permute-start.15 = (bf16[4,1,32,128]{3,2,1,0:T(8,128)(2,1)S(1)}, bf16[4,1,32,128]{3,2,1,0:T(8,128)(2,1)S(1)}, u32[]{:S(2)}, u32[]{:S(2)}) collective-permute-start(bf16[4,1,32,128]{3,2,1,0:T(8,128)(2,1)S(1)} %shard_map.84.own), channel_id=1, source_target_pairs={{0,12},{1,13},{2,14},{3,15},{4,8},{5,9},{6,10},{7,11},{8,4},{9,5},... | collective-permute-start | bytes 98312 | tf_op jit(solution)/shard_map/ppermute | solution.py:295
  121.5 2.6 %collective-permute-done.14.refs_1_ = bf16[4,1,32,128]{3,2,1,0:T(8,128)(2,1)S(1)} collective-permute-done((bf16[4,1,32,128]{3,2,1,0:T(8,128)(2,1)S(1)}, bf16[4,1,32,128]{3,2,1,0:T(8,128)(2,1)S(1)}, u32[]{:S(2)}, u32[]{:S(2)}) %collective-permute-start.14) | collective-permute-done | bytes 32800 | tf_op jit(solution)/shard_map/ppermute | solution.py:295
  125.3 1.6 %collective-permute-start.17 = (bf16[4,1,32,128]{3,2,1,0:T(8,128)(2,1)S(1)}, bf16[4,1,32,128]{3,2,1,0:T(8,128)(2,1)S(1)}, u32[]{:S(2)}, u32[]{:S(2)}) collective-permute-start(bf16[4,1,32,128]{3,2,1,0:T(8,128)(2,1)S(1)} %shard_map.85.q0), channel_id=1, source_target_pairs={{0,2},{1,3},{2,0},{3,1},{4,6},{5,7},{6,4},{7,5},{8,10},{9,11},{10,... | collective-permute-start | bytes 98312 | tf_op jit(solution)/shard_map/ppermute | solution.py:295
  127.2 2.0 %collective-permute-done.17.q2 = bf16[4,1,32,128]{3,2,1,0:T(8,128)(2,1)S(1)} collective-permute-done((bf16[4,1,32,128]{3,2,1,0:T(8,128)(2,1)S(1)}, bf16[4,1,32,128]{3,2,1,0:T(8,128)(2,1)S(1)}, u32[]{:S(2)}, u32[]{:S(2)}) %collective-permute-start.17) | collective-permute-done | bytes 32800 | tf_op jit(solution)/shard_map/ppermute | solution.py:295
  130.2 2.8 %copy-done.1 = bf16[768,4096]{1,0:T(8,128)(2,1)S(1)} copy-done((bf16[768,4096]{1,0:T(8,128)(2,1)S(1)}, bf16[768,4096]{1,0:T(8,128)(2,1)}, u32[]{:S(2)}) %copy-start.1) | copy-done | bytes 6291480
  133.0 2.4 %shard_map.86 = f32[16,768]{1,0:T(8,128)} custom-call(s32[1]{0:T(128)} %bitcast.where_ref, bf16[4,1,32,128]{3,2,1,0:T(8,128)(2,1)S(1)} %shard_map.85.q0, bf16[4,1,32,128]{3,2,1,0:T(8,128)(2,1)S(1)} %collective-permute-done.16.q1, bf16[4,1,32,128]{3,2,1,0:T(8,128)(2,1)S(1)} %collective-permute-done.17.q2, ...), custom_call_target="tpu_custom_call" | custom-call | flops 1000 | bytes 1000 | tf_op jit(solution)/shard_map/pallas_call | solution.py:271
  (73 shorter events, 17.5 us)
Async XLA Ops:
  0.0 7.9 %copy-start = (bf16[128,4096]{1,0:T(8,128)(2,1)S(1)}, bf16[128,4096]{1,0:T(8,128)(2,1)}, u32[]{:S(2)}) copy-start(bf16[128,4096]{1,0:T(8,128)(2,1)} %param.8) | copy-start | bytes 3145732
  0.0 8.5 %copy-start.2 = (bf16[128,7168]{1,0:T(8,128)(2,1)S(1)}, bf16[128,7168]{1,0:T(8,128)(2,1)}, u32[]{:S(2)}) copy-start(bf16[128,7168]{1,0:T(8,128)(2,1)} %gate_ref.1) | copy-start | bytes 5505028
  0.0 27.2 %collective-permute-start.1 = (bf16[448,4096]{1,0:T(8,128)(2,1)}, bf16[448,4096]{1,0:T(8,128)(2,1)}, u32[]{:S(2)}, u32[]{:S(2)}) collective-permute-start(bf16[448,4096]{1,0:T(8,128)(2,1)} %param.11), channel_id=1, source_target_pairs={{0,1},{1,0},{2,3},{3,2},{4,5},{5,4},{6,7},{7,6},{8,9},{9,8},{10,11... | collective-permute-start | bytes 11010056 | tf_op jit(solution)/shard_map/ppermute | solution.py:295
  0.5 26.7 %collective-permute-start = (bf16[128,4096]{1,0:T(8,128)(2,1)}, bf16[128,4096]{1,0:T(8,128)(2,1)}, u32[]{:S(2)}, u32[]{:S(2)}) collective-permute-start(bf16[128,4096]{1,0:T(8,128)(2,1)} %param.10), channel_id=1, source_target_pairs={{0,4},{1,5},{2,6},{3,7},{4,0},{5,1},{6,2},{7,3},{8,12},{9,13},{10,... | collective-permute-start | bytes 3145736 | tf_op jit(solution)/shard_map/ppermute | solution.py:295
  3.1 25.7 %collective-permute-start.4 = (bf16[128,4096]{1,0:T(8,128)(2,1)}, bf16[128,4096]{1,0:T(8,128)(2,1)}, u32[]{:S(2)}, u32[]{:S(2)}) collective-permute-start(bf16[128,4096]{1,0:T(8,128)(2,1)} %param.10), channel_id=1, source_target_pairs={{4,8},{5,9},{6,10},{7,11},{8,4},{9,5},{10,6},{11,7},{20,24},{21,25... | collective-permute-start | bytes 3145736 | tf_op jit(solution)/shard_map/ppermute | solution.py:295
  4.8 81.7 %collective-permute-start.8 = (bf16[448,4096]{1,0:T(8,128)(2,1)}, bf16[448,4096]{1,0:T(8,128)(2,1)}, u32[]{:S(2)}, u32[]{:S(2)}) collective-permute-start(bf16[448,4096]{1,0:T(8,128)(2,1)} %param.11), channel_id=1, source_target_pairs={{0,2},{1,3},{2,0},{3,1},{4,6},{5,7},{6,4},{7,5},{8,10},{9,11},{10,... | collective-permute-start | bytes 11010056 | tf_op jit(solution)/shard_map/ppermute | solution.py:295
  27.2 17.5 %collective-permute-start.2 = (bf16[128,4096]{1,0:T(8,128)(2,1)}, bf16[128,4096]{1,0:T(8,128)(2,1)}, u32[]{:S(2)}, u32[]{:S(2)}) collective-permute-start(bf16[128,4096]{1,0:T(8,128)(2,1)} %collective-permute-done), channel_id=1, source_target_pairs={{4,8},{5,9},{6,10},{7,11},{8,4},{9,5},{10,6},{11,7},{20,24},{21,25... | collective-permute-start | bytes 3145736 | tf_op jit(solution)/shard_map/ppermute | solution.py:295
  28.8 27.9 %collective-permute-start.5 = (bf16[128,4096]{1,0:T(8,128)(2,1)}, bf16[128,4096]{1,0:T(8,128)(2,1)}, u32[]{:S(2)}, u32[]{:S(2)}) collective-permute-start(bf16[128,4096]{1,0:T(8,128)(2,1)} %collective-permute-done.4), channel_id=1, source_target_pairs={{4,0},{5,1},{6,2},{7,3},{8,12},{9,13},{10,14},{11,15},{20,16},{21,... | collective-permute-start | bytes 3145736 | tf_op jit(solution)/shard_map/ppermute | solution.py:295
  38.2 56.8 %collective-permute-start.9 = (bf16[128,1792]{1,0:T(8,128)(2,1)}, bf16[128,1792]{1,0:T(8,128)(2,1)S(1)}, u32[]{:S(2)}, u32[]{:S(2)}) collective-permute-start(bf16[128,1792]{1,0:T(8,128)(2,1)} %concatenate.11), channel_id=1, source_target_pairs={{0,4},{1,5},{2,6},{3,7},{12,8},{13,9},{14,10},{15,11},{16,20},{17,... | collective-permute-start | bytes 1376264 | tf_op jit(solution)/shard_map/ppermute | solution.py:295
  44.7 48.8 %collective-permute-start.3 = (bf16[128,4096]{1,0:T(8,128)(2,1)}, bf16[128,4096]{1,0:T(8,128)(2,1)}, u32[]{:S(2)}, u32[]{:S(2)}) collective-permute-start(bf16[128,4096]{1,0:T(8,128)(2,1)} %collective-permute-done.2), channel_id=1, source_target_pairs={{4,0},{5,1},{6,2},{7,3},{8,12},{9,13},{10,14},{11,15},{20,16},{21,... | collective-permute-start | bytes 3145736 | tf_op jit(solution)/shard_map/ppermute | solution.py:295
  56.7 29.8 %collective-permute-start.7 = (bf16[144,1792]{1,0:T(8,128)(2,1)}, bf16[144,1792]{1,0:T(8,128)(2,1)S(1)}, u32[]{:S(2)}, u32[]{:S(2)}) collective-permute-start(bf16[144,1792]{1,0:T(8,128)(2,1)} %get-tuple-element.76), channel_id=1, source_target_pairs={{0,12},{1,13},{2,14},{3,15},{4,8},{5,9},{6,10},{7,11},{8,4},{9,5},... | collective-permute-start | bytes 1548296 | tf_op jit(solution)/shard_map/ppermute | solution.py:295
  60.9 3.7 %copy-start.17 = (bf16[128,4096]{1,0:T(8,128)(2,1)}, bf16[128,4096]{1,0:T(8,128)(2,1)S(1)}, u32[]{:S(2)}) copy-start(bf16[128,4096]{1,0:T(8,128)(2,1)S(1)} %broadcast_select_fusion.1) | copy-start | bytes 3145732
  68.7 21.3 %copy-start.19 = (bf16[128,4096]{1,0:T(8,128)(2,1)S(1)}, bf16[128,4096]{1,0:T(8,128)(2,1)}, u32[]{:S(2)}) copy-start(bf16[128,4096]{1,0:T(8,128)(2,1)} %param.10) | copy-start | bytes 3145732
  68.7 24.8 %collective-permute-start.6 = (bf16[128,1792]{1,0:T(8,128)(2,1)}, bf16[128,1792]{1,0:T(8,128)(2,1)S(1)}, u32[]{:S(2)}, u32[]{:S(2)}) collective-permute-start(bf16[128,1792]{1,0:T(8,128)(2,1)} %concatenate.9), channel_id=1, source_target_pairs={{0,8},{1,9},{2,10},{3,11},{12,4},{13,5},{14,6},{15,7},{16,24},{17,... | collective-permute-start | bytes 1376264 | tf_op jit(solution)/shard_map/ppermute | solution.py:295
  90.1 4.9 %copy-start.15 = (bf16[144,896]{1,0:T(8,128)(2,1)S(1)}, bf16[144,896]{1,0:T(8,128)(2,1)}, u32[]{:S(2)}) copy-start(bf16[144,896]{1,0:T(8,128)(2,1)} %copy-done.14) | copy-start | bytes 774148
  90.1 10.2 %copy-start.13 = (bf16[144,896]{1,0:T(8,128)(2,1)S(1)}, bf16[144,896]{1,0:T(8,128)(2,1)}, u32[]{:S(2)}) copy-start(bf16[144,896]{1,0:T(8,128)(2,1)} %copy-done.12) | copy-start | bytes 774148
  90.1 11.3 %copy-start.16 = (bf16[448,4096]{1,0:T(8,128)(2,1)S(1)}, bf16[448,4096]{1,0:T(8,128)(2,1)}, u32[]{:S(2)}) copy-start(bf16[448,4096]{1,0:T(8,128)(2,1)} %param.11) | copy-start | bytes 11010052
  94.9 11.0 %copy-start.18 = (bf16[128,4096]{1,0:T(8,128)(2,1)S(1)}, bf16[128,4096]{1,0:T(8,128)(2,1)}, u32[]{:S(2)}) copy-start(bf16[128,4096]{1,0:T(8,128)(2,1)} %copy-done.17) | copy-start | bytes 3145732
  94.9 15.8 %collective-permute-start.10 = (bf16[448,4096]{1,0:T(8,128)(2,1)}, bf16[448,4096]{1,0:T(8,128)(2,1)S(1)}, u32[]{:S(2)}, u32[]{:S(2)}) collective-permute-start(bf16[448,4096]{1,0:T(8,128)(2,1)} %collective-permute-done.8), channel_id=1, source_target_pairs={{0,1},{1,0},{2,3},{3,2},{4,5},{5,4},{6,7},{7,6},{8,9},{9,8},{10,11... | collective-permute-start | bytes 11010056 | tf_op jit(solution)/shard_map/ppermute | solution.py:295
  95.0 20.8 %collective-permute-start.11 = (bf16[144,896]{1,0:T(8,128)(2,1)S(1)}, bf16[144,896]{1,0:T(8,128)(2,1)S(1)}, u32[]{:S(2)}, u32[]{:S(2)}) collective-permute-start(bf16[144,896]{1,0:T(8,128)(2,1)S(1)} %copy-done.15), channel_id=1, source_target_pairs={{0,4},{1,5},{2,6},{3,7},{4,0},{5,1},{6,2},{7,3},{8,12},{9,13},{10,... | collective-permute-start | bytes 774152 | tf_op jit(solution)/shard_map/ppermute | solution.py:295
  100.3 15.5 %collective-permute-start.12 = (bf16[144,896]{1,0:T(8,128)(2,1)S(1)}, bf16[144,896]{1,0:T(8,128)(2,1)S(1)}, u32[]{:S(2)}, u32[]{:S(2)}) collective-permute-start(bf16[144,896]{1,0:T(8,128)(2,1)S(1)} %copy-done.13), channel_id=1, source_target_pairs={{0,8},{1,9},{2,10},{3,11},{4,12},{5,13},{6,14},{7,15},{8,0},{9,1},... | collective-permute-start | bytes 774152 | tf_op jit(solution)/shard_map/ppermute | solution.py:295
  110.7 3.7 %copy-start.5 = (bf16[64,1792]{1,0:T(8,128)(2,1)S(1)}, bf16[64,1792]{1,0:T(8,128)(2,1)}, u32[]{:S(2)}) copy-start(bf16[64,1792]{1,0:T(8,128)(2,1)} %copy-done.4) | copy-start | bytes 688132
  110.7 3.7 %copy-start.7 = (bf16[128,896]{1,0:T(8,128)(2,1)S(1)}, bf16[128,896]{1,0:T(8,128)(2,1)}, u32[]{:S(2)}) copy-start(bf16[128,896]{1,0:T(8,128)(2,1)} %copy-done.6) | copy-start | bytes 688132
  110.7 3.7 %copy-start.9 = (bf16[128,896]{1,0:T(8,128)(2,1)S(1)}, bf16[128,896]{1,0:T(8,128)(2,1)}, u32[]{:S(2)}) copy-start(bf16[128,896]{1,0:T(8,128)(2,1)} %copy-done.8) | copy-start | bytes 688132
  110.7 3.7 %copy-start.11 = (bf16[64,896]{1,0:T(8,128)(2,1)S(1)}, bf16[64,896]{1,0:T(8,128)(2,1)}, u32[]{:S(2)}) copy-start(bf16[64,896]{1,0:T(8,128)(2,1)} %copy-done.10) | copy-start | bytes 344068
  114.4 12.7 %copy-start.20 = (s32[16]{0:T(128)S(1)}, s32[16]{0:T(128)}, u32[]{:S(2)}) copy-start(s32[16]{0:T(128)} %param.15) | copy-start | bytes 196
  117.1 4.5 %collective-permute-start.13 = (bf16[4,1,32,128]{3,2,1,0:T(8,128)(2,1)S(1)}, bf16[4,1,32,128]{3,2,1,0:T(8,128)(2,1)S(1)}, u32[]{:S(2)}, u32[]{:S(2)}) collective-permute-start(bf16[4,1,32,128]{3,2,1,0:T(8,128)(2,1)S(1)} %shard_map.84.own), channel_id=1, source_target_pairs={{0,4},{1,5},{2,6},{3,7},{4,0},{5,1},{6,2},{7,3},{8,12},{9,13},{10,... | collective-permute-start | bytes 98312 | tf_op jit(solution)/shard_map/ppermute | solution.py:295
  119.1 5.1 %collective-permute-start.14 = (bf16[4,1,32,128]{3,2,1,0:T(8,128)(2,1)S(1)}, bf16[4,1,32,128]{3,2,1,0:T(8,128)(2,1)S(1)}, u32[]{:S(2)}, u32[]{:S(2)}) collective-permute-start(bf16[4,1,32,128]{3,2,1,0:T(8,128)(2,1)S(1)} %shard_map.84.own), channel_id=1, source_target_pairs={{0,8},{1,9},{2,10},{3,11},{4,12},{5,13},{6,14},{7,15},{8,0},{9,1},... | collective-permute-start | bytes 98312 | tf_op jit(solution)/shard_map/ppermute | solution.py:295
  119.4 5.7 %collective-permute-start.15 = (bf16[4,1,32,128]{3,2,1,0:T(8,128)(2,1)S(1)}, bf16[4,1,32,128]{3,2,1,0:T(8,128)(2,1)S(1)}, u32[]{:S(2)}, u32[]{:S(2)}) collective-permute-start(bf16[4,1,32,128]{3,2,1,0:T(8,128)(2,1)S(1)} %shard_map.84.own), channel_id=1, source_target_pairs={{0,12},{1,13},{2,14},{3,15},{4,8},{5,9},{6,10},{7,11},{8,4},{9,5},... | collective-permute-start | bytes 98312 | tf_op jit(solution)/shard_map/ppermute | solution.py:295
  125.2 2.0 %collective-permute-start.16 = (bf16[4,1,32,128]{3,2,1,0:T(8,128)(2,1)S(1)}, bf16[4,1,32,128]{3,2,1,0:T(8,128)(2,1)S(1)}, u32[]{:S(2)}, u32[]{:S(2)}) collective-permute-start(bf16[4,1,32,128]{3,2,1,0:T(8,128)(2,1)S(1)} %shard_map.85.q0), channel_id=1, source_target_pairs={{0,1},{1,0},{2,3},{3,2},{4,5},{5,4},{6,7},{7,6},{8,9},{9,8},{10,11... | collective-permute-start | bytes 98312 | tf_op jit(solution)/shard_map/ppermute | solution.py:295
  125.3 4.0 %collective-permute-start.17 = (bf16[4,1,32,128]{3,2,1,0:T(8,128)(2,1)S(1)}, bf16[4,1,32,128]{3,2,1,0:T(8,128)(2,1)S(1)}, u32[]{:S(2)}, u32[]{:S(2)}) collective-permute-start(bf16[4,1,32,128]{3,2,1,0:T(8,128)(2,1)S(1)} %shard_map.85.q0), channel_id=1, source_target_pairs={{0,2},{1,3},{2,0},{3,1},{4,6},{5,7},{6,4},{7,5},{8,10},{9,11},{10,... | collective-permute-start | bytes 98312 | tf_op jit(solution)/shard_map/ppermute | solution.py:295
  126.8 3.3 %collective-permute-start.18 = (bf16[4,1,32,128]{3,2,1,0:T(8,128)(2,1)S(1)}, bf16[4,1,32,128]{3,2,1,0:T(8,128)(2,1)S(1)}, u32[]{:S(2)}, u32[]{:S(2)}) collective-permute-start(bf16[4,1,32,128]{3,2,1,0:T(8,128)(2,1)S(1)} %shard_map.85.q0), channel_id=1, source_target_pairs={{0,3},{1,2},{2,1},{3,0},{4,7},{5,6},{6,5},{7,4},{8,11},{9,10},{10,... | collective-permute-start | bytes 98312 | tf_op jit(solution)/shard_map/ppermute | solution.py:295
  (8 other events, 8.1 us)

commit v4 on v3

--- a/solution.py
+++ b/solution.py
@@ -181,7 +181,7 @@
 def features(slots, blocks, sources, gates, rows, extras=(), before=None):
     names, operands, specs, layout = [], [], [], []
     rank, mine = rows.shape
-    tokens = blocks[0][0].shape[0]
+    tokens = sources["in"].shape[1]
     vmem = pl.BlockSpec(memory_space=pltpu.VMEM)
 
     def add(name, value):
@@ -216,6 +216,24 @@
     )(*operands)
 
 
+def hold_kernel(source, target, sem):
+    copy = pltpu.make_async_copy(source, target, sem)
+    copy.start()
+    copy.wait()
+
+
+def hold(value):
+    copied = call(
+        hold_kernel,
+        jax.ShapeDtypeStruct(value.shape, value.dtype),
+        [pl.BlockSpec(memory_space=pltpu.HBM)],
+        pl.BlockSpec(memory_space=pl.ANY),
+        scratch_shapes=[pltpu.SemaphoreType.DMA],
+        compiler_params=pltpu.CompilerParams(vmem_limit_bytes=46 << 20),
+    )(value)
+    return pltpu.with_memory_space_constraint(copied, pltpu.VMEM)
+
+
 def scale_kernel(own, *refs):
     others, out_ref = refs[:-1], refs[-1]
     width = own.shape[2] * own.shape[3]
@@ -354,20 +372,22 @@
     half = 2 * rows
     grad_c = send(grad_a, middle_swap)
     grad_d = send(grad_b, to_ends)
-    slot_1 = near_hidden(grad_a)
+    pair = near_hidden(jnp.concatenate([out_grad, grad_a], axis=0))
+    slot_1 = [value[tokens:] for value in pair]
     back_1 = send(jnp.concatenate([near[1], *slot_1], axis=1), lane_move({0: 1, 3: 2}))
     grad_c, near, far, block_3 = tie((grad_c, near, far, block_3))
 
     grad_e = send(grad_c, to_ends)
     block_3 = send(after(block_3, grad_d), flip(3 << LANE_SHIFT))
-    slot_0 = near_hidden(after(out_grad, block_3, far_w))
     grad_2 = jnp.where(at_end, grad_d, grad_c)
     slot_2 = near_hidden(grad_2)
     back_2 = send(jnp.concatenate([near[2], *slot_2], axis=1), lane_move({0: 2, 3: 1}))
-    grad_e, back_2, slot_0 = tie((grad_e, back_2, slot_0))
+    early = jnp.concatenate([out_grad, grad_a, grad_2], axis=0)
+    far_early = hidden(after(early, block_3), far_w)
+    grad_e, back_2, far_early = tie((grad_e, back_2, far_early))
     grad_3 = jnp.where(at_end, grad_e, grad_b)
     slot_3 = near_hidden(grad_3)
-    grads = jnp.concatenate([out_grad, grad_a, grad_2, grad_3], axis=0)
+    grads = jnp.concatenate([early, grad_3], axis=0)
     block_3, back_1, back_2, far_w, near, far, grad_3 = tie(
         (block_3, back_1, back_2, far_w, near, far, grad_3)
     )
@@ -375,8 +395,8 @@
     cross_w = send(far_w, flip(1))
     far_2 = send(far[2], flip(2 << LANE_SHIFT))
     far_1 = send(far[1], flip(1 << LANE_SHIFT))
-    blocks = list(zip(slot_0, slot_1, slot_2, slot_3))
-    blocks += [(hidden(grads, w),) for w in (far_w, cross_w)]
+    blocks = list(zip(pair, slot_2, slot_3))
+    blocks += [(far_early, hidden(grad_3, far_w)), (hidden(grads, cross_w),)]
     low, high = slice(0, half), slice(half, 2 * half)
     extras = [(back, near[j], sides[j]) for j, back in ((1, back_1), (2, back_2))]
     part = features(
@@ -404,7 +424,7 @@
     everyone = [queries] + [send(queries, flip(q)) for q in range(1, QUADS)]
     if devices == LANES * QUADS and tokens == SEQ_LEN:
         where = position.astype(jnp.int32).reshape(1)
-        held = pltpu.with_memory_space_constraint(stored, pltpu.VMEM)
+        held = hold(after(stored, queries))
         return scores(where, everyone, visible, held)
 
     examples_dev = tokens // SEQ_LEN

time: 136 us -> 128 us (0.941)
  waiting for transfers between devices: 44.4 us -> 24.1 us
  starting transfers between devices: 34.9 us -> 49 us
  matrix products: 34.4 us -> 25.4 us
  local copies, waits for them, and re-layouts: 11.8 us -> 14.3 us
  other arithmetic: 2.76 us -> 5.04 us
  Pallas kernels: 6.67 us -> 8.65 us
    ppermute x19, waiting for transfers between devices: 44.4 us -> 24.1 us  [send(): return lax.ppermute(value, 'row', pairs)]
    ppermute x19, starting transfers between devices: 34.9 us -> 49 us  [send(): return lax.ppermute(value, 'row', pairs)]
    dot_general x10 -> x9, matrix products: 33.9 us -> 24.9 us  [hidden(): lax.dot_general(grads, weight, (((1,), (1,)), ((), ())), preferred_elemen...]
    pallas_call x0 -> x1, Pallas kernels: none -> 2.79 us  [hold(): call(hold_kernel, jax.ShapeDtypeStruct(value.shape, value.dtype), [pl.Blo...]
    concatenate x0 -> x1, other arithmetic: none -> 1.98 us  [shards(): early = jnp.concatenate([out_grad, grad_a, grad_2], axis=0)]
    unnamed x42 -> x51, local copies, waits for them, and re-layouts: 8.2 us -> 7.54 us
  transfers between devices with their start and end apart: 19 -> 19, of which waited for: 7 -> 7; matrix products, arithmetic and copies ran while one was open for 30% -> 30% of each run, Pallas kernels for 2% -> 4%
where the time goes in v4:
time: 128 us; the launch traced here: 127 us
  starting transfers between devices  49 us (38%)
  matrix products  25.4 us (20%)
  waiting for transfers between devices  24.1 us (19%)
  local copies, waits for them, and re-layouts  14.3 us (11%)
  Pallas kernels  8.65 us (7%)
  other arithmetic  5.04 us (4%)
    ppermute x19, starting transfers between devices, send(): return lax.ppermute(value, 'row', pairs)  49 us
    dot_general x9, matrix products, hidden(): lax.dot_general(grads, weight, (((1,), (1,)), ((), ())), preferred_elemen...  24.9 us
    ppermute x19, waiting for transfers between devices, send(): return lax.ppermute(value, 'row', pairs)  24.1 us
    unnamed x51, local copies, waits for them, and re-layouts  7.54 us
    pallas_call x1, Pallas kernels, hold(): call(hold_kernel, jax.ShapeDtypeStruct(value.shape, value.dtype), [pl.Blo...  2.79 us
    pallas_call x2, Pallas kernels, features(): call(functools.partial(feature_kernel, slots, layout, gates, len(extras),...  2.62 us
  transfers between devices with their start and end apart: 19, of which 7 were waited for; matrix products, arithmetic and copies ran while one was open for 30% of the time, Pallas kernels for 4%

profile of v4, /device:TPU:0, one launch (start us, length us, event | category | flops | bytes accessed | tf_op | source)
XLA Modules:
  0.0 127.0 jit_solution(12470391966068111171)
XLA Ops:
  0.5 1.8 %collective-permute-start.2 = (bf16[128,4096]{1,0:T(8,128)(2,1)}, bf16[128,4096]{1,0:T(8,128)(2,1)}, u32[]{:S(2)}, u32[]{:S(2)}) collective-permute-start(bf16[128,4096]{1,0:T(8,128)(2,1)} %param.10), channel_id=1, source_target_pairs={{4,8},{5,9},{6,10},{7,11},{8,4},{9,5},{10,6},{11,7},{20,24},{21,25... | collective-permute-start | bytes 3145736 | tf_op jit(solution)/shard_map/ppermute | solution.py:313
  2.2 4.6 %collective-permute-start = (bf16[128,4096]{1,0:T(8,128)(2,1)}, bf16[128,4096]{1,0:T(8,128)(2,1)}, u32[]{:S(2)}, u32[]{:S(2)}) collective-permute-start(bf16[128,4096]{1,0:T(8,128)(2,1)} %param.10), channel_id=1, source_target_pairs={{0,4},{1,5},{2,6},{3,7},{4,0},{5,1},{6,2},{7,3},{8,12},{9,13},{10,... | collective-permute-start | bytes 3145736 | tf_op jit(solution)/shard_map/ppermute | solution.py:313
  6.9 1.5 %collective-permute-start.8 = (bf16[448,4096]{1,0:T(8,128)(2,1)}, bf16[448,4096]{1,0:T(8,128)(2,1)}, u32[]{:S(2)}, u32[]{:S(2)}) collective-permute-start(bf16[448,4096]{1,0:T(8,128)(2,1)} %param.11), channel_id=1, source_target_pairs={{0,2},{1,3},{2,0},{3,1},{4,6},{5,7},{6,4},{7,5},{8,10},{9,11},{10,... | collective-permute-start | bytes 11010056 | tf_op jit(solution)/shard_map/ppermute | solution.py:313
  8.4 2.2 %reshape.16 = bf16[32,2,4096]{2,1,0:T(2,128)(2,1)} reshape(bf16[64,4096]{1,0:T(8,128)(2,1)} %bitcast.40) | data formatting | bytes 1048576 | tf_op jit(solution)/shard_map/reshape | solution.py:351
  10.5 1.3 %copy.31 = bf16[2,32,4096]{2,1,0:T(8,128)(2,1)S(1)} copy(bf16[2,32,4096]{2,0,1:T(2,128)(2,1)} %bitcast.39) | data formatting | bytes 1048576 | tf_op jit(solution)/shard_map/transpose | solution.py:351
  12.4 1.3 %constant_dynamic-update-slice_fusion.1 = bf16[256,4096]{1,0:T(8,128)(2,1)S(1)} fusion(bf16[128,4096]{1,0:T(8,128)(2,1)} %param.10), kind=kLoop, calls=%fused_computation.23 | loop fusion | bytes 2097152
  20.7 1.3 %collective-permute-start.3 = (bf16[128,4096]{1,0:T(8,128)(2,1)}, bf16[128,4096]{1,0:T(8,128)(2,1)}, u32[]{:S(2)}, u32[]{:S(2)}) collective-permute-start(bf16[128,4096]{1,0:T(8,128)(2,1)} %collective-permute-done.2), channel_id=1, source_target_pairs={{4,0},{5,1},{6,2},{7,3},{8,12},{9,13},{10,14},{11,15},{20,16},{21,... | collective-permute-start | bytes 3145736 | tf_op jit(solution)/shard_map/ppermute | solution.py:313
  22.0 8.6 %collective-permute-done = bf16[128,4096]{1,0:T(8,128)(2,1)} collective-permute-done((bf16[128,4096]{1,0:T(8,128)(2,1)}, bf16[128,4096]{1,0:T(8,128)(2,1)}, u32[]{:S(2)}, u32[]{:S(2)}) %collective-permute-start) | collective-permute-done | bytes 1048608 | tf_op jit(solution)/shard_map/ppermute | solution.py:313
  30.6 1.6 %collective-permute-start.4 = (bf16[128,4096]{1,0:T(8,128)(2,1)}, bf16[128,4096]{1,0:T(8,128)(2,1)}, u32[]{:S(2)}, u32[]{:S(2)}) collective-permute-start(bf16[128,4096]{1,0:T(8,128)(2,1)} %collective-permute-done), channel_id=1, source_target_pairs={{4,8},{5,9},{6,10},{7,11},{8,4},{9,5},{10,6},{11,7},{20,24},{21,25... | collective-permute-start | bytes 3145736 | tf_op jit(solution)/shard_map/ppermute | solution.py:313
  32.2 1.3 %constant_dynamic-update-slice_fusion = bf16[256,4096]{1,0:T(8,128)(2,1)S(1)} fusion(bf16[256,4096]{1,0:T(8,128)(2,1)S(1)} %constant_dynamic-update-slice_fusion.1, bf16[128,4096]{1,0:T(8,128)(2,1)} %collective-permute-done), kind=kLoop, calls=%fused_computation.22 | loop fusion | bytes 2097152 | tf_op jit(solution)/shard_map/concatenate | solution.py:375
  33.6 3.5 %convolution_convert_fusion.1.refs_3_ = bf16[256,448]{1,0:T(8,128)(2,1)S(1)} fusion(bf16[256,4096]{1,0:T(8,128)(2,1)S(1)} %constant_dynamic-update-slice_fusion, bf16[448,4096]{1,0:T(8,128)(2,1)} %collective-permute-done.1), kind=kOutput, calls=%fused_computation.11 | convolution fusion | flops 939638784 | bytes 5996544 | tf_op jit(solution)/shard_map/dot_general | solution.py:365
  39.3 6.7 %collective-permute-start.9 = (bf16[128,1792]{1,0:T(8,128)(2,1)}, bf16[128,1792]{1,0:T(8,128)(2,1)S(1)}, u32[]{:S(2)}, u32[]{:S(2)}) collective-permute-start(bf16[128,1792]{1,0:T(8,128)(2,1)} %concatenate.19), channel_id=1, source_target_pairs={{0,4},{1,5},{2,6},{3,7},{12,8},{13,9},{14,10},{15,11},{16,20},{17,... | collective-permute-start | bytes 1376264 | tf_op jit(solution)/shard_map/ppermute | solution.py:313
  46.0 9.4 %collective-permute-done.3 = bf16[128,4096]{1,0:T(8,128)(2,1)} collective-permute-done((bf16[128,4096]{1,0:T(8,128)(2,1)}, bf16[128,4096]{1,0:T(8,128)(2,1)}, u32[]{:S(2)}, u32[]{:S(2)}) %collective-permute-start.3) | collective-permute-done | bytes 1048608 | tf_op jit(solution)/shard_map/ppermute | solution.py:313
  55.4 2.5 %collective-permute-start.7 = (bf16[144,1792]{1,0:T(8,128)(2,1)}, bf16[144,1792]{1,0:T(8,128)(2,1)S(1)}, u32[]{:S(2)}, u32[]{:S(2)}) collective-permute-start(bf16[144,1792]{1,0:T(8,128)(2,1)} %copy-done.13), channel_id=1, source_target_pairs={{0,12},{1,13},{2,14},{3,15},{4,8},{5,9},{6,10},{7,11},{8,4},{9,5},... | collective-permute-start | bytes 1548296 | tf_op jit(solution)/shard_map/ppermute | solution.py:313
  59.2 1.3 %broadcast_select_fusion.1 = bf16[128,4096]{1,0:T(8,128)(2,1)S(1)} fusion(bf16[128,4096]{1,0:T(8,128)(2,1)} %collective-permute-done.3, bf16[128,4096]{1,0:T(8,128)(2,1)} %collective-permute-done.4, pred[]{:T(512)S(6)} %or.3), kind=kLoop, calls=%fused_computation.20 | loop fusion | flops 524288 | bytes 3145729 | tf_op jit(solution)/shard_map/jit(_where)/select_n | solution.py:382
  60.5 3.7 %convolution_convert_fusion.6.refs_4_ = bf16[128,448]{1,0:T(8,128)(2,1)S(1)} fusion(bf16[128,4096]{1,0:T(8,128)(2,1)S(1)} %broadcast_select_fusion.1, bf16[448,4096]{1,0:T(8,128)(2,1)} %collective-permute-done.1), kind=kOutput, calls=%fused_computation.16 | convolution fusion | flops 469819392 | bytes 4833280 | tf_op jit(solution)/shard_map/dot_general | solution.py:365
  66.3 18.0 %collective-permute-start.6 = (bf16[128,1792]{1,0:T(8,128)(2,1)}, bf16[128,1792]{1,0:T(8,128)(2,1)S(1)}, u32[]{:S(2)}, u32[]{:S(2)}) collective-permute-start(bf16[128,1792]{1,0:T(8,128)(2,1)} %concatenate.17), channel_id=1, source_target_pairs={{0,8},{1,9},{2,10},{3,11},{12,4},{13,5},{14,6},{15,7},{16,24},{17,... | collective-permute-start | bytes 1376264 | tf_op jit(solution)/shard_map/ppermute | solution.py:313
  84.4 2.0 %pad_maximum_fusion = bf16[384,4096]{1,0:T(8,128)(2,1)S(1)} fusion(bf16[128,4096]{1,0:T(8,128)(2,1)} %copy-done.18, bf16[128,4096]{1,0:T(8,128)(2,1)} %collective-permute-done, bf16[128,4096]{1,0:T(8,128)(2,1)} %param.10), kind=kLoop, calls=%fused_computation.8 | loop fusion | flops 9437184 | bytes 6291456 | tf_op jit(solution)/shard_map/concatenate | solution.py:385
  86.4 1.8 %collective-permute-done.8 = bf16[448,4096]{1,0:T(8,128)(2,1)} collective-permute-done((bf16[448,4096]{1,0:T(8,128)(2,1)}, bf16[448,4096]{1,0:T(8,128)(2,1)}, u32[]{:S(2)}, u32[]{:S(2)}) %collective-permute-start.8) | collective-permute-done | bytes 3670048 | tf_op jit(solution)/shard_map/ppermute | solution.py:313
  88.2 3.8 %convolution_convert_fusion.refs_6_ = bf16[384,448]{1,0:T(8,128)(2,1)S(1)} fusion(bf16[384,4096]{1,0:T(8,128)(2,1)S(1)} %pad_maximum_fusion, bf16[448,4096]{1,0:T(8,128)(2,1)} %collective-permute-done.8), kind=kOutput, calls=%fused_computation.10 | convolution fusion | flops 1409458176 | bytes 7159808 | tf_op jit(solution)/shard_map/dot_general | solution.py:365
  92.7 1.6 %broadcast_select_fusion = bf16[128,4096]{1,0:T(8,128)(2,1)S(1)} fusion(bf16[128,4096]{1,0:T(8,128)(2,1)} %collective-permute-done.5, bf16[128,4096]{1,0:T(8,128)(2,1)} %collective-permute-done.2, pred[]{:T(512)S(6)} %or.3), kind=kLoop, calls=%fused_computation.19 | loop fusion | flops 524288 | bytes 3145729 | tf_op jit(solution)/shard_map/jit(_where)/select_n | solution.py:388
  95.3 1.9 %collective-permute-start.12 = (bf16[144,896]{1,0:T(8,128)(2,1)S(1)}, bf16[144,896]{1,0:T(8,128)(2,1)S(1)}, u32[]{:S(2)}, u32[]{:S(2)}) collective-permute-start(bf16[144,896]{1,0:T(8,128)(2,1)S(1)} %copy-done.15), channel_id=1, source_target_pairs={{0,8},{1,9},{2,10},{3,11},{4,12},{5,13},{6,14},{7,15},{8,0},{9,1},... | collective-permute-start | bytes 774152 | tf_op jit(solution)/shard_map/ppermute | solution.py:313
  97.2 3.3 %convolution_convert_fusion.4.refs_5_ = bf16[128,448]{1,0:T(8,128)(2,1)S(1)} fusion(bf16[128,4096]{1,0:T(8,128)(2,1)S(1)} %broadcast_select_fusion, bf16[448,4096]{1,0:T(8,128)(2,1)} %collective-permute-done.1), kind=kOutput, calls=%fused_computation.14 | convolution fusion | flops 469819392 | bytes 4833280 | tf_op jit(solution)/shard_map/dot_general | solution.py:365
  101.8 3.3 %convolution_convert_fusion.3.refs_7_ = bf16[128,448]{1,0:T(8,128)(2,1)S(1)} fusion(bf16[128,4096]{1,0:T(8,128)(2,1)S(1)} %broadcast_select_fusion, bf16[448,4096]{1,0:T(8,128)(2,1)} %collective-permute-done.8), kind=kOutput, calls=%fused_computation.13 | convolution fusion | flops 469819392 | bytes 4833280 | tf_op jit(solution)/shard_map/dot_general | solution.py:365
  105.1 3.7 %fusion.8.refs_8_ = bf16[512,448]{1,0:T(8,128)(2,1)S(1)} fusion(bf16[448,4096]{1,0:T(8,128)(2,1)S(1)} %collective-permute-done.10, bf16[128,4096]{1,0:T(8,128)(2,1)S(1)} %broadcast_select_fusion, bf16[128,4096]{1,0:T(8,128)(2,1)S(1)} %copy-done.19, bf16[128,4096]{1,0:T(8,128)(2,1)} %collective-permute-done, bf16[128,4096]{1,0:T(8,128)(2,1)S(1)} %copy-done.23), kind=kOutput, calls=%fused_computation.9 | convolution fusion | flops 1896054784 | bytes 8323072 | tf_op jit(solution)/shard_map/dot_general | solution.py:365
  108.9 1.4 %shard_map.83.refs_15_ = bf16[4,1,32,128]{3,2,1,0:T(8,128)(2,1)S(1)} custom-call(bf16[256,448]{1,0:T(8,128)(2,1)S(1)} %convolution_convert_fusion.2.refs_0_, bf16[128,448]{1,0:T(8,128)(2,1)S(1)} %convolution_convert_fusion.7.refs_1_, bf16[128,448]{1,0:T(8,128)(2,1)S(1)} %convolution_convert_fusion.5.refs_2_, ...), custom_call_target="tpu_custom_call" | custom-call | flops 1000 | bytes 1000 | tf_op jit(solution)/shard_map/pallas_call | solution.py:209
  111.9 1.9 %collective-permute-start.14 = (bf16[4,1,32,128]{3,2,1,0:T(8,128)(2,1)S(1)}, bf16[4,1,32,128]{3,2,1,0:T(8,128)(2,1)S(1)}, u32[]{:S(2)}, u32[]{:S(2)}) collective-permute-start(bf16[4,1,32,128]{3,2,1,0:T(8,128)(2,1)S(1)} %shard_map.84.own), channel_id=1, source_target_pairs={{0,8},{1,9},{2,10},{3,11},{4,12},{5,13},{6,14},{7,15},{8,0},{9,1},... | collective-permute-start | bytes 98312 | tf_op jit(solution)/shard_map/ppermute | solution.py:313
  113.8 2.2 %collective-permute-start.15 = (bf16[4,1,32,128]{3,2,1,0:T(8,128)(2,1)S(1)}, bf16[4,1,32,128]{3,2,1,0:T(8,128)(2,1)S(1)}, u32[]{:S(2)}, u32[]{:S(2)}) collective-permute-start(bf16[4,1,32,128]{3,2,1,0:T(8,128)(2,1)S(1)} %shard_map.84.own), channel_id=1, source_target_pairs={{0,12},{1,13},{2,14},{3,15},{4,8},{5,9},{6,10},{7,11},{8,4},{9,5},... | collective-permute-start | bytes 98312 | tf_op jit(solution)/shard_map/ppermute | solution.py:313
  117.0 2.5 %collective-permute-done.15.refs_2_ = bf16[4,1,32,128]{3,2,1,0:T(8,128)(2,1)S(1)} collective-permute-done((bf16[4,1,32,128]{3,2,1,0:T(8,128)(2,1)S(1)}, bf16[4,1,32,128]{3,2,1,0:T(8,128)(2,1)S(1)}, u32[]{:S(2)}, u32[]{:S(2)}) %collective-permute-start.15) | collective-permute-done | bytes 32800 | tf_op jit(solution)/shard_map/ppermute | solution.py:313
  119.7 1.6 %collective-permute-start.17 = (bf16[4,1,32,128]{3,2,1,0:T(8,128)(2,1)S(1)}, bf16[4,1,32,128]{3,2,1,0:T(8,128)(2,1)S(1)}, u32[]{:S(2)}, u32[]{:S(2)}) collective-permute-start(bf16[4,1,32,128]{3,2,1,0:T(8,128)(2,1)S(1)} %shard_map.85.q0), channel_id=1, source_target_pairs={{0,2},{1,3},{2,0},{3,1},{4,6},{5,7},{6,4},{7,5},{8,10},{9,11},{10,... | collective-permute-start | bytes 98312 | tf_op jit(solution)/shard_map/ppermute | solution.py:313
  121.6 2.8 %shard_map.86.stored_ref = bf16[768,4096]{1,0:T(8,128)(2,1)S(1)} custom-call(bf16[768,4096]{1,0:T(8,128)(2,1)} %source), custom_call_target="tpu_custom_call" | custom-call | flops 1000 | bytes 1000 | tf_op jit(solution)/shard_map/pallas_call | solution.py:226
  124.6 2.4 %shard_map.87 = f32[16,768]{1,0:T(8,128)} custom-call(s32[1]{0:T(128)} %bitcast.where_ref, bf16[4,1,32,128]{3,2,1,0:T(8,128)(2,1)S(1)} %shard_map.85.q0, bf16[4,1,32,128]{3,2,1,0:T(8,128)(2,1)S(1)} %collective-permute-done.16.q1, bf16[4,1,32,128]{3,2,1,0:T(8,128)(2,1)S(1)} %collective-permute-done.17.q2, ...), custom_call_target="tpu_custom_call" | custom-call | flops 1000 | bytes 1000 | tf_op jit(solution)/shard_map/pallas_call | solution.py:289
  (86 shorter events, 19.8 us)
Async XLA Ops:
  0.0 11.9 %copy-start = (bf16[128,4096]{1,0:T(8,128)(2,1)S(1)}, bf16[128,4096]{1,0:T(8,128)(2,1)}, u32[]{:S(2)}) copy-start(bf16[128,4096]{1,0:T(8,128)(2,1)} %param.8) | copy-start | bytes 3145732
  0.0 13.8 %copy-start.1 = (bf16[128,7168]{1,0:T(8,128)(2,1)S(1)}, bf16[128,7168]{1,0:T(8,128)(2,1)}, u32[]{:S(2)}) copy-start(bf16[128,7168]{1,0:T(8,128)(2,1)} %gate_ref.1) | copy-start | bytes 5505028
  0.0 30.6 %collective-permute-start.1 = (bf16[448,4096]{1,0:T(8,128)(2,1)}, bf16[448,4096]{1,0:T(8,128)(2,1)}, u32[]{:S(2)}, u32[]{:S(2)}) collective-permute-start(bf16[448,4096]{1,0:T(8,128)(2,1)} %param.11), channel_id=1, source_target_pairs={{0,1},{1,0},{2,3},{3,2},{4,5},{5,4},{6,7},{7,6},{8,9},{9,8},{10,11... | collective-permute-start | bytes 11010056 | tf_op jit(solution)/shard_map/ppermute | solution.py:313
  0.5 20.2 %collective-permute-start.2 = (bf16[128,4096]{1,0:T(8,128)(2,1)}, bf16[128,4096]{1,0:T(8,128)(2,1)}, u32[]{:S(2)}, u32[]{:S(2)}) collective-permute-start(bf16[128,4096]{1,0:T(8,128)(2,1)} %param.10), channel_id=1, source_target_pairs={{4,8},{5,9},{6,10},{7,11},{8,4},{9,5},{10,6},{11,7},{20,24},{21,25... | collective-permute-start | bytes 3145736 | tf_op jit(solution)/shard_map/ppermute | solution.py:313
  2.2 28.4 %collective-permute-start = (bf16[128,4096]{1,0:T(8,128)(2,1)}, bf16[128,4096]{1,0:T(8,128)(2,1)}, u32[]{:S(2)}, u32[]{:S(2)}) collective-permute-start(bf16[128,4096]{1,0:T(8,128)(2,1)} %param.10), channel_id=1, source_target_pairs={{0,4},{1,5},{2,6},{3,7},{4,0},{5,1},{6,2},{7,3},{8,12},{9,13},{10,... | collective-permute-start | bytes 3145736 | tf_op jit(solution)/shard_map/ppermute | solution.py:313
  6.9 81.4 %collective-permute-start.8 = (bf16[448,4096]{1,0:T(8,128)(2,1)}, bf16[448,4096]{1,0:T(8,128)(2,1)}, u32[]{:S(2)}, u32[]{:S(2)}) collective-permute-start(bf16[448,4096]{1,0:T(8,128)(2,1)} %param.11), channel_id=1, source_target_pairs={{0,2},{1,3},{2,0},{3,1},{4,6},{5,7},{6,4},{7,5},{8,10},{9,11},{10,... | collective-permute-start | bytes 11010056 | tf_op jit(solution)/shard_map/ppermute | solution.py:313
  20.7 34.7 %collective-permute-start.3 = (bf16[128,4096]{1,0:T(8,128)(2,1)}, bf16[128,4096]{1,0:T(8,128)(2,1)}, u32[]{:S(2)}, u32[]{:S(2)}) collective-permute-start(bf16[128,4096]{1,0:T(8,128)(2,1)} %collective-permute-done.2), channel_id=1, source_target_pairs={{4,0},{5,1},{6,2},{7,3},{8,12},{9,13},{10,14},{11,15},{20,16},{21,... | collective-permute-start | bytes 3145736 | tf_op jit(solution)/shard_map/ppermute | solution.py:313
  30.6 15.4 %collective-permute-start.4 = (bf16[128,4096]{1,0:T(8,128)(2,1)}, bf16[128,4096]{1,0:T(8,128)(2,1)}, u32[]{:S(2)}, u32[]{:S(2)}) collective-permute-start(bf16[128,4096]{1,0:T(8,128)(2,1)} %collective-permute-done), channel_id=1, source_target_pairs={{4,8},{5,9},{6,10},{7,11},{8,4},{9,5},{10,6},{11,7},{20,24},{21,25... | collective-permute-start | bytes 3145736 | tf_op jit(solution)/shard_map/ppermute | solution.py:313
  39.3 24.9 %copy-start.21 = (bf16[448,4096]{1,0:T(8,128)(2,1)S(1)}, bf16[448,4096]{1,0:T(8,128)(2,1)}, u32[]{:S(2)}) copy-start(bf16[448,4096]{1,0:T(8,128)(2,1)} %param.11) | copy-start | bytes 11010052
  39.3 55.0 %collective-permute-start.9 = (bf16[128,1792]{1,0:T(8,128)(2,1)}, bf16[128,1792]{1,0:T(8,128)(2,1)S(1)}, u32[]{:S(2)}, u32[]{:S(2)}) collective-permute-start(bf16[128,1792]{1,0:T(8,128)(2,1)} %concatenate.19), channel_id=1, source_target_pairs={{0,4},{1,5},{2,6},{3,7},{12,8},{13,9},{14,10},{15,11},{16,20},{17,... | collective-permute-start | bytes 1376264 | tf_op jit(solution)/shard_map/ppermute | solution.py:313
  55.4 31.0 %collective-permute-start.7 = (bf16[144,1792]{1,0:T(8,128)(2,1)}, bf16[144,1792]{1,0:T(8,128)(2,1)S(1)}, u32[]{:S(2)}, u32[]{:S(2)}) collective-permute-start(bf16[144,1792]{1,0:T(8,128)(2,1)} %copy-done.13), channel_id=1, source_target_pairs={{0,12},{1,13},{2,14},{3,15},{4,8},{5,9},{6,10},{7,11},{8,4},{9,5},... | collective-permute-start | bytes 1548296 | tf_op jit(solution)/shard_map/ppermute | solution.py:313
  57.9 34.8 %collective-permute-start.5 = (bf16[128,4096]{1,0:T(8,128)(2,1)}, bf16[128,4096]{1,0:T(8,128)(2,1)}, u32[]{:S(2)}, u32[]{:S(2)}) collective-permute-start(bf16[128,4096]{1,0:T(8,128)(2,1)} %collective-permute-done.4), channel_id=1, source_target_pairs={{4,0},{5,1},{6,2},{7,3},{8,12},{9,13},{10,14},{11,15},{20,16},{21,... | collective-permute-start | bytes 3145736 | tf_op jit(solution)/shard_map/ppermute | solution.py:313
  66.3 25.8 %collective-permute-start.6 = (bf16[128,1792]{1,0:T(8,128)(2,1)}, bf16[128,1792]{1,0:T(8,128)(2,1)S(1)}, u32[]{:S(2)}, u32[]{:S(2)}) collective-permute-start(bf16[128,1792]{1,0:T(8,128)(2,1)} %concatenate.17), channel_id=1, source_target_pairs={{0,8},{1,9},{2,10},{3,11},{12,4},{13,5},{14,6},{15,7},{16,24},{17,... | collective-permute-start | bytes 1376264 | tf_op jit(solution)/shard_map/ppermute | solution.py:313
  86.3 8.1 %copy-start.17 = (bf16[144,896]{1,0:T(8,128)(2,1)S(1)}, bf16[144,896]{1,0:T(8,128)(2,1)}, u32[]{:S(2)}) copy-start(bf16[144,896]{1,0:T(8,128)(2,1)} %copy-done.16) | copy-start | bytes 774148
  86.4 9.0 %copy-start.15 = (bf16[144,896]{1,0:T(8,128)(2,1)S(1)}, bf16[144,896]{1,0:T(8,128)(2,1)}, u32[]{:S(2)}) copy-start(bf16[144,896]{1,0:T(8,128)(2,1)} %copy-done.14) | copy-start | bytes 774148
  86.4 5.7 %copy-start.5 = (bf16[144,1792]{1,0:T(8,128)(2,1)}, bf16[144,1792]{1,0:T(8,128)(2,1)S(1)}, u32[]{:S(2)}) copy-start(bf16[144,1792]{1,0:T(8,128)(2,1)S(1)} %collective-permute-done.7.refs_11_) | copy-start | bytes 1548292
  92.1 8.4 %copy-start.22 = (bf16[448,4096]{1,0:T(8,128)(2,1)S(1)}, bf16[448,4096]{1,0:T(8,128)(2,1)}, u32[]{:S(2)}) copy-start(bf16[448,4096]{1,0:T(8,128)(2,1)} %param.11) | copy-start | bytes 11010052
  94.3 10.8 %collective-permute-start.10 = (bf16[448,4096]{1,0:T(8,128)(2,1)}, bf16[448,4096]{1,0:T(8,128)(2,1)S(1)}, u32[]{:S(2)}, u32[]{:S(2)}) collective-permute-start(bf16[448,4096]{1,0:T(8,128)(2,1)} %collective-permute-done.8), channel_id=1, source_target_pairs={{0,1},{1,0},{2,3},{3,2},{4,5},{5,4},{6,7},{7,6},{8,9},{9,8},{10,11... | collective-permute-start | bytes 11010056 | tf_op jit(solution)/shard_map/ppermute | solution.py:313
  94.4 15.9 %collective-permute-start.11 = (bf16[144,896]{1,0:T(8,128)(2,1)S(1)}, bf16[144,896]{1,0:T(8,128)(2,1)S(1)}, u32[]{:S(2)}, u32[]{:S(2)}) collective-permute-start(bf16[144,896]{1,0:T(8,128)(2,1)S(1)} %copy-done.17), channel_id=1, source_target_pairs={{0,4},{1,5},{2,6},{3,7},{4,0},{5,1},{6,2},{7,3},{8,12},{9,13},{10,... | collective-permute-start | bytes 774152 | tf_op jit(solution)/shard_map/ppermute | solution.py:313
  95.3 15.0 %collective-permute-start.12 = (bf16[144,896]{1,0:T(8,128)(2,1)S(1)}, bf16[144,896]{1,0:T(8,128)(2,1)S(1)}, u32[]{:S(2)}, u32[]{:S(2)}) collective-permute-start(bf16[144,896]{1,0:T(8,128)(2,1)S(1)} %copy-done.15), channel_id=1, source_target_pairs={{0,8},{1,9},{2,10},{3,11},{4,12},{5,13},{6,14},{7,15},{8,0},{9,1},... | collective-permute-start | bytes 774152 | tf_op jit(solution)/shard_map/ppermute | solution.py:313
  100.5 4.6 %copy-start.19 = (bf16[128,4096]{1,0:T(8,128)(2,1)S(1)}, bf16[128,4096]{1,0:T(8,128)(2,1)}, u32[]{:S(2)}) copy-start(bf16[128,4096]{1,0:T(8,128)(2,1)} %copy-done.18) | copy-start | bytes 3145732
  100.5 4.6 %copy-start.23 = (bf16[128,4096]{1,0:T(8,128)(2,1)S(1)}, bf16[128,4096]{1,0:T(8,128)(2,1)}, u32[]{:S(2)}) copy-start(bf16[128,4096]{1,0:T(8,128)(2,1)} %param.10) | copy-start | bytes 3145732
  105.0 3.8 %copy-start.4 = (bf16[64,1792]{1,0:T(8,128)(2,1)S(1)}, bf16[64,1792]{1,0:T(8,128)(2,1)}, u32[]{:S(2)}) copy-start(bf16[64,1792]{1,0:T(8,128)(2,1)} %copy-done.3) | copy-start | bytes 688132
  105.1 3.8 %copy-start.6 = (bf16[144,1792]{1,0:T(8,128)(2,1)S(1)}, bf16[144,1792]{1,0:T(8,128)(2,1)}, u32[]{:S(2)}) copy-start(bf16[144,1792]{1,0:T(8,128)(2,1)} %copy-done.5) | copy-start | bytes 1548292
  105.1 3.8 %copy-start.8 = (bf16[128,896]{1,0:T(8,128)(2,1)S(1)}, bf16[128,896]{1,0:T(8,128)(2,1)}, u32[]{:S(2)}) copy-start(bf16[128,896]{1,0:T(8,128)(2,1)} %copy-done.7) | copy-start | bytes 688132
  108.8 12.7 %copy-start.24 = (s32[16]{0:T(128)S(1)}, s32[16]{0:T(128)}, u32[]{:S(2)}) copy-start(s32[16]{0:T(128)} %param.15) | copy-start | bytes 196
  111.5 4.5 %collective-permute-start.13 = (bf16[4,1,32,128]{3,2,1,0:T(8,128)(2,1)S(1)}, bf16[4,1,32,128]{3,2,1,0:T(8,128)(2,1)S(1)}, u32[]{:S(2)}, u32[]{:S(2)}) collective-permute-start(bf16[4,1,32,128]{3,2,1,0:T(8,128)(2,1)S(1)} %shard_map.84.own), channel_id=1, source_target_pairs={{0,4},{1,5},{2,6},{3,7},{4,0},{5,1},{6,2},{7,3},{8,12},{9,13},{10,... | collective-permute-start | bytes 98312 | tf_op jit(solution)/shard_map/ppermute | solution.py:313
  111.9 5.1 %collective-permute-start.14 = (bf16[4,1,32,128]{3,2,1,0:T(8,128)(2,1)S(1)}, bf16[4,1,32,128]{3,2,1,0:T(8,128)(2,1)S(1)}, u32[]{:S(2)}, u32[]{:S(2)}) collective-permute-start(bf16[4,1,32,128]{3,2,1,0:T(8,128)(2,1)S(1)} %shard_map.84.own), channel_id=1, source_target_pairs={{0,8},{1,9},{2,10},{3,11},{4,12},{5,13},{6,14},{7,15},{8,0},{9,1},... | collective-permute-start | bytes 98312 | tf_op jit(solution)/shard_map/ppermute | solution.py:313
  113.8 5.7 %collective-permute-start.15 = (bf16[4,1,32,128]{3,2,1,0:T(8,128)(2,1)S(1)}, bf16[4,1,32,128]{3,2,1,0:T(8,128)(2,1)S(1)}, u32[]{:S(2)}, u32[]{:S(2)}) collective-permute-start(bf16[4,1,32,128]{3,2,1,0:T(8,128)(2,1)S(1)} %shard_map.84.own), channel_id=1, source_target_pairs={{0,12},{1,13},{2,14},{3,15},{4,8},{5,9},{6,10},{7,11},{8,4},{9,5},... | collective-permute-start | bytes 98312 | tf_op jit(solution)/shard_map/ppermute | solution.py:313
  119.6 4.8 %collective-permute-start.16 = (bf16[4,1,32,128]{3,2,1,0:T(8,128)(2,1)S(1)}, bf16[4,1,32,128]{3,2,1,0:T(8,128)(2,1)S(1)}, u32[]{:S(2)}, u32[]{:S(2)}) collective-permute-start(bf16[4,1,32,128]{3,2,1,0:T(8,128)(2,1)S(1)} %shard_map.85.q0), channel_id=1, source_target_pairs={{0,1},{1,0},{2,3},{3,2},{4,5},{5,4},{6,7},{7,6},{8,9},{9,8},{10,11... | collective-permute-start | bytes 98312 | tf_op jit(solution)/shard_map/ppermute | solution.py:313
  119.7 4.8 %collective-permute-start.17 = (bf16[4,1,32,128]{3,2,1,0:T(8,128)(2,1)S(1)}, bf16[4,1,32,128]{3,2,1,0:T(8,128)(2,1)S(1)}, u32[]{:S(2)}, u32[]{:S(2)}) collective-permute-start(bf16[4,1,32,128]{3,2,1,0:T(8,128)(2,1)S(1)} %shard_map.85.q0), channel_id=1, source_target_pairs={{0,2},{1,3},{2,0},{3,1},{4,6},{5,7},{6,4},{7,5},{8,10},{9,11},{10,... | collective-permute-start | bytes 98312 | tf_op jit(solution)/shard_map/ppermute | solution.py:313
  121.2 3.3 %collective-permute-start.18 = (bf16[4,1,32,128]{3,2,1,0:T(8,128)(2,1)S(1)}, bf16[4,1,32,128]{3,2,1,0:T(8,128)(2,1)S(1)}, u32[]{:S(2)}, u32[]{:S(2)}) collective-permute-start(bf16[4,1,32,128]{3,2,1,0:T(8,128)(2,1)S(1)} %shard_map.85.q0), channel_id=1, source_target_pairs={{0,3},{1,2},{2,1},{3,0},{4,7},{5,6},{6,5},{7,4},{8,11},{9,10},{10,... | collective-permute-start | bytes 98312 | tf_op jit(solution)/shard_map/ppermute | solution.py:313
  (12 other events, 20.9 us)

commit v5 on v4

--- a/solution.py
+++ b/solution.py
@@ -222,16 +222,15 @@
     copy.wait()
 
 
-def hold(value):
-    copied = call(
+def hold(value, limit):
+    return call(
         hold_kernel,
         jax.ShapeDtypeStruct(value.shape, value.dtype),
         [pl.BlockSpec(memory_space=pltpu.HBM)],
         pl.BlockSpec(memory_space=pl.ANY),
         scratch_shapes=[pltpu.SemaphoreType.DMA],
-        compiler_params=pltpu.CompilerParams(vmem_limit_bytes=46 << 20),
+        compiler_params=pltpu.CompilerParams(vmem_limit_bytes=limit << 20),
     )(value)
-    return pltpu.with_memory_space_constraint(copied, pltpu.VMEM)
 
 
 def scale_kernel(own, *refs):
@@ -371,11 +370,11 @@
 
     half = 2 * rows
     grad_c = send(grad_a, middle_swap)
-    grad_d = send(grad_b, to_ends)
+    grad_d = send(after(grad_b, grad_a), to_ends)
     pair = near_hidden(jnp.concatenate([out_grad, grad_a], axis=0))
     slot_1 = [value[tokens:] for value in pair]
     back_1 = send(jnp.concatenate([near[1], *slot_1], axis=1), lane_move({0: 1, 3: 2}))
-    grad_c, near, far, block_3 = tie((grad_c, near, far, block_3))
+    grad_c, near, far, block_3, pair = tie((grad_c, near, far, block_3, pair))
 
     grad_e = send(grad_c, to_ends)
     block_3 = send(after(block_3, grad_d), flip(3 << LANE_SHIFT))
@@ -383,20 +382,20 @@
     slot_2 = near_hidden(grad_2)
     back_2 = send(jnp.concatenate([near[2], *slot_2], axis=1), lane_move({0: 2, 3: 1}))
     early = jnp.concatenate([out_grad, grad_a, grad_2], axis=0)
-    far_early = hidden(after(early, block_3), far_w)
-    grad_e, back_2, far_early = tie((grad_e, back_2, far_early))
+    far_v = hold(after(far_w, block_3), 16)
+    grad_e, back_2, far_v = tie((grad_e, back_2, far_v))
+    narrow = at_end & (jnp.max(grad_e[:16, :128].astype(F32)) < jnp.inf)
+    block_3, back_1, back_2, far_w, near, far, narrow = tie(
+        (block_3, back_1, back_2, far_w, near, far, narrow)
+    )
+    cross_w = send(far_w, flip(1))
+    far_2 = send(far[2], flip(2 << LANE_SHIFT))
+    far_1 = send(far[1], flip(1 << LANE_SHIFT))
     grad_3 = jnp.where(at_end, grad_e, grad_b)
     slot_3 = near_hidden(grad_3)
     grads = jnp.concatenate([early, grad_3], axis=0)
-    block_3, back_1, back_2, far_w, near, far, grad_3 = tie(
-        (block_3, back_1, back_2, far_w, near, far, grad_3)
-    )
-
-    cross_w = send(far_w, flip(1))
-    far_2 = send(far[2], flip(2 << LANE_SHIFT))
-    far_1 = send(far[1], flip(1 << LANE_SHIFT))
     blocks = list(zip(pair, slot_2, slot_3))
-    blocks += [(far_early, hidden(grad_3, far_w)), (hidden(grads, cross_w),)]
+    blocks += [(hidden(grads, far_v),), (hidden(grads, cross_w),)]
     low, high = slice(0, half), slice(half, 2 * half)
     extras = [(back, near[j], sides[j]) for j, back in ((1, back_1), (2, back_2))]
     part = features(
@@ -424,7 +423,7 @@
     everyone = [queries] + [send(queries, flip(q)) for q in range(1, QUADS)]
     if devices == LANES * QUADS and tokens == SEQ_LEN:
         where = position.astype(jnp.int32).reshape(1)
-        held = hold(after(stored, queries))
+        held = pltpu.with_memory_space_constraint(hold(after(stored, queries), 46), pltpu.VMEM)
         return scores(where, everyone, visible, held)
 
     examples_dev = tokens // SEQ_LEN

time: 128 us -> 127 us (level)
  waiting for transfers between devices: 24.1 us -> 45 us
  starting transfers between devices: 49 us -> 29.5 us
  other arithmetic: 5.04 us -> 1.53 us
  Pallas kernels: 8.65 us -> 11.7 us
  matrix products: 25.4 us -> 23 us
    ppermute x19, waiting for transfers between devices: 24.1 us -> 45 us  [send(): return lax.ppermute(value, 'row', pairs)]
    ppermute x19, starting transfers between devices: 49 us -> 29.5 us  [send(): return lax.ppermute(value, 'row', pairs)]
    dot_general x9 -> x8, matrix products: 24.9 us -> 22.6 us  [hidden(): lax.dot_general(grads, weight, (((1,), (1,)), ((), ())), preferred_elemen...]
    pallas_call x1 -> x2, Pallas kernels: 2.79 us -> 5.03 us  [hold(): call(hold_kernel, jax.ShapeDtypeStruct(value.shape, value.dtype), [pl.Blo...]
    concatenate x1 -> x0, other arithmetic: 1.98 us -> none  [shards(): early = jnp.concatenate([out_grad, grad_a, grad_2], axis=0)]
    unnamed x51 -> x49, local copies, waits for them, and re-layouts: 7.54 us -> 7.77 us
  transfers between devices with their start and end apart: 19 -> 19, of which waited for: 7 -> 7; matrix products, arithmetic and copies ran while one was open for 30% -> 27% of each run, Pallas kernels for 4% -> 6%
where the time goes in v5:
time: 127 us; the launch traced here: 126 us
  waiting for transfers between devices  45 us (35%)
  starting transfers between devices  29.5 us (23%)
  matrix products  23 us (18%)
  local copies, waits for them, and re-layouts  15.2 us (12%)
  Pallas kernels  11.7 us (9%)
  other arithmetic  1.53 us (1%)
    ppermute x19, waiting for transfers between devices, send(): return lax.ppermute(value, 'row', pairs)  45 us
    ppermute x19, starting transfers between devices, send(): return lax.ppermute(value, 'row', pairs)  29.5 us
    dot_general x8, matrix products, hidden(): lax.dot_general(grads, weight, (((1,), (1,)), ((), ())), preferred_elemen...  22.6 us
    unnamed x49, local copies, waits for them, and re-layouts  7.77 us
    pallas_call x2, Pallas kernels, hold(): call(hold_kernel, jax.ShapeDtypeStruct(value.shape, value.dtype), [pl.Blo...  5.03 us
    pallas_call x2, Pallas kernels, features(): call(functools.partial(feature_kernel, slots, layout, gates, len(extras),...  2.61 us
  transfers between devices with their start and end apart: 19, of which 7 were waited for; matrix products, arithmetic and copies ran while one was open for 27% of the time, Pallas kernels for 6%

profile of v5, /device:TPU:0, one launch (start us, length us, event | category | flops | bytes accessed | tf_op | source)
XLA Modules:
  0.0 126.4 jit_solution(12459263968738272296)
XLA Ops:
  0.5 2.6 %collective-permute-start = (bf16[128,4096]{1,0:T(8,128)(2,1)}, bf16[128,4096]{1,0:T(8,128)(2,1)}, u32[]{:S(2)}, u32[]{:S(2)}) collective-permute-start(bf16[128,4096]{1,0:T(8,128)(2,1)} %param.10), channel_id=1, source_target_pairs={{0,4},{1,5},{2,6},{3,7},{4,0},{5,1},{6,2},{7,3},{8,12},{9,13},{10,... | collective-permute-start | bytes 3145736 | tf_op jit(solution)/shard_map/ppermute | solution.py:312
  3.1 1.6 %collective-permute-start.3 = (bf16[128,4096]{1,0:T(8,128)(2,1)}, bf16[128,4096]{1,0:T(8,128)(2,1)}, u32[]{:S(2)}, u32[]{:S(2)}) collective-permute-start(bf16[128,4096]{1,0:T(8,128)(2,1)} %param.10), channel_id=1, source_target_pairs={{4,8},{5,9},{6,10},{7,11},{8,4},{9,5},{10,6},{11,7},{20,24},{21,25... | collective-permute-start | bytes 3145736 | tf_op jit(solution)/shard_map/ppermute | solution.py:312
  4.7 1.5 %collective-permute-start.7 = (bf16[448,4096]{1,0:T(8,128)(2,1)}, bf16[448,4096]{1,0:T(8,128)(2,1)}, u32[]{:S(2)}, u32[]{:S(2)}) collective-permute-start(bf16[448,4096]{1,0:T(8,128)(2,1)} %param.11), channel_id=1, source_target_pairs={{0,2},{1,3},{2,0},{3,1},{4,6},{5,7},{6,4},{7,5},{8,10},{9,11},{10,... | collective-permute-start | bytes 11010056 | tf_op jit(solution)/shard_map/ppermute | solution.py:312
  6.2 1.4 %reshape.16 = bf16[32,2,4096]{2,1,0:T(2,128)(2,1)S(1)} reshape(bf16[64,4096]{1,0:T(8,128)(2,1)} %bitcast.37) | data formatting | bytes 1048576 | tf_op jit(solution)/shard_map/reshape | solution.py:350
  7.9 2.4 %constant_dynamic-update-slice_fusion.1 = bf16[256,4096]{1,0:T(8,128)(2,1)} fusion(bf16[128,4096]{1,0:T(8,128)(2,1)} %param.10), kind=kLoop, calls=%fused_computation.14 | loop fusion | bytes 2097152
  12.1 1.5 %shard_map.82 = (bf16[128,896]{1,0:T(8,128)(2,1)S(1)}, bf16[128,896]{1,0:T(8,128)(2,1)S(1)}, bf16[128,896]{1,0:T(8,128)(2,1)S(1)}, bf16[128,896]{1,0:T(8,128)(2,...) custom-call(s32[3]{0:T(128)S(1)} %pad_add_fusion.where_ref, ...), custom_call_target="tpu_custom_call" | custom-call | bytes 5505024 | tf_op jit(solution)/shard_map/pallas_call | solution.py:66
  17.7 9.4 %collective-permute-done = bf16[128,4096]{1,0:T(8,128)(2,1)} collective-permute-done((bf16[128,4096]{1,0:T(8,128)(2,1)}, bf16[128,4096]{1,0:T(8,128)(2,1)}, u32[]{:S(2)}, u32[]{:S(2)}) %collective-permute-start) | collective-permute-done | bytes 1048608 | tf_op jit(solution)/shard_map/ppermute | solution.py:312
  27.2 1.7 %collective-permute-start.2 = (bf16[128,4096]{1,0:T(8,128)(2,1)}, bf16[128,4096]{1,0:T(8,128)(2,1)}, u32[]{:S(2)}, u32[]{:S(2)}) collective-permute-start(bf16[128,4096]{1,0:T(8,128)(2,1)} %collective-permute-done), channel_id=1, source_target_pairs={{4,8},{5,9},{6,10},{7,11},{8,4},{9,5},{10,6},{11,7},{20,24},{21,25... | collective-permute-start | bytes 3145736 | tf_op jit(solution)/shard_map/ppermute | solution.py:312
  30.1 2.3 %constant_dynamic-update-slice_fusion = bf16[256,4096]{1,0:T(8,128)(2,1)} fusion(bf16[256,4096]{1,0:T(8,128)(2,1)} %constant_dynamic-update-slice_fusion.1, bf16[128,4096]{1,0:T(8,128)(2,1)} %collective-permute-done), kind=kLoop, calls=%fused_computation.13 | loop fusion | bytes 2097152 | tf_op jit(solution)/shard_map/concatenate | solution.py:374
  32.4 3.0 %convolution_convert_fusion.3.refs_0_ = bf16[256,448]{1,0:T(8,128)(2,1)S(1)} fusion(bf16[256,4096]{1,0:T(8,128)(2,1)} %constant_dynamic-update-slice_fusion, bf16[448,4096]{1,0:T(8,128)(2,1)S(1)} %copy-done.17), kind=kOutput, calls=%fused_computation.4 | convolution fusion | flops 939638784 | bytes 5996544 | tf_op jit(solution)/shard_map/dot_general | solution.py:364
  35.4 3.4 %convolution_convert_fusion.2.refs_3_ = bf16[256,448]{1,0:T(8,128)(2,1)S(1)} fusion(bf16[256,4096]{1,0:T(8,128)(2,1)S(1)} %copy-done.22, bf16[448,4096]{1,0:T(8,128)(2,1)} %collective-permute-done.1), kind=kOutput, calls=%fused_computation.3 | convolution fusion | flops 939638784 | bytes 5996544 | tf_op jit(solution)/shard_map/dot_general | solution.py:364
  40.1 16.5 %collective-permute-done.4 = bf16[128,4096]{1,0:T(8,128)(2,1)S(1)} collective-permute-done((bf16[128,4096]{1,0:T(8,128)(2,1)}, bf16[128,4096]{1,0:T(8,128)(2,1)S(1)}, u32[]{:S(2)}, u32[]{:S(2)}) %collective-permute-start.4) | collective-permute-done | bytes 1048608 | tf_op jit(solution)/shard_map/ppermute | solution.py:312
  56.6 2.8 %collective-permute-start.8 = (bf16[144,1792]{1,0:T(8,128)(2,1)}, bf16[144,1792]{1,0:T(8,128)(2,1)S(1)}, u32[]{:S(2)}, u32[]{:S(2)}) collective-permute-start(bf16[144,1792]{1,0:T(8,128)(2,1)} %get-tuple-element.81), channel_id=1, source_target_pairs={{0,12},{1,13},{2,14},{3,15},{4,8},{5,9},{6,10},{7,11},{8,4},{9,5},... | collective-permute-start | bytes 1548296 | tf_op jit(solution)/shard_map/ppermute | solution.py:312
  60.8 3.3 %convolution_convert_fusion.6.refs_4_ = bf16[128,448]{1,0:T(8,128)(2,1)S(1)} fusion(bf16[128,4096]{1,0:T(8,128)(2,1)S(1)} %broadcast_select_fusion.1, bf16[448,4096]{1,0:T(8,128)(2,1)} %collective-permute-done.1), kind=kOutput, calls=%fused_computation.7 | convolution fusion | flops 469819392 | bytes 4833280 | tf_op jit(solution)/shard_map/dot_general | solution.py:364
  65.0 3.3 %collective-permute-start.6 = (bf16[128,1792]{1,0:T(8,128)(2,1)}, bf16[128,1792]{1,0:T(8,128)(2,1)S(1)}, u32[]{:S(2)}, u32[]{:S(2)}) collective-permute-start(bf16[128,1792]{1,0:T(8,128)(2,1)} %concatenate.13), channel_id=1, source_target_pairs={{0,8},{1,9},{2,10},{3,11},{12,4},{13,5},{14,6},{15,7},{16,24},{17,... | collective-permute-start | bytes 1376264 | tf_op jit(solution)/shard_map/ppermute | solution.py:312
  68.9 1.8 %concatenate.15 = bf16[128,1792]{1,0:T(8,128)(2,1)} concatenate(bf16[128,896]{1,0:T(8,128)(2,1)S(1)} %get-tuple-element.100.refs_14_, bf16[128,448]{1,0:T(8,128)(2,1)S(1)} %slice.9, bf16[128,448]{1,0:T(8,128)(2,1)} %slice.10), dimensions={1} | concatenate | bytes 917504 | tf_op jit(solution)/shard_map/concatenate | solution.py:376
  70.8 2.0 %collective-permute-start.9 = (bf16[128,1792]{1,0:T(8,128)(2,1)}, bf16[128,1792]{1,0:T(8,128)(2,1)S(1)}, u32[]{:S(2)}, u32[]{:S(2)}) collective-permute-start(bf16[128,1792]{1,0:T(8,128)(2,1)} %concatenate.15), channel_id=1, source_target_pairs={{0,4},{1,5},{2,6},{3,7},{12,8},{13,9},{14,10},{15,11},{16,20},{17,... | collective-permute-start | bytes 1376264 | tf_op jit(solution)/shard_map/ppermute | solution.py:312
  72.8 13.7 %collective-permute-done.7.source = bf16[448,4096]{1,0:T(8,128)(2,1)} collective-permute-done((bf16[448,4096]{1,0:T(8,128)(2,1)}, bf16[448,4096]{1,0:T(8,128)(2,1)}, u32[]{:S(2)}, u32[]{:S(2)}) %collective-permute-start.7) | collective-permute-done | bytes 3670048 | tf_op jit(solution)/shard_map/ppermute | solution.py:312
  86.5 2.2 %shard_map.83 = bf16[448,4096]{1,0:T(8,128)(2,1)S(1)} custom-call(bf16[448,4096]{1,0:T(8,128)(2,1)} %collective-permute-done.7.source), custom_call_target="tpu_custom_call" | custom-call | flops 1000 | bytes 1000 | tf_op jit(solution)/shard_map/pallas_call | solution.py:226
  88.7 1.9 %collective-permute-done.5 = bf16[128,4096]{1,0:T(8,128)(2,1)} collective-permute-done((bf16[128,4096]{1,0:T(8,128)(2,1)}, bf16[128,4096]{1,0:T(8,128)(2,1)}, u32[]{:S(2)}, u32[]{:S(2)}) %collective-permute-start.5) | collective-permute-done | bytes 1048608 | tf_op jit(solution)/shard_map/ppermute | solution.py:312
  90.6 3.5 %collective-permute-start.11 = (bf16[144,896]{1,0:T(8,128)(2,1)S(1)}, bf16[144,896]{1,0:T(8,128)(2,1)S(1)}, u32[]{:S(2)}, u32[]{:S(2)}) collective-permute-start(bf16[144,896]{1,0:T(8,128)(2,1)S(1)} %copy-done.16), channel_id=1, source_target_pairs={{0,4},{1,5},{2,6},{3,7},{4,0},{5,1},{6,2},{7,3},{8,12},{9,13},{10,... | collective-permute-start | bytes 774152 | tf_op jit(solution)/shard_map/ppermute | solution.py:312
  95.2 1.3 %broadcast_select_fusion = bf16[128,4096]{1,0:T(8,128)(2,1)S(1)} fusion(bf16[128,4096]{1,0:T(8,128)(2,1)} %collective-permute-done.5, bf16[128,4096]{1,0:T(8,128)(2,1)} %collective-permute-done.3, pred[]{:T(512)S(6)} %or.3), kind=kLoop, calls=%fused_computation.10 | loop fusion | flops 524288 | bytes 3145729 | tf_op jit(solution)/shard_map/jit(_where)/select_n | solution.py:394
  97.8 3.3 %convolution_convert_fusion.4.refs_5_ = bf16[128,448]{1,0:T(8,128)(2,1)S(1)} fusion(bf16[128,4096]{1,0:T(8,128)(2,1)S(1)} %broadcast_select_fusion, bf16[448,4096]{1,0:T(8,128)(2,1)} %collective-permute-done.1), kind=kOutput, calls=%fused_computation.5 | convolution fusion | flops 469819392 | bytes 4833280 | tf_op jit(solution)/shard_map/dot_general | solution.py:364
  101.1 3.6 %convolution_convert_fusion.1.refs_6_ = bf16[512,448]{1,0:T(8,128)(2,1)S(1)} fusion(bf16[448,4096]{1,0:T(8,128)(2,1)S(1)} %shard_map.83, bf16[128,4096]{1,0:T(8,128)(2,1)S(1)} %broadcast_select_fusion, bf16[128,4096]{1,0:T(8,128)(2,1)S(1)} %copy-done.20, bf16[128,4096]{1,0:T(8,128)(2,1)} %collective-permute-done, bf16[128,4096]{1,0:T(8,128)(2,1)S(1)} %copy-done.21), kind=kOutput, calls=%fused_computation.2 | convolution fusion | flops 1896054784 | bytes 8323072 | tf_op jit(solution)/shard_map/dot_general | solution.py:364
  104.7 3.7 %convolution_convert_fusion.refs_7_ = bf16[512,448]{1,0:T(8,128)(2,1)S(1)} fusion(bf16[448,4096]{1,0:T(8,128)(2,1)S(1)} %collective-permute-done.10, bf16[128,4096]{1,0:T(8,128)(2,1)S(1)} %broadcast_select_fusion, bf16[128,4096]{1,0:T(8,128)(2,1)S(1)} %copy-done.20, bf16[128,4096]{1,0:T(8,128)(2,1)} %collective-permute-done, bf16[128,4096]{1,0:T(8,128)(2,1)S(1)} %copy-done.21), kind=kOutput, calls=%fused_computation.1 | convolution fusion | flops 1896054784 | bytes 8323072 | tf_op jit(solution)/shard_map/dot_general | solution.py:364
  108.5 1.4 %shard_map.84.refs_14_ = bf16[4,1,32,128]{3,2,1,0:T(8,128)(2,1)S(1)} custom-call(bf16[256,448]{1,0:T(8,128)(2,1)S(1)} %convolution_convert_fusion.3.refs_0_, bf16[128,448]{1,0:T(8,128)(2,1)S(1)} %convolution_convert_fusion.7.refs_1_, bf16[128,448]{1,0:T(8,128)(2,1)S(1)} %convolution_convert_fusion.5.refs_2_, ...), custom_call_target="tpu_custom_call" | custom-call | flops 1000 | bytes 1000 | tf_op jit(solution)/shard_map/pallas_call | solution.py:209
  111.1 2.0 %collective-permute-start.13 = (bf16[4,1,32,128]{3,2,1,0:T(8,128)(2,1)S(1)}, bf16[4,1,32,128]{3,2,1,0:T(8,128)(2,1)S(1)}, u32[]{:S(2)}, u32[]{:S(2)}) collective-permute-start(bf16[4,1,32,128]{3,2,1,0:T(8,128)(2,1)S(1)} %shard_map.85.own), channel_id=1, source_target_pairs={{0,4},{1,5},{2,6},{3,7},{4,0},{5,1},{6,2},{7,3},{8,12},{9,13},{10,... | collective-permute-start | bytes 98312 | tf_op jit(solution)/shard_map/ppermute | solution.py:312
  113.1 2.4 %collective-permute-start.15 = (bf16[4,1,32,128]{3,2,1,0:T(8,128)(2,1)S(1)}, bf16[4,1,32,128]{3,2,1,0:T(8,128)(2,1)S(1)}, u32[]{:S(2)}, u32[]{:S(2)}) collective-permute-start(bf16[4,1,32,128]{3,2,1,0:T(8,128)(2,1)S(1)} %shard_map.85.own), channel_id=1, source_target_pairs={{0,12},{1,13},{2,14},{3,15},{4,8},{5,9},{6,10},{7,11},{8,4},{9,5},... | collective-permute-start | bytes 98312 | tf_op jit(solution)/shard_map/ppermute | solution.py:312
  115.5 2.6 %collective-permute-done.14.refs_1_ = bf16[4,1,32,128]{3,2,1,0:T(8,128)(2,1)S(1)} collective-permute-done((bf16[4,1,32,128]{3,2,1,0:T(8,128)(2,1)S(1)}, bf16[4,1,32,128]{3,2,1,0:T(8,128)(2,1)S(1)}, u32[]{:S(2)}, u32[]{:S(2)}) %collective-permute-start.14) | collective-permute-done | bytes 32800 | tf_op jit(solution)/shard_map/ppermute | solution.py:312
  119.1 1.5 %collective-permute-start.17 = (bf16[4,1,32,128]{3,2,1,0:T(8,128)(2,1)S(1)}, bf16[4,1,32,128]{3,2,1,0:T(8,128)(2,1)S(1)}, u32[]{:S(2)}, u32[]{:S(2)}) collective-permute-start(bf16[4,1,32,128]{3,2,1,0:T(8,128)(2,1)S(1)} %shard_map.86.q0), channel_id=1, source_target_pairs={{0,2},{1,3},{2,0},{3,1},{4,6},{5,7},{6,4},{7,5},{8,10},{9,11},{10,... | collective-permute-start | bytes 98312 | tf_op jit(solution)/shard_map/ppermute | solution.py:312
  121.0 2.8 %shard_map.87.stored_ref = bf16[768,4096]{1,0:T(8,128)(2,1)S(1)} custom-call(bf16[768,4096]{1,0:T(8,128)(2,1)} %source), custom_call_target="tpu_custom_call" | custom-call | flops 1000 | bytes 1000 | tf_op jit(solution)/shard_map/pallas_call | solution.py:226
  124.0 2.4 %shard_map.88 = f32[16,768]{1,0:T(8,128)} custom-call(s32[1]{0:T(128)} %bitcast.where_ref, bf16[4,1,32,128]{3,2,1,0:T(8,128)(2,1)S(1)} %shard_map.86.q0, bf16[4,1,32,128]{3,2,1,0:T(8,128)(2,1)S(1)} %collective-permute-done.16.q1, bf16[4,1,32,128]{3,2,1,0:T(8,128)(2,1)S(1)} %collective-permute-done.17.q2, ...), custom_call_target="tpu_custom_call" | custom-call | flops 1000 | bytes 1000 | tf_op jit(solution)/shard_map/pallas_call | solution.py:288
  (83 shorter events, 17.1 us)
Async XLA Ops:
  0.0 10.3 %copy-start = (bf16[128,4096]{1,0:T(8,128)(2,1)S(1)}, bf16[128,4096]{1,0:T(8,128)(2,1)}, u32[]{:S(2)}) copy-start(bf16[128,4096]{1,0:T(8,128)(2,1)} %param.8) | copy-start | bytes 3145732
  0.0 10.9 %copy-start.1 = (bf16[128,7168]{1,0:T(8,128)(2,1)S(1)}, bf16[128,7168]{1,0:T(8,128)(2,1)}, u32[]{:S(2)}) copy-start(bf16[128,7168]{1,0:T(8,128)(2,1)} %gate_ref.1) | copy-start | bytes 5505028
  0.0 27.2 %collective-permute-start.1 = (bf16[448,4096]{1,0:T(8,128)(2,1)}, bf16[448,4096]{1,0:T(8,128)(2,1)}, u32[]{:S(2)}, u32[]{:S(2)}) collective-permute-start(bf16[448,4096]{1,0:T(8,128)(2,1)} %param.11), channel_id=1, source_target_pairs={{0,1},{1,0},{2,3},{3,2},{4,5},{5,4},{6,7},{7,6},{8,9},{9,8},{10,11... | collective-permute-start | bytes 11010056 | tf_op jit(solution)/shard_map/ppermute | solution.py:312
  0.5 26.7 %collective-permute-start = (bf16[128,4096]{1,0:T(8,128)(2,1)}, bf16[128,4096]{1,0:T(8,128)(2,1)}, u32[]{:S(2)}, u32[]{:S(2)}) collective-permute-start(bf16[128,4096]{1,0:T(8,128)(2,1)} %param.10), channel_id=1, source_target_pairs={{0,4},{1,5},{2,6},{3,7},{4,0},{5,1},{6,2},{7,3},{8,12},{9,13},{10,... | collective-permute-start | bytes 3145736 | tf_op jit(solution)/shard_map/ppermute | solution.py:312
  3.1 25.7 %collective-permute-start.3 = (bf16[128,4096]{1,0:T(8,128)(2,1)}, bf16[128,4096]{1,0:T(8,128)(2,1)}, u32[]{:S(2)}, u32[]{:S(2)}) collective-permute-start(bf16[128,4096]{1,0:T(8,128)(2,1)} %param.10), channel_id=1, source_target_pairs={{4,8},{5,9},{6,10},{7,11},{8,4},{9,5},{10,6},{11,7},{20,24},{21,25... | collective-permute-start | bytes 3145736 | tf_op jit(solution)/shard_map/ppermute | solution.py:312
  4.7 81.7 %collective-permute-start.7 = (bf16[448,4096]{1,0:T(8,128)(2,1)}, bf16[448,4096]{1,0:T(8,128)(2,1)}, u32[]{:S(2)}, u32[]{:S(2)}) collective-permute-start(bf16[448,4096]{1,0:T(8,128)(2,1)} %param.11), channel_id=1, source_target_pairs={{0,2},{1,3},{2,0},{3,1},{4,6},{5,7},{6,4},{7,5},{8,10},{9,11},{10,... | collective-permute-start | bytes 11010056 | tf_op jit(solution)/shard_map/ppermute | solution.py:312
  12.1 20.4 %copy-start.17 = (bf16[448,4096]{1,0:T(8,128)(2,1)S(1)}, bf16[448,4096]{1,0:T(8,128)(2,1)}, u32[]{:S(2)}) copy-start(bf16[448,4096]{1,0:T(8,128)(2,1)} %param.11) | copy-start | bytes 11010052
  27.2 11.6 %collective-permute-start.2 = (bf16[128,4096]{1,0:T(8,128)(2,1)}, bf16[128,4096]{1,0:T(8,128)(2,1)}, u32[]{:S(2)}, u32[]{:S(2)}) collective-permute-start(bf16[128,4096]{1,0:T(8,128)(2,1)} %collective-permute-done), channel_id=1, source_target_pairs={{4,8},{5,9},{6,10},{7,11},{8,4},{9,5},{10,6},{11,7},{20,24},{21,25... | collective-permute-start | bytes 3145736 | tf_op jit(solution)/shard_map/ppermute | solution.py:312
  28.8 27.8 %collective-permute-start.4 = (bf16[128,4096]{1,0:T(8,128)(2,1)}, bf16[128,4096]{1,0:T(8,128)(2,1)S(1)}, u32[]{:S(2)}, u32[]{:S(2)}) collective-permute-start(bf16[128,4096]{1,0:T(8,128)(2,1)} %collective-permute-done.3), channel_id=1, source_target_pairs={{4,0},{5,1},{6,2},{7,3},{8,12},{9,13},{10,14},{11,15},{20,16},{21,... | collective-permute-start | bytes 3145736 | tf_op jit(solution)/shard_map/ppermute | solution.py:312
  38.8 51.8 %collective-permute-start.5 = (bf16[128,4096]{1,0:T(8,128)(2,1)}, bf16[128,4096]{1,0:T(8,128)(2,1)}, u32[]{:S(2)}, u32[]{:S(2)}) collective-permute-start(bf16[128,4096]{1,0:T(8,128)(2,1)} %collective-permute-done.2), channel_id=1, source_target_pairs={{4,0},{5,1},{6,2},{7,3},{8,12},{9,13},{10,14},{11,15},{20,16},{21,... | collective-permute-start | bytes 3145736 | tf_op jit(solution)/shard_map/ppermute | solution.py:312
  56.6 29.8 %collective-permute-start.8 = (bf16[144,1792]{1,0:T(8,128)(2,1)}, bf16[144,1792]{1,0:T(8,128)(2,1)S(1)}, u32[]{:S(2)}, u32[]{:S(2)}) collective-permute-start(bf16[144,1792]{1,0:T(8,128)(2,1)} %get-tuple-element.81), channel_id=1, source_target_pairs={{0,12},{1,13},{2,14},{3,15},{4,8},{5,9},{6,10},{7,11},{8,4},{9,5},... | collective-permute-start | bytes 1548296 | tf_op jit(solution)/shard_map/ppermute | solution.py:312
  65.0 23.7 %collective-permute-start.6 = (bf16[128,1792]{1,0:T(8,128)(2,1)}, bf16[128,1792]{1,0:T(8,128)(2,1)S(1)}, u32[]{:S(2)}, u32[]{:S(2)}) collective-permute-start(bf16[128,1792]{1,0:T(8,128)(2,1)} %concatenate.13), channel_id=1, source_target_pairs={{0,8},{1,9},{2,10},{3,11},{12,4},{13,5},{14,6},{15,7},{16,24},{17,... | collective-permute-start | bytes 1376264 | tf_op jit(solution)/shard_map/ppermute | solution.py:312
  70.8 19.8 %copy-start.16 = (bf16[144,896]{1,0:T(8,128)(2,1)S(1)}, bf16[144,896]{1,0:T(8,128)(2,1)}, u32[]{:S(2)}) copy-start(bf16[144,896]{1,0:T(8,128)(2,1)} %copy-done.15) | copy-start | bytes 774148
  70.8 23.3 %copy-start.14 = (bf16[144,896]{1,0:T(8,128)(2,1)S(1)}, bf16[144,896]{1,0:T(8,128)(2,1)}, u32[]{:S(2)}) copy-start(bf16[144,896]{1,0:T(8,128)(2,1)} %copy-done.13) | copy-start | bytes 774148
  70.8 25.7 %copy-start.18 = (bf16[448,4096]{1,0:T(8,128)(2,1)S(1)}, bf16[448,4096]{1,0:T(8,128)(2,1)}, u32[]{:S(2)}) copy-start(bf16[448,4096]{1,0:T(8,128)(2,1)} %param.11) | copy-start | bytes 11010052
  70.8 19.8 %collective-permute-start.9 = (bf16[128,1792]{1,0:T(8,128)(2,1)}, bf16[128,1792]{1,0:T(8,128)(2,1)S(1)}, u32[]{:S(2)}, u32[]{:S(2)}) collective-permute-start(bf16[128,1792]{1,0:T(8,128)(2,1)} %concatenate.15), channel_id=1, source_target_pairs={{0,4},{1,5},{2,6},{3,7},{12,8},{13,9},{14,10},{15,11},{16,20},{17,... | collective-permute-start | bytes 1376264 | tf_op jit(solution)/shard_map/ppermute | solution.py:312
  90.6 14.1 %collective-permute-start.10 = (bf16[448,4096]{1,0:T(8,128)(2,1)}, bf16[448,4096]{1,0:T(8,128)(2,1)S(1)}, u32[]{:S(2)}, u32[]{:S(2)}) collective-permute-start(bf16[448,4096]{1,0:T(8,128)(2,1)} %collective-permute-done.7.source), channel_id=1, source_target_pairs={{0,1},{1,0},{2,3},{3,2},{4,5},{5,4},{6,7},{7,6},{8,9},{9,8},{10,11... | collective-permute-start | bytes 11010056 | tf_op jit(solution)/shard_map/ppermute | solution.py:312
  90.6 19.3 %collective-permute-start.11 = (bf16[144,896]{1,0:T(8,128)(2,1)S(1)}, bf16[144,896]{1,0:T(8,128)(2,1)S(1)}, u32[]{:S(2)}, u32[]{:S(2)}) collective-permute-start(bf16[144,896]{1,0:T(8,128)(2,1)S(1)} %copy-done.16), channel_id=1, source_target_pairs={{0,4},{1,5},{2,6},{3,7},{4,0},{5,1},{6,2},{7,3},{8,12},{9,13},{10,... | collective-permute-start | bytes 774152 | tf_op jit(solution)/shard_map/ppermute | solution.py:312
  94.1 15.8 %collective-permute-start.12 = (bf16[144,896]{1,0:T(8,128)(2,1)S(1)}, bf16[144,896]{1,0:T(8,128)(2,1)S(1)}, u32[]{:S(2)}, u32[]{:S(2)}) collective-permute-start(bf16[144,896]{1,0:T(8,128)(2,1)S(1)} %copy-done.14), channel_id=1, source_target_pairs={{0,8},{1,9},{2,10},{3,11},{4,12},{5,13},{6,14},{7,15},{8,0},{9,1},... | collective-permute-start | bytes 774152 | tf_op jit(solution)/shard_map/ppermute | solution.py:312
  96.5 4.5 %copy-start.20 = (bf16[128,4096]{1,0:T(8,128)(2,1)S(1)}, bf16[128,4096]{1,0:T(8,128)(2,1)}, u32[]{:S(2)}) copy-start(bf16[128,4096]{1,0:T(8,128)(2,1)} %copy-done.19) | copy-start | bytes 3145732
  96.5 4.5 %copy-start.21 = (bf16[128,4096]{1,0:T(8,128)(2,1)S(1)}, bf16[128,4096]{1,0:T(8,128)(2,1)}, u32[]{:S(2)}) copy-start(bf16[128,4096]{1,0:T(8,128)(2,1)} %param.10) | copy-start | bytes 3145732
  104.7 3.7 %copy-start.4 = (bf16[64,1792]{1,0:T(8,128)(2,1)S(1)}, bf16[64,1792]{1,0:T(8,128)(2,1)}, u32[]{:S(2)}) copy-start(bf16[64,1792]{1,0:T(8,128)(2,1)} %copy-done.3) | copy-start | bytes 688132
  104.7 3.7 %copy-start.6 = (bf16[144,1792]{1,0:T(8,128)(2,1)S(1)}, bf16[144,1792]{1,0:T(8,128)(2,1)}, u32[]{:S(2)}) copy-start(bf16[144,1792]{1,0:T(8,128)(2,1)} %copy-done.5) | copy-start | bytes 1548292
  104.7 3.7 %copy-start.8 = (bf16[128,896]{1,0:T(8,128)(2,1)S(1)}, bf16[128,896]{1,0:T(8,128)(2,1)}, u32[]{:S(2)}) copy-start(bf16[128,896]{1,0:T(8,128)(2,1)} %copy-done.7) | copy-start | bytes 688132
  104.7 3.7 %copy-start.10 = (bf16[128,896]{1,0:T(8,128)(2,1)S(1)}, bf16[128,896]{1,0:T(8,128)(2,1)}, u32[]{:S(2)}) copy-start(bf16[128,896]{1,0:T(8,128)(2,1)} %copy-done.9) | copy-start | bytes 688132
  108.4 12.5 %copy-start.23 = (s32[16]{0:T(128)S(1)}, s32[16]{0:T(128)}, u32[]{:S(2)}) copy-start(s32[16]{0:T(128)} %param.15) | copy-start | bytes 196
  111.1 4.5 %collective-permute-start.13 = (bf16[4,1,32,128]{3,2,1,0:T(8,128)(2,1)S(1)}, bf16[4,1,32,128]{3,2,1,0:T(8,128)(2,1)S(1)}, u32[]{:S(2)}, u32[]{:S(2)}) collective-permute-start(bf16[4,1,32,128]{3,2,1,0:T(8,128)(2,1)S(1)} %shard_map.85.own), channel_id=1, source_target_pairs={{0,4},{1,5},{2,6},{3,7},{4,0},{5,1},{6,2},{7,3},{8,12},{9,13},{10,... | collective-permute-start | bytes 98312 | tf_op jit(solution)/shard_map/ppermute | solution.py:312
  113.1 5.1 %collective-permute-start.14 = (bf16[4,1,32,128]{3,2,1,0:T(8,128)(2,1)S(1)}, bf16[4,1,32,128]{3,2,1,0:T(8,128)(2,1)S(1)}, u32[]{:S(2)}, u32[]{:S(2)}) collective-permute-start(bf16[4,1,32,128]{3,2,1,0:T(8,128)(2,1)S(1)} %shard_map.85.own), channel_id=1, source_target_pairs={{0,8},{1,9},{2,10},{3,11},{4,12},{5,13},{6,14},{7,15},{8,0},{9,1},... | collective-permute-start | bytes 98312 | tf_op jit(solution)/shard_map/ppermute | solution.py:312
  113.1 5.7 %collective-permute-start.15 = (bf16[4,1,32,128]{3,2,1,0:T(8,128)(2,1)S(1)}, bf16[4,1,32,128]{3,2,1,0:T(8,128)(2,1)S(1)}, u32[]{:S(2)}, u32[]{:S(2)}) collective-permute-start(bf16[4,1,32,128]{3,2,1,0:T(8,128)(2,1)S(1)} %shard_map.85.own), channel_id=1, source_target_pairs={{0,12},{1,13},{2,14},{3,15},{4,8},{5,9},{6,10},{7,11},{8,4},{9,5},... | collective-permute-start | bytes 98312 | tf_op jit(solution)/shard_map/ppermute | solution.py:312
  119.0 4.8 %collective-permute-start.16 = (bf16[4,1,32,128]{3,2,1,0:T(8,128)(2,1)S(1)}, bf16[4,1,32,128]{3,2,1,0:T(8,128)(2,1)S(1)}, u32[]{:S(2)}, u32[]{:S(2)}) collective-permute-start(bf16[4,1,32,128]{3,2,1,0:T(8,128)(2,1)S(1)} %shard_map.86.q0), channel_id=1, source_target_pairs={{0,1},{1,0},{2,3},{3,2},{4,5},{5,4},{6,7},{7,6},{8,9},{9,8},{10,11... | collective-permute-start | bytes 98312 | tf_op jit(solution)/shard_map/ppermute | solution.py:312
  119.1 4.8 %collective-permute-start.17 = (bf16[4,1,32,128]{3,2,1,0:T(8,128)(2,1)S(1)}, bf16[4,1,32,128]{3,2,1,0:T(8,128)(2,1)S(1)}, u32[]{:S(2)}, u32[]{:S(2)}) collective-permute-start(bf16[4,1,32,128]{3,2,1,0:T(8,128)(2,1)S(1)} %shard_map.86.q0), channel_id=1, source_target_pairs={{0,2},{1,3},{2,0},{3,1},{4,6},{5,7},{6,4},{7,5},{8,10},{9,11},{10,... | collective-permute-start | bytes 98312 | tf_op jit(solution)/shard_map/ppermute | solution.py:312
  120.6 3.3 %collective-permute-start.18 = (bf16[4,1,32,128]{3,2,1,0:T(8,128)(2,1)S(1)}, bf16[4,1,32,128]{3,2,1,0:T(8,128)(2,1)S(1)}, u32[]{:S(2)}, u32[]{:S(2)}) collective-permute-start(bf16[4,1,32,128]{3,2,1,0:T(8,128)(2,1)S(1)} %shard_map.86.q0), channel_id=1, source_target_pairs={{0,3},{1,2},{2,1},{3,0},{4,7},{5,6},{6,5},{7,4},{8,11},{9,10},{10,... | collective-permute-start | bytes 98312 | tf_op jit(solution)/shard_map/ppermute | solution.py:312
  (11 other events, 15.5 us)

commit v6 on v5

--- a/solution.py
+++ b/solution.py
@@ -398,25 +398,28 @@
     blocks += [(hidden(grads, far_v),), (hidden(grads, cross_w),)]
     low, high = slice(0, half), slice(half, 2 * half)
     extras = [(back, near[j], sides[j]) for j, back in ((1, back_1), (2, back_2))]
-    part = features(
-        (0, 3),
+    far_1, far_2, blocks = tie((far_1, far_2, blocks))
+    own = features(
+        (0, 1, 2, 3),
         blocks,
-        {"near": near[0], "far": far[0], "block": block_3, "in": in_proj},
-        {0: (("near", low), ("far", low)), 3: (("block", low), ("block", high))},
+        {
+            "near": near[0],
+            "far": far[0],
+            ("far", 1): far_1,
+            ("far", 2): far_2,
+            "back1": back_1,
+            "back2": back_2,
+            "block": block_3,
+            "in": in_proj,
+        },
+        {
+            0: (("near", low), ("far", low)),
+            1: (("back1", low), (("far", 1), low)),
+            2: (("back2", low), (("far", 2), low)),
+            3: (("block", low), ("block", high)),
+        },
         sides[0],
         extras,
-    )
-    far_1, far_2, part = tie((far_1, far_2, part))
-    own = features(
-        (1, 2),
-        blocks,
-        {("far", 1): far_1, ("far", 2): far_2, "back1": back_1, "back2": back_2, "in": in_proj},
-        {
-            1: (("back1", low), (("far", 1), low)),
-            2: (("back2", low), (("far", 2), low)),
-        },
-        sides[0],
-        before=part,
     )
     queries = scaled(own, [send(own, flip(k << LANE_SHIFT)) for k in range(1, LANES)])
     quad = position & QUADS - 1

time: 127 us -> 129 us (1.016)
  starting transfers between devices: 29.5 us -> 31.7 us
    ppermute x19, starting transfers between devices: 29.5 us -> 31.7 us  [send(): return lax.ppermute(value, 'row', pairs)]
    pallas_call x2 -> x1, Pallas kernels: 2.61 us -> 2.17 us  [features(): call(functools.partial(feature_kernel, slots, layout, gates, len(extras),...]
  transfers between devices with their start and end apart: 19 -> 19, of which waited for: 7 -> 7; matrix products, arithmetic and copies ran while one was open for 27% -> 27% of each run, Pallas kernels for 6% -> 5%
where the time goes in v6:
time: 129 us; the launch traced here: 128 us
  waiting for transfers between devices  44.1 us (34%)
  starting transfers between devices  31.7 us (25%)
  matrix products  23.1 us (18%)
  local copies, waits for them, and re-layouts  15.9 us (12%)
  Pallas kernels  11.2 us (9%)
  other arithmetic  1.54 us (1%)
    ppermute x19, waiting for transfers between devices, send(): return lax.ppermute(value, 'row', pairs)  44.1 us
    ppermute x19, starting transfers between devices, send(): return lax.ppermute(value, 'row', pairs)  31.7 us
    dot_general x8, matrix products, hidden(): lax.dot_general(grads, weight, (((1,), (1,)), ((), ())), preferred_elemen...  22.6 us
    unnamed x49, local copies, waits for them, and re-layouts  7.76 us
    pallas_call x2, Pallas kernels, hold(): call(hold_kernel, jax.ShapeDtypeStruct(value.shape, value.dtype), [pl.Blo...  5.03 us
  transfers between devices with their start and end apart: 19, of which 7 were waited for; matrix products, arithmetic and copies ran while one was open for 27% of the time, Pallas kernels for 5%

profile of v6, /device:TPU:0, one launch (start us, length us, event | category | flops | bytes accessed | tf_op | source)
XLA Modules:
  0.0 127.9 jit_solution(13448152875123098402)
XLA Ops:
  0.5 2.6 %collective-permute-start = (bf16[128,4096]{1,0:T(8,128)(2,1)}, bf16[128,4096]{1,0:T(8,128)(2,1)}, u32[]{:S(2)}, u32[]{:S(2)}) collective-permute-start(bf16[128,4096]{1,0:T(8,128)(2,1)} %param.10), channel_id=1, source_target_pairs={{0,4},{1,5},{2,6},{3,7},{4,0},{5,1},{6,2},{7,3},{8,12},{9,13},{10,... | collective-permute-start | bytes 3145736 | tf_op jit(solution)/shard_map/ppermute | solution.py:312
  3.1 1.6 %collective-permute-start.3 = (bf16[128,4096]{1,0:T(8,128)(2,1)}, bf16[128,4096]{1,0:T(8,128)(2,1)}, u32[]{:S(2)}, u32[]{:S(2)}) collective-permute-start(bf16[128,4096]{1,0:T(8,128)(2,1)} %param.10), channel_id=1, source_target_pairs={{4,8},{5,9},{6,10},{7,11},{8,4},{9,5},{10,6},{11,7},{20,24},{21,25... | collective-permute-start | bytes 3145736 | tf_op jit(solution)/shard_map/ppermute | solution.py:312
  4.7 1.5 %collective-permute-start.9 = (bf16[448,4096]{1,0:T(8,128)(2,1)}, bf16[448,4096]{1,0:T(8,128)(2,1)}, u32[]{:S(2)}, u32[]{:S(2)}) collective-permute-start(bf16[448,4096]{1,0:T(8,128)(2,1)} %param.11), channel_id=1, source_target_pairs={{0,2},{1,3},{2,0},{3,1},{4,6},{5,7},{6,4},{7,5},{8,10},{9,11},{10,... | collective-permute-start | bytes 11010056 | tf_op jit(solution)/shard_map/ppermute | solution.py:312
  6.2 1.4 %reshape.16 = bf16[32,2,4096]{2,1,0:T(2,128)(2,1)S(1)} reshape(bf16[64,4096]{1,0:T(8,128)(2,1)} %bitcast.37) | data formatting | bytes 1048576 | tf_op jit(solution)/shard_map/reshape | solution.py:350
  7.9 2.4 %constant_dynamic-update-slice_fusion.1 = bf16[256,4096]{1,0:T(8,128)(2,1)} fusion(bf16[128,4096]{1,0:T(8,128)(2,1)} %param.10), kind=kLoop, calls=%fused_computation.14 | loop fusion | bytes 2097152
  12.1 1.5 %shard_map.82 = (bf16[128,896]{1,0:T(8,128)(2,1)S(1)}, bf16[128,896]{1,0:T(8,128)(2,1)S(1)}, bf16[128,896]{1,0:T(8,128)(2,1)S(1)}, bf16[128,896]{1,0:T(8,128)(2,...) custom-call(s32[3]{0:T(128)S(1)} %pad_add_fusion.where_ref, ...), custom_call_target="tpu_custom_call" | custom-call | bytes 5505024 | tf_op jit(solution)/shard_map/pallas_call | solution.py:66
  17.7 9.4 %collective-permute-done = bf16[128,4096]{1,0:T(8,128)(2,1)} collective-permute-done((bf16[128,4096]{1,0:T(8,128)(2,1)}, bf16[128,4096]{1,0:T(8,128)(2,1)}, u32[]{:S(2)}, u32[]{:S(2)}) %collective-permute-start) | collective-permute-done | bytes 1048608 | tf_op jit(solution)/shard_map/ppermute | solution.py:312
  27.2 1.7 %collective-permute-start.2 = (bf16[128,4096]{1,0:T(8,128)(2,1)}, bf16[128,4096]{1,0:T(8,128)(2,1)}, u32[]{:S(2)}, u32[]{:S(2)}) collective-permute-start(bf16[128,4096]{1,0:T(8,128)(2,1)} %collective-permute-done), channel_id=1, source_target_pairs={{4,8},{5,9},{6,10},{7,11},{8,4},{9,5},{10,6},{11,7},{20,24},{21,25... | collective-permute-start | bytes 3145736 | tf_op jit(solution)/shard_map/ppermute | solution.py:312
  30.1 2.3 %constant_dynamic-update-slice_fusion = bf16[256,4096]{1,0:T(8,128)(2,1)} fusion(bf16[256,4096]{1,0:T(8,128)(2,1)} %constant_dynamic-update-slice_fusion.1, bf16[128,4096]{1,0:T(8,128)(2,1)} %collective-permute-done), kind=kLoop, calls=%fused_computation.13 | loop fusion | bytes 2097152 | tf_op jit(solution)/shard_map/concatenate | solution.py:374
  32.4 3.0 %convolution_convert_fusion.3.refs_0_ = bf16[256,448]{1,0:T(8,128)(2,1)S(1)} fusion(bf16[256,4096]{1,0:T(8,128)(2,1)} %constant_dynamic-update-slice_fusion, bf16[448,4096]{1,0:T(8,128)(2,1)S(1)} %copy-done.17), kind=kOutput, calls=%fused_computation.4 | convolution fusion | flops 939638784 | bytes 5996544 | tf_op jit(solution)/shard_map/dot_general | solution.py:364
  35.4 3.4 %convolution_convert_fusion.2.refs_3_ = bf16[256,448]{1,0:T(8,128)(2,1)S(1)} fusion(bf16[256,4096]{1,0:T(8,128)(2,1)S(1)} %copy-done.22, bf16[448,4096]{1,0:T(8,128)(2,1)} %collective-permute-done.1), kind=kOutput, calls=%fused_computation.3 | convolution fusion | flops 939638784 | bytes 5996544 | tf_op jit(solution)/shard_map/dot_general | solution.py:364
  38.8 17.8 %collective-permute-done.4 = bf16[128,4096]{1,0:T(8,128)(2,1)S(1)} collective-permute-done((bf16[128,4096]{1,0:T(8,128)(2,1)}, bf16[128,4096]{1,0:T(8,128)(2,1)S(1)}, u32[]{:S(2)}, u32[]{:S(2)}) %collective-permute-start.4) | collective-permute-done | bytes 1048608 | tf_op jit(solution)/shard_map/ppermute | solution.py:312
  56.6 2.8 %collective-permute-start.5 = (bf16[144,1792]{1,0:T(8,128)(2,1)}, bf16[144,1792]{1,0:T(8,128)(2,1)S(1)}, u32[]{:S(2)}, u32[]{:S(2)}) collective-permute-start(bf16[144,1792]{1,0:T(8,128)(2,1)} %get-tuple-element.85), channel_id=1, source_target_pairs={{0,12},{1,13},{2,14},{3,15},{4,8},{5,9},{6,10},{7,11},{8,4},{9,5},... | collective-permute-start | bytes 1548296 | tf_op jit(solution)/shard_map/ppermute | solution.py:312
  62.1 3.3 %convolution_convert_fusion.6.refs_4_ = bf16[128,448]{1,0:T(8,128)(2,1)S(1)} fusion(bf16[128,4096]{1,0:T(8,128)(2,1)S(1)} %broadcast_select_fusion.1, bf16[448,4096]{1,0:T(8,128)(2,1)} %collective-permute-done.1), kind=kOutput, calls=%fused_computation.7 | convolution fusion | flops 469819392 | bytes 4833280 | tf_op jit(solution)/shard_map/dot_general | solution.py:364
  66.3 6.3 %collective-permute-start.8 = (bf16[128,1792]{1,0:T(8,128)(2,1)}, bf16[128,1792]{1,0:T(8,128)(2,1)S(1)}, u32[]{:S(2)}, u32[]{:S(2)}) collective-permute-start(bf16[128,1792]{1,0:T(8,128)(2,1)} %concatenate.14), channel_id=1, source_target_pairs={{0,8},{1,9},{2,10},{3,11},{12,4},{13,5},{14,6},{15,7},{16,24},{17,... | collective-permute-start | bytes 1376264 | tf_op jit(solution)/shard_map/ppermute | solution.py:312
  73.9 1.9 %concatenate.13 = bf16[128,1792]{1,0:T(8,128)(2,1)} concatenate(bf16[128,896]{1,0:T(8,128)(2,1)S(1)} %get-tuple-element.118.refs_18_, bf16[128,448]{1,0:T(8,128)(2,1)} %slice.9, bf16[128,448]{1,0:T(8,128)(2,1)} %slice.10), dimensions={1} | concatenate | bytes 917504 | tf_op jit(solution)/shard_map/concatenate | solution.py:376
  75.8 2.3 %collective-permute-start.6 = (bf16[128,1792]{1,0:T(8,128)(2,1)}, bf16[128,1792]{1,0:T(8,128)(2,1)S(1)}, u32[]{:S(2)}, u32[]{:S(2)}) collective-permute-start(bf16[128,1792]{1,0:T(8,128)(2,1)} %concatenate.13), channel_id=1, source_target_pairs={{0,4},{1,5},{2,6},{3,7},{12,8},{13,9},{14,10},{15,11},{16,20},{17,... | collective-permute-start | bytes 1376264 | tf_op jit(solution)/shard_map/ppermute | solution.py:312
  78.1 8.4 %collective-permute-done.9.source = bf16[448,4096]{1,0:T(8,128)(2,1)} collective-permute-done((bf16[448,4096]{1,0:T(8,128)(2,1)}, bf16[448,4096]{1,0:T(8,128)(2,1)}, u32[]{:S(2)}, u32[]{:S(2)}) %collective-permute-start.9) | collective-permute-done | bytes 3670048 | tf_op jit(solution)/shard_map/ppermute | solution.py:312
  86.5 2.2 %shard_map.83 = bf16[448,4096]{1,0:T(8,128)(2,1)S(1)} custom-call(bf16[448,4096]{1,0:T(8,128)(2,1)} %collective-permute-done.9.source), custom_call_target="tpu_custom_call" | custom-call | flops 1000 | bytes 1000 | tf_op jit(solution)/shard_map/pallas_call | solution.py:226
  88.7 5.1 %collective-permute-done.7 = bf16[128,4096]{1,0:T(8,128)(2,1)} collective-permute-done((bf16[128,4096]{1,0:T(8,128)(2,1)}, bf16[128,4096]{1,0:T(8,128)(2,1)}, u32[]{:S(2)}, u32[]{:S(2)}) %collective-permute-start.7) | collective-permute-done | bytes 1048608 | tf_op jit(solution)/shard_map/ppermute | solution.py:312
  93.9 3.4 %collective-permute-start.11 = (bf16[144,896]{1,0:T(8,128)(2,1)S(1)}, bf16[144,896]{1,0:T(8,128)(2,1)S(1)}, u32[]{:S(2)}, u32[]{:S(2)}) collective-permute-start(bf16[144,896]{1,0:T(8,128)(2,1)S(1)} %copy-done.14), channel_id=1, source_target_pairs={{0,8},{1,9},{2,10},{3,11},{4,12},{5,13},{6,14},{7,15},{8,0},{9,1},... | collective-permute-start | bytes 774152 | tf_op jit(solution)/shard_map/ppermute | solution.py:312
  97.3 1.3 %broadcast_select_fusion = bf16[128,4096]{1,0:T(8,128)(2,1)S(1)} fusion(bf16[128,4096]{1,0:T(8,128)(2,1)} %collective-permute-done.7, bf16[128,4096]{1,0:T(8,128)(2,1)} %collective-permute-done.3, pred[]{:T(512)S(6)} %or.3), kind=kLoop, calls=%fused_computation.10 | loop fusion | flops 524288 | bytes 3145729 | tf_op jit(solution)/shard_map/jit(_where)/select_n | solution.py:394
  99.9 3.3 %convolution_convert_fusion.4.refs_5_ = bf16[128,448]{1,0:T(8,128)(2,1)S(1)} fusion(bf16[128,4096]{1,0:T(8,128)(2,1)S(1)} %broadcast_select_fusion, bf16[448,4096]{1,0:T(8,128)(2,1)} %collective-permute-done.1), kind=kOutput, calls=%fused_computation.5 | convolution fusion | flops 469819392 | bytes 4833280 | tf_op jit(solution)/shard_map/dot_general | solution.py:364
  103.2 3.6 %convolution_convert_fusion.1.refs_6_ = bf16[512,448]{1,0:T(8,128)(2,1)S(1)} fusion(bf16[448,4096]{1,0:T(8,128)(2,1)S(1)} %shard_map.83, bf16[128,4096]{1,0:T(8,128)(2,1)S(1)} %broadcast_select_fusion, bf16[128,4096]{1,0:T(8,128)(2,1)S(1)} %copy-done.20, bf16[128,4096]{1,0:T(8,128)(2,1)} %collective-permute-done, bf16[128,4096]{1,0:T(8,128)(2,1)S(1)} %copy-done.21), kind=kOutput, calls=%fused_computation.2 | convolution fusion | flops 1896054784 | bytes 8323072 | tf_op jit(solution)/shard_map/dot_general | solution.py:364
  106.8 3.7 %convolution_convert_fusion.refs_7_ = bf16[512,448]{1,0:T(8,128)(2,1)S(1)} fusion(bf16[448,4096]{1,0:T(8,128)(2,1)S(1)} %collective-permute-done.12, bf16[128,4096]{1,0:T(8,128)(2,1)S(1)} %broadcast_select_fusion, bf16[128,4096]{1,0:T(8,128)(2,1)S(1)} %copy-done.20, bf16[128,4096]{1,0:T(8,128)(2,1)} %collective-permute-done, bf16[128,4096]{1,0:T(8,128)(2,1)S(1)} %copy-done.21), kind=kOutput, calls=%fused_computation.1 | convolution fusion | flops 1896054784 | bytes 8323072 | tf_op jit(solution)/shard_map/dot_general | solution.py:364
  110.6 2.2 %shard_map.84.own = bf16[4,1,32,128]{3,2,1,0:T(8,128)(2,1)S(1)} custom-call(bf16[256,448]{1,0:T(8,128)(2,1)S(1)} %convolution_convert_fusion.3.refs_0_, bf16[128,448]{1,0:T(8,128)(2,1)S(1)} %convolution_convert_fusion.7.refs_1_, bf16[128,448]{1,0:T(8,128)(2,1)S(1)} %convolution_convert_fusion.5.refs_2_, ...), custom_call_target="tpu_custom_call" | custom-call | flops 1000 | bytes 1000 | tf_op jit(solution)/shard_map/pallas_call | solution.py:209
  112.9 1.8 %collective-permute-start.14 = (bf16[4,1,32,128]{3,2,1,0:T(8,128)(2,1)S(1)}, bf16[4,1,32,128]{3,2,1,0:T(8,128)(2,1)S(1)}, u32[]{:S(2)}, u32[]{:S(2)}) collective-permute-start(bf16[4,1,32,128]{3,2,1,0:T(8,128)(2,1)S(1)} %shard_map.84.own), channel_id=1, source_target_pairs={{0,8},{1,9},{2,10},{3,11},{4,12},{5,13},{6,14},{7,15},{8,0},{9,1},... | collective-permute-start | bytes 98312 | tf_op jit(solution)/shard_map/ppermute | solution.py:312
  114.7 2.5 %collective-permute-start.15 = (bf16[4,1,32,128]{3,2,1,0:T(8,128)(2,1)S(1)}, bf16[4,1,32,128]{3,2,1,0:T(8,128)(2,1)S(1)}, u32[]{:S(2)}, u32[]{:S(2)}) collective-permute-start(bf16[4,1,32,128]{3,2,1,0:T(8,128)(2,1)S(1)} %shard_map.84.own), channel_id=1, source_target_pairs={{0,12},{1,13},{2,14},{3,15},{4,8},{5,9},{6,10},{7,11},{8,4},{9,5},... | collective-permute-start | bytes 98312 | tf_op jit(solution)/shard_map/ppermute | solution.py:312
  118.1 2.3 %collective-permute-done.15.refs_2_ = bf16[4,1,32,128]{3,2,1,0:T(8,128)(2,1)S(1)} collective-permute-done((bf16[4,1,32,128]{3,2,1,0:T(8,128)(2,1)S(1)}, bf16[4,1,32,128]{3,2,1,0:T(8,128)(2,1)S(1)}, u32[]{:S(2)}, u32[]{:S(2)}) %collective-permute-start.15) | collective-permute-done | bytes 32800 | tf_op jit(solution)/shard_map/ppermute | solution.py:312
  120.6 1.6 %collective-permute-start.17 = (bf16[4,1,32,128]{3,2,1,0:T(8,128)(2,1)S(1)}, bf16[4,1,32,128]{3,2,1,0:T(8,128)(2,1)S(1)}, u32[]{:S(2)}, u32[]{:S(2)}) collective-permute-start(bf16[4,1,32,128]{3,2,1,0:T(8,128)(2,1)S(1)} %shard_map.85.q0), channel_id=1, source_target_pairs={{0,2},{1,3},{2,0},{3,1},{4,6},{5,7},{6,4},{7,5},{8,10},{9,11},{10,... | collective-permute-start | bytes 98312 | tf_op jit(solution)/shard_map/ppermute | solution.py:312
  122.6 2.8 %shard_map.86.stored_ref = bf16[768,4096]{1,0:T(8,128)(2,1)S(1)} custom-call(bf16[768,4096]{1,0:T(8,128)(2,1)} %source), custom_call_target="tpu_custom_call" | custom-call | flops 1000 | bytes 1000 | tf_op jit(solution)/shard_map/pallas_call | solution.py:226
  125.5 2.4 %shard_map.87 = f32[16,768]{1,0:T(8,128)} custom-call(s32[1]{0:T(128)} %bitcast.where_ref, bf16[4,1,32,128]{3,2,1,0:T(8,128)(2,1)S(1)} %shard_map.85.q0, bf16[4,1,32,128]{3,2,1,0:T(8,128)(2,1)S(1)} %collective-permute-done.16.q1, bf16[4,1,32,128]{3,2,1,0:T(8,128)(2,1)S(1)} %collective-permute-done.17.q2, ...), custom_call_target="tpu_custom_call" | custom-call | flops 1000 | bytes 1000 | tf_op jit(solution)/shard_map/pallas_call | solution.py:288
  (82 shorter events, 15.8 us)
Async XLA Ops:
  0.0 10.3 %copy-start = (bf16[128,4096]{1,0:T(8,128)(2,1)S(1)}, bf16[128,4096]{1,0:T(8,128)(2,1)}, u32[]{:S(2)}) copy-start(bf16[128,4096]{1,0:T(8,128)(2,1)} %param.8) | copy-start | bytes 3145732
  0.0 10.9 %copy-start.1 = (bf16[128,7168]{1,0:T(8,128)(2,1)S(1)}, bf16[128,7168]{1,0:T(8,128)(2,1)}, u32[]{:S(2)}) copy-start(bf16[128,7168]{1,0:T(8,128)(2,1)} %gate_ref.1) | copy-start | bytes 5505028
  0.0 27.2 %collective-permute-start.1 = (bf16[448,4096]{1,0:T(8,128)(2,1)}, bf16[448,4096]{1,0:T(8,128)(2,1)}, u32[]{:S(2)}, u32[]{:S(2)}) collective-permute-start(bf16[448,4096]{1,0:T(8,128)(2,1)} %param.11), channel_id=1, source_target_pairs={{0,1},{1,0},{2,3},{3,2},{4,5},{5,4},{6,7},{7,6},{8,9},{9,8},{10,11... | collective-permute-start | bytes 11010056 | tf_op jit(solution)/shard_map/ppermute | solution.py:312
  0.5 26.7 %collective-permute-start = (bf16[128,4096]{1,0:T(8,128)(2,1)}, bf16[128,4096]{1,0:T(8,128)(2,1)}, u32[]{:S(2)}, u32[]{:S(2)}) collective-permute-start(bf16[128,4096]{1,0:T(8,128)(2,1)} %param.10), channel_id=1, source_target_pairs={{0,4},{1,5},{2,6},{3,7},{4,0},{5,1},{6,2},{7,3},{8,12},{9,13},{10,... | collective-permute-start | bytes 3145736 | tf_op jit(solution)/shard_map/ppermute | solution.py:312
  3.1 25.7 %collective-permute-start.3 = (bf16[128,4096]{1,0:T(8,128)(2,1)}, bf16[128,4096]{1,0:T(8,128)(2,1)}, u32[]{:S(2)}, u32[]{:S(2)}) collective-permute-start(bf16[128,4096]{1,0:T(8,128)(2,1)} %param.10), channel_id=1, source_target_pairs={{4,8},{5,9},{6,10},{7,11},{8,4},{9,5},{10,6},{11,7},{20,24},{21,25... | collective-permute-start | bytes 3145736 | tf_op jit(solution)/shard_map/ppermute | solution.py:312
  4.7 81.7 %collective-permute-start.9 = (bf16[448,4096]{1,0:T(8,128)(2,1)}, bf16[448,4096]{1,0:T(8,128)(2,1)}, u32[]{:S(2)}, u32[]{:S(2)}) collective-permute-start(bf16[448,4096]{1,0:T(8,128)(2,1)} %param.11), channel_id=1, source_target_pairs={{0,2},{1,3},{2,0},{3,1},{4,6},{5,7},{6,4},{7,5},{8,10},{9,11},{10,... | collective-permute-start | bytes 11010056 | tf_op jit(solution)/shard_map/ppermute | solution.py:312
  12.1 20.4 %copy-start.17 = (bf16[448,4096]{1,0:T(8,128)(2,1)S(1)}, bf16[448,4096]{1,0:T(8,128)(2,1)}, u32[]{:S(2)}) copy-start(bf16[448,4096]{1,0:T(8,128)(2,1)} %param.11) | copy-start | bytes 11010052
  27.2 11.6 %collective-permute-start.2 = (bf16[128,4096]{1,0:T(8,128)(2,1)}, bf16[128,4096]{1,0:T(8,128)(2,1)}, u32[]{:S(2)}, u32[]{:S(2)}) collective-permute-start(bf16[128,4096]{1,0:T(8,128)(2,1)} %collective-permute-done), channel_id=1, source_target_pairs={{4,8},{5,9},{6,10},{7,11},{8,4},{9,5},{10,6},{11,7},{20,24},{21,25... | collective-permute-start | bytes 3145736 | tf_op jit(solution)/shard_map/ppermute | solution.py:312
  28.8 27.8 %collective-permute-start.4 = (bf16[128,4096]{1,0:T(8,128)(2,1)}, bf16[128,4096]{1,0:T(8,128)(2,1)S(1)}, u32[]{:S(2)}, u32[]{:S(2)}) collective-permute-start(bf16[128,4096]{1,0:T(8,128)(2,1)} %collective-permute-done.3), channel_id=1, source_target_pairs={{4,0},{5,1},{6,2},{7,3},{8,12},{9,13},{10,14},{11,15},{20,16},{21,... | collective-permute-start | bytes 3145736 | tf_op jit(solution)/shard_map/ppermute | solution.py:312
  56.6 29.8 %collective-permute-start.5 = (bf16[144,1792]{1,0:T(8,128)(2,1)}, bf16[144,1792]{1,0:T(8,128)(2,1)S(1)}, u32[]{:S(2)}, u32[]{:S(2)}) collective-permute-start(bf16[144,1792]{1,0:T(8,128)(2,1)} %get-tuple-element.85), channel_id=1, source_target_pairs={{0,12},{1,13},{2,14},{3,15},{4,8},{5,9},{6,10},{7,11},{8,4},{9,5},... | collective-permute-start | bytes 1548296 | tf_op jit(solution)/shard_map/ppermute | solution.py:312
  59.4 34.4 %collective-permute-start.7 = (bf16[128,4096]{1,0:T(8,128)(2,1)}, bf16[128,4096]{1,0:T(8,128)(2,1)}, u32[]{:S(2)}, u32[]{:S(2)}) collective-permute-start(bf16[128,4096]{1,0:T(8,128)(2,1)} %collective-permute-done.2), channel_id=1, source_target_pairs={{4,0},{5,1},{6,2},{7,3},{8,12},{9,13},{10,14},{11,15},{20,16},{21,... | collective-permute-start | bytes 3145736 | tf_op jit(solution)/shard_map/ppermute | solution.py:312
  66.3 22.4 %collective-permute-start.8 = (bf16[128,1792]{1,0:T(8,128)(2,1)}, bf16[128,1792]{1,0:T(8,128)(2,1)S(1)}, u32[]{:S(2)}, u32[]{:S(2)}) collective-permute-start(bf16[128,1792]{1,0:T(8,128)(2,1)} %concatenate.14), channel_id=1, source_target_pairs={{0,8},{1,9},{2,10},{3,11},{12,4},{13,5},{14,6},{15,7},{16,24},{17,... | collective-permute-start | bytes 1376264 | tf_op jit(solution)/shard_map/ppermute | solution.py:312
  75.8 18.1 %copy-start.16 = (bf16[144,896]{1,0:T(8,128)(2,1)S(1)}, bf16[144,896]{1,0:T(8,128)(2,1)}, u32[]{:S(2)}) copy-start(bf16[144,896]{1,0:T(8,128)(2,1)} %copy-done.15) | copy-start | bytes 774148
  75.8 18.2 %copy-start.14 = (bf16[144,896]{1,0:T(8,128)(2,1)S(1)}, bf16[144,896]{1,0:T(8,128)(2,1)}, u32[]{:S(2)}) copy-start(bf16[144,896]{1,0:T(8,128)(2,1)} %copy-done.13) | copy-start | bytes 774148
  75.8 22.9 %copy-start.18 = (bf16[448,4096]{1,0:T(8,128)(2,1)S(1)}, bf16[448,4096]{1,0:T(8,128)(2,1)}, u32[]{:S(2)}) copy-start(bf16[448,4096]{1,0:T(8,128)(2,1)} %param.11) | copy-start | bytes 11010052
  75.8 18.1 %collective-permute-start.6 = (bf16[128,1792]{1,0:T(8,128)(2,1)}, bf16[128,1792]{1,0:T(8,128)(2,1)S(1)}, u32[]{:S(2)}, u32[]{:S(2)}) collective-permute-start(bf16[128,1792]{1,0:T(8,128)(2,1)} %concatenate.13), channel_id=1, source_target_pairs={{0,4},{1,5},{2,6},{3,7},{12,8},{13,9},{14,10},{15,11},{16,20},{17,... | collective-permute-start | bytes 1376264 | tf_op jit(solution)/shard_map/ppermute | solution.py:312
  93.8 13.0 %collective-permute-start.12 = (bf16[448,4096]{1,0:T(8,128)(2,1)}, bf16[448,4096]{1,0:T(8,128)(2,1)S(1)}, u32[]{:S(2)}, u32[]{:S(2)}) collective-permute-start(bf16[448,4096]{1,0:T(8,128)(2,1)} %collective-permute-done.9.source), channel_id=1, source_target_pairs={{0,1},{1,0},{2,3},{3,2},{4,5},{5,4},{6,7},{7,6},{8,9},{9,8},{10,11... | collective-permute-start | bytes 11010056 | tf_op jit(solution)/shard_map/ppermute | solution.py:312
  93.9 16.7 %collective-permute-start.10 = (bf16[144,896]{1,0:T(8,128)(2,1)S(1)}, bf16[144,896]{1,0:T(8,128)(2,1)S(1)}, u32[]{:S(2)}, u32[]{:S(2)}) collective-permute-start(bf16[144,896]{1,0:T(8,128)(2,1)S(1)} %copy-done.16), channel_id=1, source_target_pairs={{0,4},{1,5},{2,6},{3,7},{4,0},{5,1},{6,2},{7,3},{8,12},{9,13},{10,... | collective-permute-start | bytes 774152 | tf_op jit(solution)/shard_map/ppermute | solution.py:312
  93.9 16.6 %collective-permute-start.11 = (bf16[144,896]{1,0:T(8,128)(2,1)S(1)}, bf16[144,896]{1,0:T(8,128)(2,1)S(1)}, u32[]{:S(2)}, u32[]{:S(2)}) collective-permute-start(bf16[144,896]{1,0:T(8,128)(2,1)S(1)} %copy-done.14), channel_id=1, source_target_pairs={{0,8},{1,9},{2,10},{3,11},{4,12},{5,13},{6,14},{7,15},{8,0},{9,1},... | collective-permute-start | bytes 774152 | tf_op jit(solution)/shard_map/ppermute | solution.py:312
  98.7 4.5 %copy-start.20 = (bf16[128,4096]{1,0:T(8,128)(2,1)S(1)}, bf16[128,4096]{1,0:T(8,128)(2,1)}, u32[]{:S(2)}) copy-start(bf16[128,4096]{1,0:T(8,128)(2,1)} %copy-done.19) | copy-start | bytes 3145732
  98.7 4.5 %copy-start.21 = (bf16[128,4096]{1,0:T(8,128)(2,1)S(1)}, bf16[128,4096]{1,0:T(8,128)(2,1)}, u32[]{:S(2)}) copy-start(bf16[128,4096]{1,0:T(8,128)(2,1)} %param.10) | copy-start | bytes 3145732
  106.8 3.8 %copy-start.4 = (bf16[144,1792]{1,0:T(8,128)(2,1)S(1)}, bf16[144,1792]{1,0:T(8,128)(2,1)}, u32[]{:S(2)}) copy-start(bf16[144,1792]{1,0:T(8,128)(2,1)} %copy-done.3) | copy-start | bytes 1548292
  106.8 3.8 %copy-start.6 = (bf16[128,896]{1,0:T(8,128)(2,1)S(1)}, bf16[128,896]{1,0:T(8,128)(2,1)}, u32[]{:S(2)}) copy-start(bf16[128,896]{1,0:T(8,128)(2,1)} %copy-done.5) | copy-start | bytes 688132
  106.8 3.8 %copy-start.8 = (bf16[128,896]{1,0:T(8,128)(2,1)S(1)}, bf16[128,896]{1,0:T(8,128)(2,1)}, u32[]{:S(2)}) copy-start(bf16[128,896]{1,0:T(8,128)(2,1)} %copy-done.7) | copy-start | bytes 688132
  106.8 3.8 %copy-start.10 = (bf16[64,1792]{1,0:T(8,128)(2,1)S(1)}, bf16[64,1792]{1,0:T(8,128)(2,1)}, u32[]{:S(2)}) copy-start(bf16[64,1792]{1,0:T(8,128)(2,1)} %copy-done.9) | copy-start | bytes 688132
  110.5 12.0 %copy-start.23 = (s32[16]{0:T(128)S(1)}, s32[16]{0:T(128)}, u32[]{:S(2)}) copy-start(s32[16]{0:T(128)} %param.15) | copy-start | bytes 196
  112.8 4.5 %collective-permute-start.13 = (bf16[4,1,32,128]{3,2,1,0:T(8,128)(2,1)S(1)}, bf16[4,1,32,128]{3,2,1,0:T(8,128)(2,1)S(1)}, u32[]{:S(2)}, u32[]{:S(2)}) collective-permute-start(bf16[4,1,32,128]{3,2,1,0:T(8,128)(2,1)S(1)} %shard_map.84.own), channel_id=1, source_target_pairs={{0,4},{1,5},{2,6},{3,7},{4,0},{5,1},{6,2},{7,3},{8,12},{9,13},{10,... | collective-permute-start | bytes 98312 | tf_op jit(solution)/shard_map/ppermute | solution.py:312
  112.9 5.2 %collective-permute-start.14 = (bf16[4,1,32,128]{3,2,1,0:T(8,128)(2,1)S(1)}, bf16[4,1,32,128]{3,2,1,0:T(8,128)(2,1)S(1)}, u32[]{:S(2)}, u32[]{:S(2)}) collective-permute-start(bf16[4,1,32,128]{3,2,1,0:T(8,128)(2,1)S(1)} %shard_map.84.own), channel_id=1, source_target_pairs={{0,8},{1,9},{2,10},{3,11},{4,12},{5,13},{6,14},{7,15},{8,0},{9,1},... | collective-permute-start | bytes 98312 | tf_op jit(solution)/shard_map/ppermute | solution.py:312
  114.7 5.7 %collective-permute-start.15 = (bf16[4,1,32,128]{3,2,1,0:T(8,128)(2,1)S(1)}, bf16[4,1,32,128]{3,2,1,0:T(8,128)(2,1)S(1)}, u32[]{:S(2)}, u32[]{:S(2)}) collective-permute-start(bf16[4,1,32,128]{3,2,1,0:T(8,128)(2,1)S(1)} %shard_map.84.own), channel_id=1, source_target_pairs={{0,12},{1,13},{2,14},{3,15},{4,8},{5,9},{6,10},{7,11},{8,4},{9,5},... | collective-permute-start | bytes 98312 | tf_op jit(solution)/shard_map/ppermute | solution.py:312
  120.5 4.8 %collective-permute-start.16 = (bf16[4,1,32,128]{3,2,1,0:T(8,128)(2,1)S(1)}, bf16[4,1,32,128]{3,2,1,0:T(8,128)(2,1)S(1)}, u32[]{:S(2)}, u32[]{:S(2)}) collective-permute-start(bf16[4,1,32,128]{3,2,1,0:T(8,128)(2,1)S(1)} %shard_map.85.q0), channel_id=1, source_target_pairs={{0,1},{1,0},{2,3},{3,2},{4,5},{5,4},{6,7},{7,6},{8,9},{9,8},{10,11... | collective-permute-start | bytes 98312 | tf_op jit(solution)/shard_map/ppermute | solution.py:312
  120.6 4.8 %collective-permute-start.17 = (bf16[4,1,32,128]{3,2,1,0:T(8,128)(2,1)S(1)}, bf16[4,1,32,128]{3,2,1,0:T(8,128)(2,1)S(1)}, u32[]{:S(2)}, u32[]{:S(2)}) collective-permute-start(bf16[4,1,32,128]{3,2,1,0:T(8,128)(2,1)S(1)} %shard_map.85.q0), channel_id=1, source_target_pairs={{0,2},{1,3},{2,0},{3,1},{4,6},{5,7},{6,4},{7,5},{8,10},{9,11},{10,... | collective-permute-start | bytes 98312 | tf_op jit(solution)/shard_map/ppermute | solution.py:312
  122.2 3.3 %collective-permute-start.18 = (bf16[4,1,32,128]{3,2,1,0:T(8,128)(2,1)S(1)}, bf16[4,1,32,128]{3,2,1,0:T(8,128)(2,1)S(1)}, u32[]{:S(2)}, u32[]{:S(2)}) collective-permute-start(bf16[4,1,32,128]{3,2,1,0:T(8,128)(2,1)S(1)} %shard_map.85.q0), channel_id=1, source_target_pairs={{0,3},{1,2},{2,1},{3,0},{4,7},{5,6},{6,5},{7,4},{8,11},{9,10},{10,... | collective-permute-start | bytes 98312 | tf_op jit(solution)/shard_map/ppermute | solution.py:312
  (11 other events, 15.6 us)
